TPU v7x, 256 devices: a whole 4x4x8 slice. The times are simulated.
256 devices in a mesh: row: 64 (over y_lo, x, z), col: 4 (over y_hi, core).
Axes of the slice: x: 4, y: 4 (y_hi: 2, y_lo: 2; y = y_hi * 2 + y_lo), z: 8, core: 2. Of those that a mesh axis runs over, the one named last changes fastest.
Arguments:
- amplitudes: float32 [4096, 2048], P(('row', 'col')), may hold values from -6 to 6
- integrals: float32 [2048, 89600], P('col', 'row'), may hold values from -0.125 to 0.125
Outputs:
- ladder: float32 [4096, 89600], P(('row', 'col'))
All inputs are finite; a program needn't handle non-finite values.
Results may differ from a plain program's by a relative error of at most 0.000071.
Values sent between devices are 32-bit elements; how exact they have to be, the bound alone decides.
No kernel may reach another device: no remote copies, remote signals or barrier semaphores. Data moves between devices by JAX's collectives and lax.ppermute only.
A program may use at most 128 MiB of HBM per device.

v0:
```python
import jax
import jax.numpy as jnp
from jax import lax
from jax.sharding import PartitionSpec as P


def on_device(amplitudes, integrals):
    gathered = lax.all_gather(amplitudes, "row", axis=0, tiled=True)
    whole = lax.all_gather(integrals, "col", axis=0, tiled=True)
    summed = jnp.dot(
        gathered, whole, precision=lax.Precision.HIGHEST, preferred_element_type=jnp.float32
    )
    partial_value = 0.5 * summed
    return lax.all_to_all(partial_value, "row", split_axis=0, concat_axis=1, tiled=True)


def solution(mesh):
    placed = (P(("row", "col"), None), P("col", "row"))
    return jax.shard_map(
        on_device, mesh=mesh, in_specs=placed, out_specs=P(("row", "col"), None), check_vma=False
    )
```

profile of v0, /device:TPU:24, one launch (start us, length us, event | category | flops | bytes accessed | tf_op | source)
XLA Modules:
  0.0 611.7 jit_solution(5352480398713094493)
XLA Ops:
  6.5 0.0 all-gather.3.cloned.1.call-start
  6.5 0.7 all-gather.3.cloned.1.call-update
  7.3 0.0 all-gather.5.cloned.1.call-start
  7.3 0.7 all-gather.5.cloned.1.call-update
  8.0 315.1 %all-gather.3.cloned.1.call-done = f32[1024,2048]{1,0:T(8,128)} async-done(((f32[16,2048]{1,0:T(8,128)}), f32[1024,2048]{1,0:T(8,128)}) %all-gather.3.cloned.1.call-update) | async-done | bytes 8388624 | tf_op jit(solution)/shard_map/all_gather | solution.py:8
  323.1 80.7 %all-gather.5.cloned.1.call-done = f32[2048,1400]{0,1:T(8,128)} async-done(((f32[512,1400]{0,1:T(8,128)}), f32[2048,1400]{0,1:T(8,128)}) %all-gather.5.cloned.1.call-update) | async-done | bytes 11468816 | tf_op jit(solution)/shard_map/all_gather | solution.py:9
  403.8 41.9 %convolution_multiply_fusion = f32[1024,1400]{0,1:T(8,128)} fusion(f32[1024,2048]{1,0:T(8,128)} %all-gather.3.cloned.1.call-done, f32[2048,1400]{0,1:T(8,128)} %all-gather.5.cloned.1.call-done), kind=kOutput, calls=%fused_computation | convolution fusion | flops 35233587200 | bytes 25591808 | tf_op jit(solution)/shard_map/dot_general | solution.py:10
  445.7 6.3 %copy.5 = f32[1024,1400]{1,0:T(8,128)} copy(f32[1024,1400]{0,1:T(8,128)} %convolution_multiply_fusion) | data formatting | bytes 11468800 | tf_op jit(solution)/shard_map/mul | solution.py:13
  451.9 141.8 %all_to_all.19 = f32[64,16,1400]{2,1,0:T(8,128)S(1)} all-to-all(f32[64,16,1400]{2,1,0:T(8,128)} %bitcast.4), channel_id=1, replica_groups=mesh['row'=64,'col'=4] {'row'}, dimensions={0} | all-to-all | bytes 11468800 | tf_op jit(solution)/shard_map/all_to_all | solution.py:14
  593.7 4.2 copy.6
  597.9 7.0 %all_to_all.17 = f32[16,89600]{1,0:T(8,128)} reshape(f32[16,64,1400]{2,1,0:T(8,128)} %copy.6) | data formatting | bytes 11468800 | tf_op jit(solution)/shard_map/all_to_all | solution.py:14
Async XLA Ops:
  6.5 316.5 %all-gather.3.cloned.1.call-start = ((), (), s32[]{:S(2)}) async-start(), calls=%async_computation.1 | async-start | bytes 8519680 | tf_op jit(solution)/shard_map/all_gather | solution.py:8
  7.3 396.5 %all-gather.5.cloned.1.call-start = ((), (), s32[]{:S(2)}) async-start(), calls=%async_computation.2 | async-start | bytes 14336000 | tf_op jit(solution)/shard_map/all_gather | solution.py:9
Sparse Core Ops, SparseCore 0:
  9.1 313.8 all-gather.2
  324.9 78.8 all-gather.4
where the time goes:
time: 613 us; the launch traced here: 612 us
  waiting for transfers between devices  397 us (65%)
  blocking collectives  142 us (23%)
  matrix products  41.9 us (7%)
  local copies, waits for them, and re-layouts  17.5 us (3%)
  between operations  13.4 us (2%)
    all_gather x1, waiting for transfers between devices, on_device(): gathered = lax.all_gather(amplitudes, 'row', axis=0, tiled=True)  315 us
    all_to_all x1, blocking collectives, on_device(): lax.all_to_all(partial_value, 'row', split_axis=0, concat_axis=1, tiled=T...  142 us
    all_gather x1, waiting for transfers between devices, on_device(): whole = lax.all_gather(integrals, 'col', axis=0, tiled=True)  80.7 us
    dot_general x1, matrix products, on_device(): jnp.dot(gathered, whole, precision=lax.Precision.HIGHEST, preferred_eleme...  41.9 us
  transfers between devices with their start and end apart: 2, of which 2 were waited for; matrix products, arithmetic and copies ran while one was open for 0% of the time, Pallas kernels for 0%

commit v1 on v0

v1 whole, which is shorter than its diff:
```python
import functools

import jax
import jax.numpy as jnp
from jax import lax
from jax.experimental import pallas as pl
from jax.experimental.pallas import tpu as pltpu
from jax.sharding import Mesh, PartitionSpec as P

AXES = ("yl", "x", "z", "yh", "core")
TILE = 256
SPLIT = 3
GROUP = 16


def swap_core(value):
    return lax.ppermute(value, "core", [(0, 1), (1, 0)])


def swap_near(value):
    return lax.ppermute(value, "yl", [(0, 1), (1, 0)])


def swap_far(value):
    return lax.ppermute(value, ("yl", "yh"), [(2, 1), (1, 2), (3, 0), (0, 3)])


def halves(value):
    top = value.astype(jnp.bfloat16)
    rest = (value - top.astype(jnp.float32)).astype(jnp.bfloat16)
    return top, rest


def split_kernel(own_ref, t_ref, top_ref, rest_ref):
    part = t_ref.shape[1] // 4
    for q in range(4):
        source = pl.multiple_of((own_ref[0] ^ q) * part, part)
        depth = pl.ds(q * part, part)
        top_ref[:, depth], rest_ref[:, depth] = halves(t_ref[:, pl.ds(source, part)])


def split(own, t):
    rows, depth = t.shape
    block = min(rows, 128)
    spec = pl.BlockSpec((block, depth), lambda r, own: (r, 0))
    return pl.pallas_call(
        split_kernel,
        grid_spec=pltpu.PrefetchScalarGridSpec(
            num_scalar_prefetch=1, grid=(rows // block,), in_specs=[spec], out_specs=[spec] * 2
        ),
        out_shape=[jax.ShapeDtypeStruct((rows, depth), jnp.bfloat16)] * 2,
        cost_estimate=pl.CostEstimate(
            flops=4 * rows * depth, bytes_accessed=8 * rows * depth, transcendentals=0
        ),
    )(own, t)


def product_kernel(counts, top_ref, rest_ref, *refs):
    pieces, out_ref = refs[:-1], refs[-1]
    dot = functools.partial(
        lax.dot_general,
        dimension_numbers=(((1,), (1,)), ((), ())),
        preferred_element_type=jnp.float32,
    )
    total, at = None, 0
    for q, count in enumerate(counts):
        value = pieces[at][...]
        if count == 2:
            value = jnp.where(pl.program_id(0) < SPLIT, value, pieces[at + 1][...])
        at += count
        top, rest = halves(value)
        depth = pl.ds(q * value.shape[1], value.shape[1])
        t_top, t_rest = top_ref[:, depth], rest_ref[:, depth]
        term = dot(t_top, rest) + dot(t_rest, top) + dot(t_top, top)
        total = term if total is None else total + term
    out_ref[...] = 0.5 * total


def product(t_top, t_rest, quarters, columns):
    rows, depth = t_top.shape
    part = depth // 4
    whole = pl.BlockSpec((rows, depth), lambda n: (0, 0), pipeline_mode=pl.Buffered(1))
    specs, pieces = [], []
    for quarter in quarters:
        if len(quarter) == 1:
            specs += [pl.BlockSpec((TILE, part), lambda n: (n, 0))]
        else:
            specs += [
                pl.BlockSpec((TILE, part), lambda n: (jnp.minimum(n, SPLIT - 1), 0)),
                pl.BlockSpec((TILE, part), lambda n: (jnp.maximum(n - SPLIT, 0), 0)),
            ]
        pieces += quarter
    return pl.pallas_call(
        functools.partial(product_kernel, [len(quarter) for quarter in quarters]),
        grid=(pl.cdiv(columns, TILE),),
        in_specs=[whole] * 2 + specs,
        out_specs=pl.BlockSpec((rows, TILE), lambda n: (0, n)),
        out_shape=jax.ShapeDtypeStruct((rows, columns), jnp.float32),
        compiler_params=pltpu.CompilerParams(vmem_limit_bytes=32 << 20),
        cost_estimate=pl.CostEstimate(
            flops=6 * rows * depth * columns,
            bytes_accessed=4 * (rows * depth + depth * columns + rows * columns),
            transcendentals=0,
        ),
    )(t_top, t_rest, *pieces)


def place_kernel(at_ref, block_ref, *refs):
    out_ref = refs[-1]
    width = block_ref.shape[2]
    for s in range(GROUP):
        out_ref[:, s * width : (s + 1) * width] = block_ref[s]


def place(at, block, out=None):
    sources, rows, width = block.shape
    steps = sources // GROUP
    return pl.pallas_call(
        place_kernel,
        grid_spec=pltpu.PrefetchScalarGridSpec(
            num_scalar_prefetch=1,
            grid=(steps,),
            in_specs=[pl.BlockSpec((GROUP, rows, width), lambda g, at: (g, 0, 0))]
            + ([] if out is None else [pl.BlockSpec(memory_space=pl.ANY)]),
            out_specs=pl.BlockSpec((rows, GROUP * width), lambda g, at: (0, at[0] * steps + g)),
        ),
        out_shape=jax.ShapeDtypeStruct((rows, 2 * sources * width), jnp.float32),
        input_output_aliases={} if out is None else {2: 0},
        compiler_params=pltpu.CompilerParams(vmem_limit_bytes=16 << 20),
        cost_estimate=pl.CostEstimate(
            flops=0, bytes_accessed=8 * sources * rows * width, transcendentals=0
        ),
    )(at, block, *([] if out is None else [out]))


def on_device(amplitudes, integrals):
    yl, yh, core = (lax.axis_index(name) for name in ("yl", "yh", "core"))
    rows = amplitudes.shape[0]
    columns = integrals.shape[1]
    t = lax.all_gather(amplitudes, ("x", "z"), axis=0, tiled=True)
    t_top, t_rest = split((2 * yh + core).reshape(1), t)

    own = integrals.T
    near, far = swap_near(own), swap_far(own)
    cut = SPLIT * TILE
    across = [swap_far(near[:cut]), swap_near(far[cut:])]
    own2, near2, far2 = swap_core(own), swap_core(near), swap_core(far)
    across2 = [swap_core(v) for v in across]

    def exchange(v):
        return lax.all_to_all(
            v.reshape(-1, rows, columns), ("x", "z"), split_axis=0, concat_axis=0, tiled=True
        )

    other_block = exchange(product(t_top, t_rest, [[near], [near2], [far], [far2]], columns))
    own_block = exchange(product(t_top, t_rest, [[own], [own2], across, across2], columns))
    out = place((1 - yl).reshape(1), other_block)
    return place(yl.reshape(1), own_block, out)


def solution(mesh):
    grid = Mesh(mesh.devices.reshape(2, 4, 8, 2, 2), AXES)
    return jax.shard_map(
        on_device,
        mesh=grid,
        in_specs=(P(AXES, None), P(("yh", "core"), ("yl", "x", "z"))),
        out_specs=P(AXES, None),
        check_vma=False,
    )
```

time: 613 us -> 271 us (0.44)
  waiting for transfers between devices: 397 us -> 197 us
  blocking collectives: 142 us -> 0 us
  matrix products: 41.9 us -> 0 us
  Pallas kernels: 0 us -> 34.5 us
  starting transfers between devices: 0.04 us -> 14.9 us
  local copies, waits for them, and re-layouts: 17.5 us -> 11 us
    all_gather x2 -> x1, waiting for transfers between devices: 396 us -> 21.2 us  [on_device(): t = lax.all_gather(amplitudes, ('x', 'z'), axis=0, tiled=True)]
    all_to_all x1 -> x0, blocking collectives: 142 us -> none  [on_device(): lax.all_to_all(partial_value, 'row', split_axis=0, concat_axis=1, tiled=T...]
    ppermute x0 -> x9, waiting for transfers between devices: none -> 100 us  [the longest x2 62 us: swap_near(): return lax.ppermute(value, 'yl', [(0, 1), (1, 0)])]
    all_to_all x0 -> x2, waiting for transfers between devices: none -> 74.8 us  [exchange(): lax.all_to_all(v.reshape(-1, rows, columns), ('x', 'z'), split_axis=0, co...]
    dot_general x1 -> x0, matrix products: 41.9 us -> none  [on_device(): jnp.dot(gathered, whole, precision=lax.Precision.HIGHEST, preferred_eleme...]
    pallas_call x0 -> x5, Pallas kernels: none -> 34.5 us  [the longest x2 24.3 us: product(): pl.pallas_call(functools.partial(product_kernel, [len(quarter) for quarte...]
    all_to_all x2 -> x0, local copies, waits for them, and re-layouts: 11.2 us -> none  [on_device(): lax.all_to_all(partial_value, 'row', split_axis=0, concat_axis=1, tiled=T...]
    all_to_all x0 -> x2, starting transfers between devices: none -> 10.6 us  [exchange(): lax.all_to_all(v.reshape(-1, rows, columns), ('x', 'z'), split_axis=0, co...]
  transfers between devices with their start and end apart: 2 -> 12, of which waited for: 2 -> 7; matrix products, arithmetic and copies ran while one was open for 0% -> 1% of each run, Pallas kernels for 0% -> 7%
where the time goes in v1:
time: 271 us
  waiting for transfers between devices  197 us (73%)
  Pallas kernels  34.5 us (13%)
  starting transfers between devices  14.9 us (5%)
  between operations  13.5 us (5%)
  local copies, waits for them, and re-layouts  11 us (4%)
    all_to_all x2, waiting for transfers between devices, exchange(): lax.all_to_all(v.reshape(-1, rows, columns), ('x', 'z'), split_axis=0, co...  74.8 us
    ppermute x2, waiting for transfers between devices, swap_near(): return lax.ppermute(value, 'yl', [(0, 1), (1, 0)])  62 us
    ppermute x2, waiting for transfers between devices, swap_far(): return lax.ppermute(value, ('yl', 'yh'), [(2, 1), (1, 2), (3, 0), (0, 3)])  33.3 us
    pallas_call x2, Pallas kernels, product(): pl.pallas_call(functools.partial(product_kernel, [len(quarter) for quarte...  24.3 us
    all_gather x1, waiting for transfers between devices, on_device(): t = lax.all_gather(amplitudes, ('x', 'z'), axis=0, tiled=True)  21.2 us
    all_to_all x2, starting transfers between devices, exchange(): lax.all_to_all(v.reshape(-1, rows, columns), ('x', 'z'), split_axis=0, co...  10.6 us
    unnamed x16, local copies, waits for them, and re-layouts  7.93 us
  transfers between devices with their start and end apart: 12, of which 7 were waited for; matrix products, arithmetic and copies ran while one was open for 1% of the time, Pallas kernels for 7%

profile of v1, /device:TPU:24, one launch (start us, length us, event | category | flops | bytes accessed | tf_op | source)
XLA Modules:
  0.0 270.7 jit_solution(4572411955966655096)
XLA Ops:
  6.5 0.7 all-gather.2.cloned.1.call-update
  7.3 0.8 collective-permute-start.1
  8.1 1.3 collective-permute-start.3
  9.4 62.0 %collective-permute-done.1.refs_0_ = f32[1400,512]{1,0:T(8,128)S(1)} collective-permute-done((f32[1400,512]{1,0:T(8,128)}, f32[1400,512]{1,0:T(8,128)S(1)}, u32[]{:S(2)}, u32[]{:S(2)}) %collective-permute-start.1) | collective-permute-done | bytes 2867232 | tf_op jit(solution)/shard_map/ppermute | solution.py:21
  71.4 0.0 collective-permute-start.7
  71.4 1.8 collective-permute-done.3.refs_2_
  73.2 21.2 %all-gather.2.cloned.1.call-done.t_ref = f32[512,2048]{1,0:T(8,128)} async-done(((f32[16,2048]{1,0:T(8,128)}), f32[512,2048]{1,0:T(8,128)}) %all-gather.2.cloned.1.call-update) | async-done | bytes 4194320 | tf_op jit(solution)/shard_map/all_gather | solution.py:140
  94.4 4.9 %shard_map.28 = (bf16[512,2048]{1,0:T(8,128)(2,1)}, bf16[512,2048]{1,0:T(8,128)(2,1)}) custom-call(s32[1]{0:T(128)} %bitcast.1.own_ref, f32[512,2048]{1,0:T(8,128)} %all-gather.2.cloned.1.call-done.t_ref), custom_call_target="tpu_custom_call" | custom-call | flops 4194304 | bytes 8388608 | tf_op jit(solution)/shard_map/pallas_call | solution.py:46
  99.3 0.0 collective-permute-done.7.refs_1_
  99.3 0.0 collective-permute-done.8.refs_3_
  99.3 1.6 copy-done.4
  100.9 1.6 copy-done.6
  102.5 12.9 %shard_map.30 = f32[512,1400]{1,0:T(8,128)S(1)} custom-call(bf16[512,2048]{1,0:T(8,128)(2,1)S(1)} %copy-done.4, bf16[512,2048]{1,0:T(8,128)(2,1)S(1)} %copy-done.6, f32[1400,512]{1,0:T(8,128)S(1)} %collective-permute-done.1.refs_0_, f32[1400,512]{1,0:T(8,128)} %collective-permute-done.7.refs_1_, f32[1400,512]{1,0:T(8,128)} %collective-permute-done.3.refs_2_, ...), custom_call_target="tpu_custom_call" | custom-call | flops 8808038400 | bytes 18530304 | tf_op jit(solution)/shard_map/pallas_call | solution.py:93
  115.3 0.0 copy-start
  115.3 1.6 copy-done
  116.9 5.8 %all-to-all-start.1 = ((f32[32,16,1400]{2,1,0:T(8,128)}), f32[32,16,1400]{2,1,0:T(8,128)S(1)}, u32[]{:S(2)}, u32[]{:S(2)}) async-start(f32[32,16,1400]{2,1,0:T(8,128)} %bitcast.6), calls=%async_computation.1 | async-start | bytes 5767168 | tf_op jit(solution)/shard_map/all_to_all | solution.py:151
  122.7 0.0 copy-start.3
  122.8 1.7 slice.8
  124.4 0.6 collective-permute-start.2
  125.0 1.4 slice.9
  126.4 1.1 collective-permute-start.4
  127.5 31.5 %collective-permute-done.2.refs_2_ = f32[768,512]{1,0:T(8,128)S(1)} collective-permute-done((f32[768,512]{1,0:T(8,128)S(1)}, f32[768,512]{1,0:T(8,128)S(1)}, u32[]{:S(2)}, u32[]{:S(2)}) %collective-permute-start.2) | collective-permute-done | bytes 1572896 | tf_op jit(solution)/shard_map/ppermute | solution.py:25
  159.0 0.5 collective-permute-start.6
  159.6 4.7 %collective-permute-done.6.refs_5_ = f32[632,512]{1,0:T(8,128)S(1)} collective-permute-done((f32[632,512]{1,0:T(8,128)S(1)}, f32[632,512]{1,0:T(8,128)S(1)}, u32[]{:S(2)}, u32[]{:S(2)}) %collective-permute-start.6) | collective-permute-done | bytes 1294368 | tf_op jit(solution)/shard_map/ppermute | solution.py:17
  164.3 1.6 copy-done.7
  165.9 11.4 %shard_map.29 = f32[512,1400]{1,0:T(8,128)S(1)} custom-call(bf16[512,2048]{1,0:T(8,128)(2,1)S(1)} %copy-done.5, bf16[512,2048]{1,0:T(8,128)(2,1)S(1)} %copy-done.7, f32[1400,512]{1,0:T(8,128)S(1)} %bitcast.11, f32[1400,512]{1,0:T(8,128)S(1)} %collective-permute-done.refs_1_, f32[768,512]{1,0:T(8,128)S(1)} %collective-permute-done.2.refs_2_, ...), custom_call_target="tpu_custom_call" | custom-call | flops 8808038400 | bytes 18530304 | tf_op jit(solution)/shard_map/pallas_call | solution.py:93
  177.3 1.6 copy-done.1
  178.9 10.3 %all-to-all-done.1.block_ref = f32[32,16,1400]{2,1,0:T(8,128)S(1)} async-done(((f32[32,16,1400]{2,1,0:T(8,128)}), f32[32,16,1400]{2,1,0:T(8,128)S(1)}, u32[]{:S(2)}, u32[]{:S(2)}) %all-to-all-start.1) | async-done | bytes 2867232 | tf_op jit(solution)/shard_map/all_to_all | solution.py:151
  189.2 4.8 %all-to-all-start = ((f32[32,16,1400]{2,1,0:T(8,128)}), f32[32,16,1400]{2,1,0:T(8,128)}, u32[]{:S(2)}, u32[]{:S(2)}) async-start(f32[32,16,1400]{2,1,0:T(8,128)} %bitcast.7), calls=%async_computation | async-start | bytes 5767168 | tf_op jit(solution)/shard_map/all_to_all | solution.py:151
  194.0 2.0 shard_map.31.refs_0_
  196.1 64.5 %all-to-all-done.block_ref = f32[32,16,1400]{2,1,0:T(8,128)} async-done(((f32[32,16,1400]{2,1,0:T(8,128)}), f32[32,16,1400]{2,1,0:T(8,128)}, u32[]{:S(2)}, u32[]{:S(2)}) %all-to-all-start) | async-done | bytes 2867232 | tf_op jit(solution)/shard_map/all_to_all | solution.py:151
  260.6 3.3 %shard_map.32 = f32[16,89600]{1,0:T(8,128)} custom-call(s32[1]{0:T(128)} %bitcast.at_ref, f32[32,16,1400]{2,1,0:T(8,128)} %all-to-all-done.block_ref, f32[16,89600]{1,0:T(8,128)} %shard_map.31.refs_0_), custom_call_target="tpu_custom_call", output_to_operand_aliasing={{}: (2, {})} | custom-call | bytes 5734400 | tf_op jit(solution)/shard_map/pallas_call | solution.py:118
  (16 shorter events, 0.0 us)
Async XLA Ops:
  6.5 87.9 %all-gather.2.cloned.1.call-start = ((), (), s32[]{:S(2)}) async-start(), calls=%async_computation.2 | async-start | bytes 4325376 | tf_op jit(solution)/shard_map/all_gather | solution.py:140
  7.3 64.2 %collective-permute-start.1 = (f32[1400,512]{1,0:T(8,128)}, f32[1400,512]{1,0:T(8,128)S(1)}, u32[]{:S(2)}, u32[]{:S(2)}) collective-permute-start(f32[1400,512]{1,0:T(8,128)} %bitcast.8), channel_id=1, source_target_pairs={{0,128},{128,0},{1,129},{129,1},{2,130},{130,2},{3,131},{131,3},{4... | collective-permute-start | bytes 8601608 | tf_op jit(solution)/shard_map/ppermute | solution.py:21
  8.1 65.1 %collective-permute-start.3 = (f32[1400,512]{1,0:T(8,128)}, f32[1400,512]{1,0:T(8,128)}, u32[]{:S(2)}, u32[]{:S(2)}) collective-permute-start(f32[1400,512]{1,0:T(8,128)} %bitcast.9), channel_id=1, source_target_pairs={{128,2},{2,128},{130,0},{0,130},{129,3},{3,129},{131,1},{1,131},{1... | collective-permute-start | bytes 8601608 | tf_op jit(solution)/shard_map/ppermute | solution.py:25
  71.4 43.9 %copy-start.2 = (f32[1400,512]{1,0:T(8,128)}, f32[1400,512]{1,0:T(8,128)S(1)}, u32[]{:S(2)}) copy-start(f32[1400,512]{1,0:T(8,128)S(1)} %collective-permute-done.1.refs_0_) | copy-start | bytes 8601604
  71.4 27.8 %collective-permute-start.7 = (f32[1400,512]{1,0:T(8,128)S(1)}, f32[1400,512]{1,0:T(8,128)}, u32[]{:S(2)}, u32[]{:S(2)}) collective-permute-start(f32[1400,512]{1,0:T(8,128)S(1)} %collective-permute-done.1.refs_0_), channel_id=1, source_target_pairs={{0,1},{1,0},{2,3},{3,2},{4,5},{5,4},{6,7},{7,6},{8,9},{9,8},{10,11... | collective-permute-start | bytes 8601608 | tf_op jit(solution)/shard_map/ppermute | solution.py:17
  73.2 26.1 %collective-permute-start.8 = (f32[1400,512]{1,0:T(8,128)}, f32[1400,512]{1,0:T(8,128)}, u32[]{:S(2)}, u32[]{:S(2)}) collective-permute-start(f32[1400,512]{1,0:T(8,128)} %collective-permute-done.3.refs_2_), channel_id=1, source_target_pairs={{0,1},{1,0},{2,3},{3,2},{4,5},{5,4},{6,7},{7,6},{8,9},{9,8},{10,11... | collective-permute-start | bytes 8601608 | tf_op jit(solution)/shard_map/ppermute | solution.py:17
  99.3 1.6 copy-start.4
  100.9 1.6 copy-start.6
  115.3 1.6 copy-start
  116.9 72.3 %all-to-all-start.1 = ((f32[32,16,1400]{2,1,0:T(8,128)}), f32[32,16,1400]{2,1,0:T(8,128)S(1)}, u32[]{:S(2)}, u32[]{:S(2)}) async-start(f32[32,16,1400]{2,1,0:T(8,128)} %bitcast.6), calls=%async_computation.1 | async-start | bytes 5767168 | tf_op jit(solution)/shard_map/all_to_all | solution.py:151
  122.7 2.3 copy-start.3
  122.7 41.6 %copy-start.5 = (bf16[512,2048]{1,0:T(8,128)(2,1)S(1)}, bf16[512,2048]{1,0:T(8,128)(2,1)}, u32[]{:S(2)}) copy-start(bf16[512,2048]{1,0:T(8,128)(2,1)} %get-tuple-element.7.top_ref) | copy-start | bytes 6291460
  124.4 34.6 %collective-permute-start.2 = (f32[768,512]{1,0:T(8,128)S(1)}, f32[768,512]{1,0:T(8,128)S(1)}, u32[]{:S(2)}, u32[]{:S(2)}) collective-permute-start(f32[768,512]{1,0:T(8,128)S(1)} %slice.8), channel_id=1, source_target_pairs={{128,2},{2,128},{130,0},{0,130},{129,3},{3,129},{131,1},{1,131},{1... | collective-permute-start | bytes 4718600 | tf_op jit(solution)/shard_map/ppermute | solution.py:25
  125.0 34.5 %collective-permute-start = (f32[1400,512]{1,0:T(8,128)S(1)}, f32[1400,512]{1,0:T(8,128)S(1)}, u32[]{:S(2)}, u32[]{:S(2)}) collective-permute-start(f32[1400,512]{1,0:T(8,128)S(1)} %bitcast.10), channel_id=1, source_target_pairs={{0,1},{1,0},{2,3},{3,2},{4,5},{5,4},{6,7},{7,6},{8,9},{9,8},{10,11... | collective-permute-start | bytes 8601608 | tf_op jit(solution)/shard_map/ppermute | solution.py:17
  126.4 32.6 %collective-permute-start.4 = (f32[632,512]{1,0:T(8,128)S(1)}, f32[632,512]{1,0:T(8,128)S(1)}, u32[]{:S(2)}, u32[]{:S(2)}) collective-permute-start(f32[632,512]{1,0:T(8,128)S(1)} %slice.9), channel_id=1, source_target_pairs={{0,128},{128,0},{1,129},{129,1},{2,130},{130,2},{3,131},{131,3},{4... | collective-permute-start | bytes 3883016 | tf_op jit(solution)/shard_map/ppermute | solution.py:21
  159.0 5.3 %collective-permute-start.5 = (f32[768,512]{1,0:T(8,128)S(1)}, f32[768,512]{1,0:T(8,128)S(1)}, u32[]{:S(2)}, u32[]{:S(2)}) collective-permute-start(f32[768,512]{1,0:T(8,128)S(1)} %collective-permute-done.2.refs_2_), channel_id=1, source_target_pairs={{0,1},{1,0},{2,3},{3,2},{4,5},{5,4},{6,7},{7,6},{8,9},{9,8},{10,11... | collective-permute-start | bytes 4718600 | tf_op jit(solution)/shard_map/ppermute | solution.py:17
  159.0 5.3 %collective-permute-start.6 = (f32[632,512]{1,0:T(8,128)S(1)}, f32[632,512]{1,0:T(8,128)S(1)}, u32[]{:S(2)}, u32[]{:S(2)}) collective-permute-start(f32[632,512]{1,0:T(8,128)S(1)} %collective-permute-done.4.refs_3_), channel_id=1, source_target_pairs={{0,1},{1,0},{2,3},{3,2},{4,5},{5,4},{6,7},{7,6},{8,9},{9,8},{10,11... | collective-permute-start | bytes 3883016 | tf_op jit(solution)/shard_map/ppermute | solution.py:17
  164.3 1.6 copy-start.7
  177.3 1.6 copy-start.1
  189.2 71.3 %all-to-all-start = ((f32[32,16,1400]{2,1,0:T(8,128)}), f32[32,16,1400]{2,1,0:T(8,128)}, u32[]{:S(2)}, u32[]{:S(2)}) async-start(f32[32,16,1400]{2,1,0:T(8,128)} %bitcast.7), calls=%async_computation | async-start | bytes 5767168 | tf_op jit(solution)/shard_map/all_to_all | solution.py:151
Sparse Core Ops, SparseCore 0:
  9.9 84.4 all-gather.1

commit v2 on v1

v2 whole, which is shorter than its diff:
```python
import functools
import math

import jax
import jax.numpy as jnp
from jax import lax
from jax.experimental import pallas as pl
from jax.experimental.pallas import tpu as pltpu
from jax.sharding import Mesh, PartitionSpec as P

AXES = ("yl", "x", "z", "yh", "core")
TILE = 256
CUT = 768
GROUP = 16


def swap_core(value):
    return lax.ppermute(value, "core", [(0, 1), (1, 0)])


def shift_x(value, by):
    return lax.ppermute(value, "x", [(i, (i + by) % 4) for i in range(4)])


def swap_near(value):
    return lax.ppermute(value, "yl", [(0, 1), (1, 0)])


def swap_far(value):
    return lax.ppermute(value, ("yl", "yh"), [(2, 1), (1, 2), (3, 0), (0, 3)])


def halves(value):
    top = value.astype(jnp.bfloat16)
    rest = (value - top.astype(jnp.float32)).astype(jnp.bfloat16)
    return top, rest


def load_amplitudes(place_ref, pieces, last_ref, top_ref, rest_ref):
    own, x = place_ref[0], place_ref[1]
    part = last_ref.shape[3]

    @pl.loop(0, 4)
    def _(q):
        source = own ^ q
        take = pl.ds(pl.multiple_of(jnp.minimum(source, 2) * part, part), part)
        into = pl.ds(pl.multiple_of(q * part, part), part)
        for d, refs in enumerate(pieces):
            last = last_ref[:, d].reshape(-1, part)
            row = lax.rem(x + d, 4) * last.shape[0]
            at = 0
            for ref in refs:
                count = ref.shape[0]
                value = jnp.where(source < 3, ref[:, take], last[at : at + count])
                rows = pl.ds(pl.multiple_of(row + at, count), count)
                top_ref[rows, into], rest_ref[rows, into] = halves(value)
                at += count


def product_kernel(counts, place_ref, *refs):
    pieces, (out_ref, top_ref, rest_ref) = refs[6:-3], refs[-3:]

    @pl.when(pl.program_id(0) == 0)
    def _():
        here, ahead, behind, low, high, last_ref = refs[:6]
        load_amplitudes(
            place_ref, [[here], [ahead], [low, high], [behind]], last_ref, top_ref, rest_ref
        )

    dot = functools.partial(
        lax.dot_general,
        dimension_numbers=(((1,), (1,)), ((), ())),
        preferred_element_type=jnp.float32,
    )
    total, at = None, 0
    for q, tiles in enumerate(counts):
        value, start = pieces[at][...], tiles[0]
        for i, count in enumerate(tiles[1:]):
            value = jnp.where(pl.program_id(0) < start, value, pieces[at + 1 + i][...])
            start += count
        at += len(tiles)
        top, rest = halves(value)
        depth = pl.ds(q * value.shape[1], value.shape[1])
        t_top, t_rest = top_ref[:, depth], rest_ref[:, depth]
        term = dot(t_top, rest) + dot(t_rest, top) + dot(t_top, top)
        total = term if total is None else total + term
    out_ref[...] = 0.5 * total


def product(place, amplitudes, quarters):
    last = amplitudes[-1]
    rows, part = math.prod(last.shape[:3]), last.shape[3]
    depth = 4 * part
    columns = sum(piece.shape[0] for piece in quarters[0])
    specs, counts = [], []
    for quarter in quarters:
        start, tiles = 0, []
        for piece in quarter:
            count = pl.cdiv(piece.shape[0], TILE)
            specs.append(
                pl.BlockSpec(
                    (TILE, part),
                    lambda n, place, start=start, count=count: (jnp.clip(n - start, 0, count - 1), 0),
                )
            )
            tiles.append(count)
            start += count
        counts.append(tiles)
    whole = [
        pl.BlockSpec(v.shape, lambda n, place, v=v: (0,) * v.ndim, pipeline_mode=pl.Buffered(1))
        for v in amplitudes
    ]
    return pl.pallas_call(
        functools.partial(product_kernel, counts),
        grid_spec=pltpu.PrefetchScalarGridSpec(
            num_scalar_prefetch=1,
            grid=(pl.cdiv(columns, TILE),),
            in_specs=whole + specs,
            out_specs=pl.BlockSpec((rows, TILE), lambda n, place: (0, n)),
            scratch_shapes=[pltpu.VMEM((rows, depth), jnp.bfloat16)] * 2,
        ),
        out_shape=jax.ShapeDtypeStruct((rows, columns), jnp.float32),
        compiler_params=pltpu.CompilerParams(vmem_limit_bytes=60 << 20),
        cost_estimate=pl.CostEstimate(
            flops=6 * rows * depth * columns,
            bytes_accessed=4 * (rows * depth + depth * columns + rows * columns),
            transcendentals=0,
        ),
    )(place, *amplitudes, *[piece for quarter in quarters for piece in quarter])


def place_kernel(count, at_ref, *refs):
    blocks, out_ref = refs[:count], refs[-1]
    width = sum(ref.shape[2] for ref in blocks)
    for s in range(GROUP):
        start = s * width
        for ref in blocks:
            out_ref[:, start : start + ref.shape[2]] = ref[s]
            start += ref.shape[2]


def place(at, blocks, out=None):
    sources, rows, _ = blocks[0].shape
    width = sum(block.shape[2] for block in blocks)
    steps = sources // GROUP
    count = len(blocks)
    return pl.pallas_call(
        functools.partial(place_kernel, count),
        grid_spec=pltpu.PrefetchScalarGridSpec(
            num_scalar_prefetch=1,
            grid=(steps,),
            in_specs=[
                pl.BlockSpec((GROUP, rows, block.shape[2]), lambda g, at: (g, 0, 0))
                for block in blocks
            ]
            + ([] if out is None else [pl.BlockSpec(memory_space=pl.ANY)]),
            out_specs=pl.BlockSpec((rows, GROUP * width), lambda g, at: (0, at[0] * steps + g)),
        ),
        out_shape=jax.ShapeDtypeStruct((rows, 2 * sources * width), jnp.float32),
        input_output_aliases={} if out is None else {1 + count: 0},
        compiler_params=pltpu.CompilerParams(vmem_limit_bytes=16 << 20),
        cost_estimate=pl.CostEstimate(
            flops=0, bytes_accessed=8 * sources * rows * width, transcendentals=0
        ),
    )(at, *blocks, *([] if out is None else [out]))


def gather_amplitudes(amplitudes):
    rows, depth = amplitudes.shape
    part = depth // 4
    last = amplitudes[:, 3 * part :]
    last = jnp.concatenate([last] + [shift_x(last, -d) for d in (1, 2, 3)])
    last = lax.all_gather(last, "z", axis=0).reshape(8, 4, rows, part)
    here = jnp.broadcast_to(amplitudes[None, :, : 3 * part], (8, rows, 3 * part))
    here = lax.all_to_all(here, "z", split_axis=0, concat_axis=0, tiled=True).reshape(-1, 3 * part)
    ahead, behind = shift_x(here, -1), shift_x(here, 1)
    half = here.shape[0] // 2
    low, high = shift_x(ahead[:half], -1), shift_x(behind[half:], 1)
    return [here, ahead, behind, low, high, last]


def on_device(amplitudes, integrals):
    x, yl, yh, core = (lax.axis_index(name) for name in ("x", "yl", "yh", "core"))
    rows = amplitudes.shape[0]
    columns = integrals.shape[1]
    spot = jnp.stack([2 * yh + core, x])
    t = gather_amplitudes(amplitudes)

    own = [integrals.T[:CUT], integrals.T[CUT:]]
    near, far = [swap_near(v) for v in own], [swap_far(v) for v in own]
    across = [swap_far(near[0]), swap_near(far[1])]

    def exchange(v):
        return lax.all_to_all(
            v.reshape(-1, rows, v.shape[1]), ("x", "z"), split_axis=0, concat_axis=0, tiled=True
        )

    other_block = [
        exchange(product(spot, t, [[n], [swap_core(n)], [f], [swap_core(f)]]))
        for n, f in zip(near, far)
    ]
    own2, across2 = [swap_core(v) for v in own], [swap_core(v) for v in across]
    own_block = exchange(product(spot, t, [own, own2, across, across2]))
    out = place((1 - yl).reshape(1), other_block)
    return place(yl.reshape(1), [own_block], out)


def solution(mesh):
    grid = Mesh(mesh.devices.reshape(2, 4, 8, 2, 2), AXES)
    return jax.shard_map(
        on_device,
        mesh=grid,
        in_specs=(P(AXES, None), P(("yh", "core"), ("yl", "x", "z"))),
        out_specs=P(AXES, None),
        check_vma=False,
    )
```

time: 271 us -> 258 us (0.952)
  waiting for transfers between devices: 197 us -> 141 us
  starting transfers between devices: 14.9 us -> 40.6 us
  Pallas kernels: 34.5 us -> 42.8 us
  local copies, waits for them, and re-layouts: 11 us -> 17.7 us
    ppermute x2 -> x3, waiting for transfers between devices: 62 us -> 9.2 us  [swap_near(): return lax.ppermute(value, 'yl', [(0, 1), (1, 0)])]
    ppermute x2 -> x3, waiting for transfers between devices: 33.3 us -> 6.91 us  [swap_far(): return lax.ppermute(value, ('yl', 'yh'), [(2, 1), (1, 2), (3, 0), (0, 3)])]
    ppermute x0 -> x7, waiting for transfers between devices: none -> 26.4 us  [shift_x(): return lax.ppermute(value, 'x', [(i, (i + by) % 4) for i in range(4)])]
    all_gather x1, waiting for transfers between devices: 21.2 us -> 0.01 us  [gather_amplitudes(): last = lax.all_gather(last, 'z', axis=0).reshape(8, 4, rows, part)]
    all_to_all x2 -> x4, waiting for transfers between devices: 74.8 us -> 91.3 us  [the longest x3 82.1 us: exchange(): lax.all_to_all(v.reshape(-1, rows, v.shape[1]), ('x', 'z'), split_axis=0,...]
    all_to_all x2 -> x4, starting transfers between devices: 10.6 us -> 23.1 us  [the longest x3 14.6 us: exchange(): lax.all_to_all(v.reshape(-1, rows, v.shape[1]), ('x', 'z'), split_axis=0,...]
    ppermute x0 -> x7, starting transfers between devices: none -> 12.2 us  [shift_x(): return lax.ppermute(value, 'x', [(i, (i + by) % 4) for i in range(4)])]
    pallas_call x5, Pallas kernels: 34.5 us -> 42.8 us  [the longest x3 38.8 us: product(): pl.pallas_call(functools.partial(product_kernel, counts), grid_spec=pltpu...]
  transfers between devices with their start and end apart: 12 -> 26, of which waited for: 7 -> 18; matrix products, arithmetic and copies ran while one was open for 1% -> 2% of each run, Pallas kernels for 7% -> 16%
where the time goes in v2:
time: 258 us; the launch traced here: 257 us
  waiting for transfers between devices  141 us (55%)
  Pallas kernels  42.8 us (17%)
  starting transfers between devices  40.6 us (16%)
  local copies, waits for them, and re-layouts  17.7 us (7%)
  between operations  13.5 us (5%)
    all_to_all x3, waiting for transfers between devices, exchange(): lax.all_to_all(v.reshape(-1, rows, v.shape[1]), ('x', 'z'), split_axis=0,...  82.1 us
    pallas_call x3, Pallas kernels, product(): pl.pallas_call(functools.partial(product_kernel, counts), grid_spec=pltpu...  38.8 us
    ppermute x7, waiting for transfers between devices, shift_x(): return lax.ppermute(value, 'x', [(i, (i + by) % 4) for i in range(4)])  26.4 us
    all_to_all x3, starting transfers between devices, exchange(): lax.all_to_all(v.reshape(-1, rows, v.shape[1]), ('x', 'z'), split_axis=0,...  14.6 us
    ppermute x7, starting transfers between devices, shift_x(): return lax.ppermute(value, 'x', [(i, (i + by) % 4) for i in range(4)])  12.2 us
    unnamed x28, local copies, waits for them, and re-layouts  11.1 us
    ppermute x3, waiting for transfers between devices, swap_near(): return lax.ppermute(value, 'yl', [(0, 1), (1, 0)])  9.2 us
    all_to_all x1, waiting for transfers between devices, gather_amplitudes(): lax.all_to_all(here, 'z', split_axis=0, concat_axis=0, tiled=True)  9.16 us
  transfers between devices with their start and end apart: 26, of which 18 were waited for; matrix products, arithmetic and copies ran while one was open for 2% of the time, Pallas kernels for 16%

profile of v2, /device:TPU:24, one launch (start us, length us, event | category | flops | bytes accessed | tf_op | source)
XLA Modules:
  0.0 257.4 jit_solution(17273881327729016974)
XLA Ops:
  8.4 8.5 %all-to-all-start = ((f32[8,16,1536]{2,1,0:T(8,128)}), f32[8,16,1536]{2,1,0:T(8,128)}, u32[]{:S(2)}, u32[]{:S(2)}) async-start(f32[8,16,1536]{2,1,0:T(8,128)} %broadcast_in_dim.2), calls=%async_computation | async-start | bytes 1572864 | tf_op jit(solution)/shard_map/all_to_all | solution.py:175
  16.9 2.6 %slice.27.refs_7_ = f32[632,512]{1,0:T(8,128)} slice(f32[1400,512]{1,0:T(8,128)} %bitcast.11), slice={[768:1400], [0:512]} | slice | bytes 2588672 | tf_op jit(solution)/shard_map/slice | solution.py:189
  22.1 1.5 collective-permute-start.6
  23.6 2.7 %collective-permute-start.5 = (f32[16,512]{1,0:T(8,128)S(1)}, f32[16,512]{1,0:T(8,128)S(1)}, u32[]{:S(2)}, u32[]{:S(2)}) collective-permute-start(f32[16,512]{1,0:T(8,128)S(1)} %slice.21), channel_id=1, source_target_pairs={{0,64},{32,96},{64,0},{96,32},{1,65},{33,97},{65,1},{97,33},{2,66}... | collective-permute-start | bytes 98312 | tf_op jit(solution)/shard_map/ppermute | solution.py:22
  26.3 1.4 collective-permute-start.4
  30.9 9.2 %all-to-all-done = f32[8,16,1536]{2,1,0:T(8,128)} async-done(((f32[8,16,1536]{2,1,0:T(8,128)}), f32[8,16,1536]{2,1,0:T(8,128)}, u32[]{:S(2)}, u32[]{:S(2)}) %all-to-all-start) | async-done | bytes 786464 | tf_op jit(solution)/shard_map/all_to_all | solution.py:175
  40.1 2.8 %collective-permute-start = (f32[128,1536]{1,0:T(8,128)}, f32[128,1536]{1,0:T(8,128)S(1)}, u32[]{:S(2)}, u32[]{:S(2)}) collective-permute-start(f32[128,1536]{1,0:T(8,128)} %bitcast.3.refs_0_), channel_id=1, source_target_pairs={{0,96},{32,0},{64,32},{96,64},{1,97},{33,1},{65,33},{97,65},{2,98}... | collective-permute-start | bytes 2359304 | tf_op jit(solution)/shard_map/ppermute | solution.py:22
  42.8 6.9 %collective-permute-done.18.refs_6_ = f32[632,512]{1,0:T(8,128)} collective-permute-done((f32[632,512]{1,0:T(8,128)}, f32[632,512]{1,0:T(8,128)}, u32[]{:S(2)}, u32[]{:S(2)}) %collective-permute-start.18) | collective-permute-done | bytes 1294368 | tf_op jit(solution)/shard_map/ppermute | solution.py:26
  49.7 1.7 collective-permute-done.11.refs_8_
  51.4 8.7 %collective-permute-done.refs_1_ = f32[128,1536]{1,0:T(8,128)S(1)} collective-permute-done((f32[128,1536]{1,0:T(8,128)}, f32[128,1536]{1,0:T(8,128)S(1)}, u32[]{:S(2)}, u32[]{:S(2)}) %collective-permute-start) | collective-permute-done | bytes 786464 | tf_op jit(solution)/shard_map/ppermute | solution.py:22
  61.0 3.7 %collective-permute-start.2 = (f32[64,1536]{1,0:T(8,128)S(1)}, f32[64,1536]{1,0:T(8,128)S(1)}, u32[]{:S(2)}, u32[]{:S(2)}) collective-permute-start(f32[64,1536]{1,0:T(8,128)S(1)} %slice.24), channel_id=1, source_target_pairs={{0,96},{32,0},{64,32},{96,64},{1,97},{33,1},{65,33},{97,65},{2,98}... | collective-permute-start | bytes 1179656 | tf_op jit(solution)/shard_map/ppermute | solution.py:22
  64.7 1.3 slice.26.refs_6_
  67.8 4.6 %collective-permute-done.2.refs_3_ = f32[64,1536]{1,0:T(8,128)S(1)} collective-permute-done((f32[64,1536]{1,0:T(8,128)S(1)}, f32[64,1536]{1,0:T(8,128)S(1)}, u32[]{:S(2)}, u32[]{:S(2)}) %collective-permute-start.2) | collective-permute-done | bytes 393248 | tf_op jit(solution)/shard_map/ppermute | solution.py:22
  73.2 10.6 %collective-permute-done.3.refs_4_ = f32[64,1536]{1,0:T(8,128)S(1)} collective-permute-done((f32[64,1536]{1,0:T(8,128)S(1)}, f32[64,1536]{1,0:T(8,128)S(1)}, u32[]{:S(2)}, u32[]{:S(2)}) %collective-permute-start.3) | collective-permute-done | bytes 393248 | tf_op jit(solution)/shard_map/ppermute | solution.py:22
  84.5 10.6 %shard_map.30 = f32[512,632]{1,0:T(8,128)} custom-call(s32[2]{0:T(128)} %pad_add_fusion.place_ref, f32[128,1536]{1,0:T(8,128)} %bitcast.3.refs_0_, f32[128,1536]{1,0:T(8,128)} %copy-done.5, f32[128,1536]{1,0:T(8,128)} %copy-done.6, f32[64,1536]{1,0:T(8,128)} %copy-done.12, f32[64,1536]{1,0:T(8,128)} %copy-done.13, f32[8,4,16,512]{3,2,1,0:T(8,128)} %bitcast.15, ...), custom_call_target="tpu_custom_call" | custom-call | flops 3976200192 | bytes 10665984 | tf_op jit(solution)/shard_map/pallas_call | solution.py:113
  95.1 4.0 %all-to-all-start.3 = ((f32[32,16,632]{2,1,0:T(8,128)}), f32[32,16,632]{2,1,0:T(8,128)S(1)}, u32[]{:S(2)}, u32[]{:S(2)}) async-start(f32[32,16,632]{2,1,0:T(8,128)} %bitcast.14), calls=%async_computation.3 | async-start | bytes 2621440 | tf_op jit(solution)/shard_map/all_to_all | solution.py:194
  99.1 2.3 collective-permute-done.9.refs_6_
  101.4 1.8 collective-permute-done.16.refs_8_
  105.9 1.5 collective-permute-done.17.refs_9_
  107.4 10.9 %shard_map.29 = f32[512,768]{1,0:T(8,128)} custom-call(s32[2]{0:T(128)} %pad_add_fusion.place_ref, f32[128,1536]{1,0:T(8,128)} %bitcast.3.refs_0_, f32[128,1536]{1,0:T(8,128)} %copy-done.5, f32[128,1536]{1,0:T(8,128)} %copy-done.6, f32[64,1536]{1,0:T(8,128)} %copy-done.12, f32[64,1536]{1,0:T(8,128)} %copy-done.13, f32[8,4,16,512]{3,2,1,0:T(8,128)} %bitcast.16, ...), custom_call_target="tpu_custom_call" | custom-call | flops 4831838208 | bytes 12058624 | tf_op jit(solution)/shard_map/pallas_call | solution.py:113
  118.2 12.9 %all-to-all-done.3.refs_1_ = f32[32,16,632]{2,1,0:T(8,128)S(1)} async-done(((f32[32,16,632]{2,1,0:T(8,128)}), f32[32,16,632]{2,1,0:T(8,128)S(1)}, u32[]{:S(2)}, u32[]{:S(2)}) %all-to-all-start.3) | async-done | bytes 1294368 | tf_op jit(solution)/shard_map/all_to_all | solution.py:194
  132.2 5.5 %all-to-all-start.2 = ((f32[32,16,768]{2,1,0:T(8,128)}), f32[32,16,768]{2,1,0:T(8,128)S(1)}, u32[]{:S(2)}, u32[]{:S(2)}) async-start(f32[32,16,768]{2,1,0:T(8,128)} %bitcast.13), calls=%async_computation.2 | async-start | bytes 3145728 | tf_op jit(solution)/shard_map/all_to_all | solution.py:194
  137.8 3.5 %collective-permute-done.10.refs_10_ = f32[768,512]{1,0:T(8,128)} collective-permute-done((f32[768,512]{1,0:T(8,128)S(1)}, f32[768,512]{1,0:T(8,128)}, u32[]{:S(2)}, u32[]{:S(2)}) %collective-permute-start.10) | collective-permute-done | bytes 1572896 | tf_op jit(solution)/shard_map/ppermute | solution.py:30
  141.8 5.0 %collective-permute-done.8.refs_9_ = f32[632,512]{1,0:T(8,128)S(1)} collective-permute-done((f32[632,512]{1,0:T(8,128)}, f32[632,512]{1,0:T(8,128)S(1)}, u32[]{:S(2)}, u32[]{:S(2)}) %collective-permute-start.8) | collective-permute-done | bytes 1294368 | tf_op jit(solution)/shard_map/ppermute | solution.py:18
  150.9 17.4 %shard_map.28 = f32[512,1400]{1,0:T(8,128)} custom-call(s32[2]{0:T(128)} %pad_add_fusion.place_ref, f32[128,1536]{1,0:T(8,128)} %bitcast.3.refs_0_, f32[128,1536]{1,0:T(8,128)} %copy-done.5, f32[128,1536]{1,0:T(8,128)} %copy-done.6, f32[64,1536]{1,0:T(8,128)} %copy-done.12, f32[64,1536]{1,0:T(8,128)} %copy-done.13, f32[8,4,16,512]{3,2,1,0:T(8,128)} %bitcast.17, ...), custom_call_target="tpu_custom_call" | custom-call | flops 8808038400 | bytes 18530304 | tf_op jit(solution)/shard_map/pallas_call | solution.py:113
  168.3 7.0 %all-to-all-done.2.refs_0_ = f32[32,16,768]{2,1,0:T(8,128)S(1)} async-done(((f32[32,16,768]{2,1,0:T(8,128)}), f32[32,16,768]{2,1,0:T(8,128)S(1)}, u32[]{:S(2)}, u32[]{:S(2)}) %all-to-all-start.2) | async-done | bytes 1572896 | tf_op jit(solution)/shard_map/all_to_all | solution.py:194
  176.5 5.1 %all-to-all-start.1 = ((f32[32,16,1400]{2,1,0:T(8,128)}), f32[32,16,1400]{2,1,0:T(8,128)S(1)}, u32[]{:S(2)}, u32[]{:S(2)}) async-start(f32[32,16,1400]{2,1,0:T(8,128)} %bitcast.10), calls=%async_computation.1 | async-start | bytes 5767168 | tf_op jit(solution)/shard_map/all_to_all | solution.py:194
  181.6 1.4 copy-done.1
  183.0 1.3 copy-done.3
  184.4 2.0 shard_map.31.refs_1_
  186.3 62.2 %all-to-all-done.1.refs_0_ = f32[32,16,1400]{2,1,0:T(8,128)S(1)} async-done(((f32[32,16,1400]{2,1,0:T(8,128)}), f32[32,16,1400]{2,1,0:T(8,128)S(1)}, u32[]{:S(2)}, u32[]{:S(2)}) %all-to-all-start.1) | async-done | bytes 2867232 | tf_op jit(solution)/shard_map/all_to_all | solution.py:194
  248.5 2.0 shard_map.32
  (63 shorter events, 21.6 us)
Async XLA Ops:
  8.4 31.7 %all-to-all-start = ((f32[8,16,1536]{2,1,0:T(8,128)}), f32[8,16,1536]{2,1,0:T(8,128)}, u32[]{:S(2)}, u32[]{:S(2)}) async-start(f32[8,16,1536]{2,1,0:T(8,128)} %broadcast_in_dim.2), calls=%async_computation | async-start | bytes 1572864 | tf_op jit(solution)/shard_map/all_to_all | solution.py:175
  16.9 56.3 %all-gather.3.cloned.1.call-start = ((), (), s32[]{:S(2)}) async-start(), calls=%async_computation.4 | async-start | bytes 1179648 | tf_op jit(solution)/shard_map/all_gather | solution.py:173
  16.9 47.8 %copy-start.4 = (f32[512,1400]{0,1:T(8,128)S(1)}, f32[512,1400]{0,1:T(8,128)}, u32[]{:S(2)}) copy-start(f32[512,1400]{0,1:T(8,128)} %param.3) | copy-start | bytes 8601604
  19.5 30.2 %collective-permute-start.18 = (f32[632,512]{1,0:T(8,128)}, f32[632,512]{1,0:T(8,128)}, u32[]{:S(2)}, u32[]{:S(2)}) collective-permute-start(f32[632,512]{1,0:T(8,128)} %slice.27.refs_7_), channel_id=1, source_target_pairs={{0,128},{128,0},{1,129},{129,1},{2,130},{130,2},{3,131},{131,3},{4... | collective-permute-start | bytes 3883016 | tf_op jit(solution)/shard_map/ppermute | solution.py:26
  20.3 31.1 %collective-permute-start.11 = (f32[632,512]{1,0:T(8,128)}, f32[632,512]{1,0:T(8,128)}, u32[]{:S(2)}, u32[]{:S(2)}) collective-permute-start(f32[632,512]{1,0:T(8,128)} %slice.27.refs_7_), channel_id=1, source_target_pairs={{128,2},{2,128},{130,0},{0,130},{129,3},{3,129},{131,1},{1,131},{1... | collective-permute-start | bytes 3883016 | tf_op jit(solution)/shard_map/ppermute | solution.py:30
  22.1 5.7 %collective-permute-start.6 = (f32[16,512]{1,0:T(8,128)S(1)}, f32[16,512]{1,0:T(8,128)S(1)}, u32[]{:S(2)}, u32[]{:S(2)}) collective-permute-start(f32[16,512]{1,0:T(8,128)S(1)} %slice.21), channel_id=1, source_target_pairs={{0,32},{32,64},{64,96},{96,0},{1,33},{33,65},{65,97},{97,1},{2,34}... | collective-permute-start | bytes 98312 | tf_op jit(solution)/shard_map/ppermute | solution.py:22
  23.6 5.4 %collective-permute-start.5 = (f32[16,512]{1,0:T(8,128)S(1)}, f32[16,512]{1,0:T(8,128)S(1)}, u32[]{:S(2)}, u32[]{:S(2)}) collective-permute-start(f32[16,512]{1,0:T(8,128)S(1)} %slice.21), channel_id=1, source_target_pairs={{0,64},{32,96},{64,0},{96,32},{1,65},{33,97},{65,1},{97,33},{2,66}... | collective-permute-start | bytes 98312 | tf_op jit(solution)/shard_map/ppermute | solution.py:22
  26.3 3.9 %collective-permute-start.4 = (f32[16,512]{1,0:T(8,128)S(1)}, f32[16,512]{1,0:T(8,128)S(1)}, u32[]{:S(2)}, u32[]{:S(2)}) collective-permute-start(f32[16,512]{1,0:T(8,128)S(1)} %slice.21), channel_id=1, source_target_pairs={{0,96},{32,0},{64,32},{96,64},{1,97},{33,1},{65,33},{97,65},{2,98}... | collective-permute-start | bytes 98312 | tf_op jit(solution)/shard_map/ppermute | solution.py:22
  40.1 20.1 %collective-permute-start = (f32[128,1536]{1,0:T(8,128)}, f32[128,1536]{1,0:T(8,128)S(1)}, u32[]{:S(2)}, u32[]{:S(2)}) collective-permute-start(f32[128,1536]{1,0:T(8,128)} %bitcast.3.refs_0_), channel_id=1, source_target_pairs={{0,96},{32,0},{64,32},{96,64},{1,97},{33,1},{65,33},{97,65},{2,98}... | collective-permute-start | bytes 2359304 | tf_op jit(solution)/shard_map/ppermute | solution.py:22
  42.8 23.9 %collective-permute-start.1 = (f32[128,1536]{1,0:T(8,128)}, f32[128,1536]{1,0:T(8,128)S(1)}, u32[]{:S(2)}, u32[]{:S(2)}) collective-permute-start(f32[128,1536]{1,0:T(8,128)} %bitcast.3.refs_0_), channel_id=1, source_target_pairs={{0,32},{32,64},{64,96},{96,0},{1,33},{33,65},{65,97},{97,1},{2,34}... | collective-permute-start | bytes 2359304 | tf_op jit(solution)/shard_map/ppermute | solution.py:22
  49.7 34.0 %collective-permute-start.19 = (f32[632,512]{1,0:T(8,128)}, f32[632,512]{1,0:T(8,128)}, u32[]{:S(2)}, u32[]{:S(2)}) collective-permute-start(f32[632,512]{1,0:T(8,128)} %collective-permute-done.18.refs_6_), channel_id=1, source_target_pairs={{0,1},{1,0},{2,3},{3,2},{4,5},{5,4},{6,7},{7,6},{8,9},{9,8},{10,11... | collective-permute-start | bytes 3883016 | tf_op jit(solution)/shard_map/ppermute | solution.py:18
  51.4 32.3 %collective-permute-start.20 = (f32[632,512]{1,0:T(8,128)}, f32[632,512]{1,0:T(8,128)}, u32[]{:S(2)}, u32[]{:S(2)}) collective-permute-start(f32[632,512]{1,0:T(8,128)} %collective-permute-done.11.refs_8_), channel_id=1, source_target_pairs={{0,1},{1,0},{2,3},{3,2},{4,5},{5,4},{6,7},{7,6},{8,9},{9,8},{10,11... | collective-permute-start | bytes 3883016 | tf_op jit(solution)/shard_map/ppermute | solution.py:18
  61.0 11.4 %collective-permute-start.2 = (f32[64,1536]{1,0:T(8,128)S(1)}, f32[64,1536]{1,0:T(8,128)S(1)}, u32[]{:S(2)}, u32[]{:S(2)}) collective-permute-start(f32[64,1536]{1,0:T(8,128)S(1)} %slice.24), channel_id=1, source_target_pairs={{0,96},{32,0},{64,32},{96,64},{1,97},{33,1},{65,33},{97,65},{2,98}... | collective-permute-start | bytes 1179656 | tf_op jit(solution)/shard_map/ppermute | solution.py:22
  66.0 35.4 %collective-permute-start.9 = (f32[768,512]{1,0:T(8,128)}, f32[768,512]{1,0:T(8,128)S(1)}, u32[]{:S(2)}, u32[]{:S(2)}) collective-permute-start(f32[768,512]{1,0:T(8,128)} %slice.26.refs_6_), channel_id=1, source_target_pairs={{0,128},{128,0},{1,129},{129,1},{2,130},{130,2},{3,131},{131,3},{4... | collective-permute-start | bytes 4718600 | tf_op jit(solution)/shard_map/ppermute | solution.py:26
  66.7 5.8 %copy-start.6 = (f32[128,1536]{1,0:T(8,128)}, f32[128,1536]{1,0:T(8,128)S(1)}, u32[]{:S(2)}) copy-start(f32[128,1536]{1,0:T(8,128)S(1)} %collective-permute-done.1.refs_2_) | copy-start | bytes 2359300
  66.7 36.4 %collective-permute-start.16 = (f32[768,512]{1,0:T(8,128)}, f32[768,512]{1,0:T(8,128)}, u32[]{:S(2)}, u32[]{:S(2)}) collective-permute-start(f32[768,512]{1,0:T(8,128)} %slice.26.refs_6_), channel_id=1, source_target_pairs={{128,2},{2,128},{130,0},{0,130},{129,3},{3,129},{131,1},{1,131},{1... | collective-permute-start | bytes 4718600 | tf_op jit(solution)/shard_map/ppermute | solution.py:30
  72.4 11.3 %copy-start.12 = (f32[64,1536]{1,0:T(8,128)}, f32[64,1536]{1,0:T(8,128)S(1)}, u32[]{:S(2)}) copy-start(f32[64,1536]{1,0:T(8,128)S(1)} %collective-permute-done.2.refs_3_) | copy-start | bytes 1179652
  72.4 11.3 %collective-permute-start.3 = (f32[64,1536]{1,0:T(8,128)S(1)}, f32[64,1536]{1,0:T(8,128)S(1)}, u32[]{:S(2)}, u32[]{:S(2)}) collective-permute-start(f32[64,1536]{1,0:T(8,128)S(1)} %slice.25), channel_id=1, source_target_pairs={{0,32},{32,64},{64,96},{96,0},{1,33},{33,65},{65,97},{97,1},{2,34}... | collective-permute-start | bytes 1179656 | tf_op jit(solution)/shard_map/ppermute | solution.py:22
  95.1 36.0 %all-to-all-start.3 = ((f32[32,16,632]{2,1,0:T(8,128)}), f32[32,16,632]{2,1,0:T(8,128)S(1)}, u32[]{:S(2)}, u32[]{:S(2)}) async-start(f32[32,16,632]{2,1,0:T(8,128)} %bitcast.14), calls=%async_computation.3 | async-start | bytes 2621440 | tf_op jit(solution)/shard_map/all_to_all | solution.py:194
  101.4 6.0 %copy-start.7 = (f32[768,512]{1,0:T(8,128)}, f32[768,512]{1,0:T(8,128)S(1)}, u32[]{:S(2)}) copy-start(f32[768,512]{1,0:T(8,128)S(1)} %collective-permute-done.9.refs_6_) | copy-start | bytes 4718596
  101.4 3.4 %collective-permute-start.15 = (f32[768,512]{1,0:T(8,128)S(1)}, f32[768,512]{1,0:T(8,128)S(1)}, u32[]{:S(2)}, u32[]{:S(2)}) collective-permute-start(f32[768,512]{1,0:T(8,128)S(1)} %collective-permute-done.9.refs_6_), channel_id=1, source_target_pairs={{0,1},{1,0},{2,3},{3,2},{4,5},{5,4},{6,7},{7,6},{8,9},{9,8},{10,11... | collective-permute-start | bytes 4718600 | tf_op jit(solution)/shard_map/ppermute | solution.py:18
  103.1 4.2 %collective-permute-start.17 = (f32[768,512]{1,0:T(8,128)}, f32[768,512]{1,0:T(8,128)}, u32[]{:S(2)}, u32[]{:S(2)}) collective-permute-start(f32[768,512]{1,0:T(8,128)} %collective-permute-done.16.refs_8_), channel_id=1, source_target_pairs={{0,1},{1,0},{2,3},{3,2},{4,5},{5,4},{6,7},{7,6},{8,9},{9,8},{10,11... | collective-permute-start | bytes 4718600 | tf_op jit(solution)/shard_map/ppermute | solution.py:18
  103.1 38.1 %collective-permute-start.10 = (f32[768,512]{1,0:T(8,128)S(1)}, f32[768,512]{1,0:T(8,128)}, u32[]{:S(2)}, u32[]{:S(2)}) collective-permute-start(f32[768,512]{1,0:T(8,128)S(1)} %collective-permute-done.9.refs_6_), channel_id=1, source_target_pairs={{128,2},{2,128},{130,0},{0,130},{129,3},{3,129},{131,1},{1,131},{1... | collective-permute-start | bytes 4718600 | tf_op jit(solution)/shard_map/ppermute | solution.py:30
  104.2 37.6 %collective-permute-start.12 = (f32[632,512]{1,0:T(8,128)}, f32[632,512]{1,0:T(8,128)}, u32[]{:S(2)}, u32[]{:S(2)}) collective-permute-start(f32[632,512]{1,0:T(8,128)} %collective-permute-done.11.refs_8_), channel_id=1, source_target_pairs={{0,128},{128,0},{1,129},{129,1},{2,130},{130,2},{3,131},{131,3},{4... | collective-permute-start | bytes 3883016 | tf_op jit(solution)/shard_map/ppermute | solution.py:26
  132.2 43.2 %all-to-all-start.2 = ((f32[32,16,768]{2,1,0:T(8,128)}), f32[32,16,768]{2,1,0:T(8,128)S(1)}, u32[]{:S(2)}, u32[]{:S(2)}) async-start(f32[32,16,768]{2,1,0:T(8,128)} %bitcast.13), calls=%async_computation.2 | async-start | bytes 3145728 | tf_op jit(solution)/shard_map/all_to_all | solution.py:194
  137.7 9.0 %collective-permute-start.7 = (f32[768,512]{1,0:T(8,128)}, f32[768,512]{1,0:T(8,128)}, u32[]{:S(2)}, u32[]{:S(2)}) collective-permute-start(f32[768,512]{1,0:T(8,128)} %slice.26.refs_6_), channel_id=1, source_target_pairs={{0,1},{1,0},{2,3},{3,2},{4,5},{5,4},{6,7},{7,6},{8,9},{9,8},{10,11... | collective-permute-start | bytes 4718600 | tf_op jit(solution)/shard_map/ppermute | solution.py:18
  141.3 8.4 %collective-permute-start.13 = (f32[768,512]{1,0:T(8,128)}, f32[768,512]{1,0:T(8,128)S(1)}, u32[]{:S(2)}, u32[]{:S(2)}) collective-permute-start(f32[768,512]{1,0:T(8,128)} %collective-permute-done.10.refs_10_), channel_id=1, source_target_pairs={{0,1},{1,0},{2,3},{3,2},{4,5},{5,4},{6,7},{7,6},{8,9},{9,8},{10,11... | collective-permute-start | bytes 4718600 | tf_op jit(solution)/shard_map/ppermute | solution.py:18
  141.3 5.5 %collective-permute-start.8 = (f32[632,512]{1,0:T(8,128)}, f32[632,512]{1,0:T(8,128)S(1)}, u32[]{:S(2)}, u32[]{:S(2)}) collective-permute-start(f32[632,512]{1,0:T(8,128)} %slice.27.refs_7_), channel_id=1, source_target_pairs={{0,1},{1,0},{2,3},{3,2},{4,5},{5,4},{6,7},{7,6},{8,9},{9,8},{10,11... | collective-permute-start | bytes 3883016 | tf_op jit(solution)/shard_map/ppermute | solution.py:18
  141.8 6.8 %collective-permute-start.14 = (f32[632,512]{1,0:T(8,128)}, f32[632,512]{1,0:T(8,128)S(1)}, u32[]{:S(2)}, u32[]{:S(2)}) collective-permute-start(f32[632,512]{1,0:T(8,128)} %collective-permute-done.12.refs_11_), channel_id=1, source_target_pairs={{0,1},{1,0},{2,3},{3,2},{4,5},{5,4},{6,7},{7,6},{8,9},{9,8},{10,11... | collective-permute-start | bytes 3883016 | tf_op jit(solution)/shard_map/ppermute | solution.py:18
  176.5 72.1 %all-to-all-start.1 = ((f32[32,16,1400]{2,1,0:T(8,128)}), f32[32,16,1400]{2,1,0:T(8,128)S(1)}, u32[]{:S(2)}, u32[]{:S(2)}) async-start(f32[32,16,1400]{2,1,0:T(8,128)} %bitcast.10), calls=%async_computation.1 | async-start | bytes 5767168 | tf_op jit(solution)/shard_map/all_to_all | solution.py:194
  181.6 1.4 copy-start.1
  183.0 1.3 copy-start.3
  (8 other events, 8.4 us)
Sparse Core Ops, SparseCore 0:
  31.0 39.5 all-gather.2

commit v3 on v2

v3 whole, which is shorter than its diff:
```python
import functools
import math

import jax
import jax.numpy as jnp
from jax import lax
from jax.experimental import pallas as pl
from jax.experimental.pallas import tpu as pltpu
from jax.sharding import Mesh, PartitionSpec as P

AXES = ("yl", "x", "z", "yh", "core")
TILE = 256
CUT = 768
ORDER = (1, 7, 3, 5, 2, 6, 4)
GROUP = 16


def swap_core(value):
    return lax.ppermute(value, "core", [(0, 1), (1, 0)])


def shift_x(value, by):
    return lax.ppermute(value, "x", [(i, (i + by) % 4) for i in range(4)])


def shift_z(value, by):
    return lax.ppermute(value, "z", [(i, (i + by) % 8) for i in range(8)])


def swap_near(value):
    return lax.ppermute(value, "yl", [(0, 1), (1, 0)])


def swap_far(value):
    return lax.ppermute(value, ("yl", "yh"), [(2, 1), (1, 2), (3, 0), (0, 3)])


def halves(value):
    top = value.astype(jnp.bfloat16)
    rest = (value - top.astype(jnp.float32)).astype(jnp.bfloat16)
    return top, rest


def load_amplitudes(place_ref, around, first_refs, last_ref, top_ref, rest_ref):
    here_ref, ahead_ref, low_ref, high_ref, behind_ref = first_refs
    own, x, z = place_ref[0], place_ref[1], place_ref[2]
    heights, _, rows, half = last_ref.shape
    part = half // 2

    @pl.loop(0, 4 * heights)
    def _(i):
        q, there = i // heights, lax.rem(i, heights)
        source = own ^ q
        take = pl.ds(pl.multiple_of((source & 1) * part, part), part)
        into = pl.ds(pl.multiple_of(q * part, part), part)
        below = there < heights // 2
        opposite = jnp.where(
            below,
            low_ref[jnp.minimum(there, heights // 2 - 1), :, take],
            high_ref[jnp.maximum(there - heights // 2, 0), :, take],
        )
        first = [here_ref[there, :, take], ahead_ref[there, :, take], opposite, behind_ref[there, :, take]]
        for d in range(4):
            value = jnp.where(source < 2, first[d], last_ref[there, d, :, take])
            if around:
                row = lax.rem(there - z + heights, heights) * (4 * rows) + d * rows
            else:
                row = lax.rem(x + d, 4) * (heights * rows) + there * rows
            into_rows = pl.ds(pl.multiple_of(row, rows), rows)
            top_ref[into_rows, into], rest_ref[into_rows, into] = halves(value)


def product_kernel(around, counts, place_ref, *refs):
    pieces = refs[6 : 6 + sum(len(tiles) for tiles in counts)]
    outs, (top_ref, rest_ref) = refs[6 + len(pieces) : -2], refs[-2:]

    @pl.when(pl.program_id(0) == 0)
    def _():
        load_amplitudes(place_ref, around, refs[:5], refs[5], top_ref, rest_ref)

    dot = functools.partial(
        lax.dot_general,
        dimension_numbers=(((1,), (1,)), ((), ())),
        preferred_element_type=jnp.float32,
    )
    total, at = None, 0
    for q, tiles in enumerate(counts):
        value, start = pieces[at][...], tiles[0]
        for i, count in enumerate(tiles[1:]):
            value = jnp.where(pl.program_id(0) < start, value, pieces[at + 1 + i][...])
            start += count
        at += len(tiles)
        top, rest = halves(value)
        depth = pl.ds(q * value.shape[1], value.shape[1])
        t_top, t_rest = top_ref[:, depth], rest_ref[:, depth]
        term = dot(t_top, rest) + dot(t_rest, top) + dot(t_top, top)
        total = term if total is None else total + term
    count = total.shape[0] // len(outs)
    for i, out_ref in enumerate(outs):
        out_ref[...] = 0.5 * total[i * count : (i + 1) * count]


def product(place, amplitudes, quarters, around=False):
    last = amplitudes[-1]
    rows, depth = math.prod(last.shape[:3]), 2 * last.shape[3]
    part = depth // 4
    outs = last.shape[0] if around else 1
    columns = sum(piece.shape[0] for piece in quarters[0])
    specs, counts = [], []
    for quarter in quarters:
        start, tiles = 0, []
        for piece in quarter:
            count = pl.cdiv(piece.shape[0], TILE)
            specs.append(
                pl.BlockSpec(
                    (TILE, part),
                    lambda n, place, start=start, count=count: (jnp.clip(n - start, 0, count - 1), 0),
                )
            )
            tiles.append(count)
            start += count
        counts.append(tiles)
    whole = [
        pl.BlockSpec(v.shape, lambda n, place, v=v: (0,) * v.ndim, pipeline_mode=pl.Buffered(1))
        for v in amplitudes
    ]
    return pl.pallas_call(
        functools.partial(product_kernel, around, counts),
        grid_spec=pltpu.PrefetchScalarGridSpec(
            num_scalar_prefetch=1,
            grid=(pl.cdiv(columns, TILE),),
            in_specs=whole + specs,
            out_specs=[pl.BlockSpec((rows // outs, TILE), lambda n, place: (0, n))] * outs,
            scratch_shapes=[pltpu.VMEM((rows, depth), jnp.bfloat16)] * 2,
        ),
        out_shape=[jax.ShapeDtypeStruct((rows // outs, columns), jnp.float32)] * outs,
        compiler_params=pltpu.CompilerParams(vmem_limit_bytes=60 << 20),
        cost_estimate=pl.CostEstimate(
            flops=6 * rows * depth * columns,
            bytes_accessed=4 * (rows * depth + depth * columns + rows * columns),
            transcendentals=0,
        ),
    )(place, *amplitudes, *[piece for quarter in quarters for piece in quarter])


def regroup_kernel(chunks, z_ref, *refs):
    heights = len(refs[: -4]) // chunks
    outs = refs[-4:]
    for e in range(heights):
        source = lax.rem(z_ref[0] - e + heights, heights)
        at = 0
        for c in range(chunks):
            piece_ref = refs[c * heights + e]
            width = piece_ref.shape[2]
            for d, out_ref in enumerate(outs):
                out_ref[source, :, at : at + width] = piece_ref[d]
            at += width


def regroup(z, chunks):
    heights = len(chunks[0])
    _, rows, _ = chunks[0][0].shape
    width = sum(chunk[0].shape[2] for chunk in chunks)
    pieces = [piece for chunk in chunks for piece in chunk]
    return pl.pallas_call(
        functools.partial(regroup_kernel, len(chunks)),
        grid_spec=pltpu.PrefetchScalarGridSpec(
            num_scalar_prefetch=1,
            grid=(1,),
            in_specs=[pl.BlockSpec(v.shape, lambda n, z: (0, 0, 0)) for v in pieces],
            out_specs=[pl.BlockSpec((heights, rows, width), lambda n, z: (0, 0, 0))] * 4,
        ),
        out_shape=[jax.ShapeDtypeStruct((heights, rows, width), jnp.float32)] * 4,
        compiler_params=pltpu.CompilerParams(vmem_limit_bytes=32 << 20),
        cost_estimate=pl.CostEstimate(
            flops=0, bytes_accessed=32 * heights * rows * width, transcendentals=0
        ),
    )(z, *pieces)


def place_kernel(at_ref, block_ref, _, out_ref):
    width = block_ref.shape[2]
    for s in range(GROUP):
        out_ref[:, s * width : (s + 1) * width] = block_ref[s]


def place(at, block, out):
    sources, rows, width = block.shape
    steps = sources // GROUP
    return pl.pallas_call(
        place_kernel,
        grid_spec=pltpu.PrefetchScalarGridSpec(
            num_scalar_prefetch=1,
            grid=(steps,),
            in_specs=[
                pl.BlockSpec((GROUP, rows, width), lambda g, at: (g, 0, 0)),
                pl.BlockSpec(memory_space=pl.ANY),
            ],
            out_specs=pl.BlockSpec((rows, GROUP * width), lambda g, at: (0, at[0] * steps + g)),
        ),
        out_shape=jax.ShapeDtypeStruct(out.shape, jnp.float32),
        input_output_aliases={2: 0},
        compiler_params=pltpu.CompilerParams(vmem_limit_bytes=16 << 20),
        cost_estimate=pl.CostEstimate(
            flops=0, bytes_accessed=8 * sources * rows * width, transcendentals=0
        ),
    )(at, block, out)


def place_by_x_kernel(at_ref, *refs):
    blocks, out_ref, by_source_ref = refs[:-2], refs[-2], refs[-1]
    heights, _, width = blocks[0].shape

    @pl.when(pl.program_id(0) == 0)
    def _():
        for d, ref in enumerate(blocks):
            source = lax.rem(at_ref[1] - d + 4, 4) * heights

            @pl.loop(0, heights)
            def _(s, ref=ref, source=source):
                by_source_ref[source + s] = ref[s]

    for s in range(GROUP):
        out_ref[:, s * width : (s + 1) * width] = by_source_ref[pl.program_id(0) * GROUP + s]


def place_by_x(at, blocks):
    heights, rows, width = blocks[0].shape
    steps = 4 * heights // GROUP
    return pl.pallas_call(
        place_by_x_kernel,
        grid_spec=pltpu.PrefetchScalarGridSpec(
            num_scalar_prefetch=1,
            grid=(steps,),
            in_specs=[pl.BlockSpec((heights, rows, width), lambda g, at: (0, 0, 0))] * 4,
            out_specs=pl.BlockSpec((rows, GROUP * width), lambda g, at: (0, at[0] * steps + g)),
            scratch_shapes=[pltpu.VMEM((4 * heights, rows, width), jnp.float32)],
        ),
        out_shape=jax.ShapeDtypeStruct((rows, 8 * heights * width), jnp.float32),
        compiler_params=pltpu.CompilerParams(vmem_limit_bytes=32 << 20),
        cost_estimate=pl.CostEstimate(
            flops=0, bytes_accessed=32 * heights * rows * width, transcendentals=0
        ),
    )(at, *blocks)


def after(value, *others):
    return lax.optimization_barrier((value, *others))[0]


def on_device(amplitudes, integrals):
    x, z, yl, yh, core = (lax.axis_index(name) for name in ("x", "z", "yl", "yh", "core"))
    rows, depth = amplitudes.shape
    columns = integrals.shape[1]
    half = depth // 2
    spot = jnp.stack([2 * yh + core, x, z])

    turns = [shift_x(amplitudes[:, half:], -d) for d in (1, 2, 3)]
    last = jnp.concatenate([amplitudes[:, half:]] + turns)
    here = jnp.broadcast_to(after(amplitudes[:, :half], turns[2])[None], (8, rows, half))
    here = lax.all_to_all(here, "z", split_axis=0, concat_axis=0, tiled=True)
    here = after(here, last)
    last = lax.all_gather(last, "z", axis=0).reshape(8, 4, rows, half)
    ahead, behind = shift_x(here, -1), shift_x(here, 1)
    low, high = shift_x(ahead[:4], -1), shift_x(behind[4:], 1)
    t = (here, ahead, low, high, behind, last)

    own = after(integrals.T, *turns)
    near, far = swap_near(own), swap_far(own)
    near, far = after((near, far), low, high)
    across = [swap_far(near[:CUT]), swap_near(far[CUT:])]
    results = product(spot, t, [[near], [swap_core(near)], [far], [swap_core(far)]], around=True)
    sent = {e: shift_z(results[e], e) for e in ORDER}
    own2 = swap_core(after(own, here))
    across = after(across, sent[3], sent[5])
    across2 = [swap_core(v) for v in across]
    t = after(t, sent[3], sent[5])
    (own_block,) = product(spot, t, [[own], [own2], across, across2])
    own_block = after(own_block, *sent.values())
    own_block = lax.all_to_all(
        own_block.reshape(32, rows, columns), ("x", "z"), split_axis=0, concat_axis=0, tiled=True
    )
    chunks = [[v.reshape(4, rows, columns) for v in [results[0]] + [sent[e] for e in range(1, 8)]]]
    by_x = regroup(z.reshape(1), chunks)
    by_x = [by_x[0]] + [shift_x(by_x[d], d) for d in (1, 2, 3)]
    out = place_by_x(jnp.stack([1 - yl, x]), by_x)
    return place(yl.reshape(1), own_block, out)


def solution(mesh):
    grid = Mesh(mesh.devices.reshape(2, 4, 8, 2, 2), AXES)
    return jax.shard_map(
        on_device,
        mesh=grid,
        in_specs=(P(AXES, None), P(("yh", "core"), ("yl", "x", "z"))),
        out_specs=P(AXES, None),
        check_vma=False,
    )
```

time: 258 us -> 281 us (1.089)
  starting transfers between devices: 40.6 us -> 60.8 us
    all_to_all x4 -> x2, waiting for transfers between devices: 91.3 us -> 15 us  [the longest x1 15 us: on_device(): here = lax.all_to_all(here, 'z', split_axis=0, concat_axis=0, tiled=True)]
    ppermute x7 -> x10, waiting for transfers between devices: 26.4 us -> 73.9 us  [shift_x(): return lax.ppermute(value, 'x', [(i, (i + by) % 4) for i in range(4)])]
    ppermute x0 -> x7, waiting for transfers between devices: none -> 26.5 us  [shift_z(): return lax.ppermute(value, 'z', [(i, (i + by) % 8) for i in range(8)])]
    ppermute x0 -> x7, starting transfers between devices: none -> 21.4 us  [shift_z(): return lax.ppermute(value, 'z', [(i, (i + by) % 8) for i in range(8)])]
    ppermute x3 -> x2, waiting for transfers between devices: 9.2 us -> 15.6 us  [swap_near(): return lax.ppermute(value, 'yl', [(0, 1), (1, 0)])]
    ppermute x7 -> x10, starting transfers between devices: 12.2 us -> 16.6 us  [shift_x(): return lax.ppermute(value, 'x', [(i, (i + by) % 4) for i in range(4)])]
    all_to_all x4 -> x2, starting transfers between devices: 23.1 us -> 18.7 us  [the longest x1 10.2 us: on_device(): lax.all_to_all(own_block.reshape(32, rows, columns), ('x', 'z'), split_ax...]
    ppermute x8 -> x5, waiting for transfers between devices: 7.72 us -> 4.25 us  [swap_core(): return lax.ppermute(value, 'core', [(0, 1), (1, 0)])]
  transfers between devices with their start and end apart: 26 -> 29, of which waited for: 18 -> 17; matrix products, arithmetic and copies ran while one was open for 2% -> 2% of each run, Pallas kernels for 16% -> 15%
where the time goes in v3:
time: 281 us; the launch traced here: 279 us
  waiting for transfers between devices  141 us (50%)
  starting transfers between devices  60.8 us (22%)
  Pallas kernels  43 us (15%)
  local copies, waits for them, and re-layouts  18.8 us (7%)
  between operations  13.5 us (5%)
    ppermute x10, waiting for transfers between devices, shift_x(): return lax.ppermute(value, 'x', [(i, (i + by) % 4) for i in range(4)])  73.9 us
    pallas_call x2, Pallas kernels, product(): pl.pallas_call(functools.partial(product_kernel, around, counts), grid_sp...  35.1 us
    ppermute x7, waiting for transfers between devices, shift_z(): return lax.ppermute(value, 'z', [(i, (i + by) % 8) for i in range(8)])  26.5 us
    ppermute x7, starting transfers between devices, shift_z(): return lax.ppermute(value, 'z', [(i, (i + by) % 8) for i in range(8)])  21.4 us
    ppermute x10, starting transfers between devices, shift_x(): return lax.ppermute(value, 'x', [(i, (i + by) % 4) for i in range(4)])  16.6 us
    ppermute x2, waiting for transfers between devices, swap_near(): return lax.ppermute(value, 'yl', [(0, 1), (1, 0)])  15.6 us
    all_to_all x1, waiting for transfers between devices, on_device(): here = lax.all_to_all(here, 'z', split_axis=0, concat_axis=0, tiled=True)  15 us
    unnamed x48, local copies, waits for them, and re-layouts  14.1 us
  transfers between devices with their start and end apart: 29, of which 17 were waited for; matrix products, arithmetic and copies ran while one was open for 2% of the time, Pallas kernels for 15%

profile of v3, /device:TPU:24, one launch (start us, length us, event | category | flops | bytes accessed | tf_op | source)
XLA Modules:
  0.0 278.6 jit_solution(6685683950217783626)
XLA Ops:
  7.4 1.6 collective-permute-start
  9.0 2.7 collective-permute-start.2
  18.6 8.5 %all-to-all-start = ((f32[8,16,1024]{2,1,0:T(8,128)}), f32[8,16,1024]{2,1,0:T(8,128)S(1)}, u32[]{:S(2)}, u32[]{:S(2)}) async-start(f32[8,16,1024]{2,1,0:T(8,128)} %broadcast_in_dim.2), calls=%async_computation | async-start | bytes 1048576 | tf_op jit(solution)/shard_map/all_to_all | solution.py:261
  27.9 15.0 %all-to-all-done.refs_0_ = f32[8,16,1024]{2,1,0:T(8,128)S(1)} async-done(((f32[8,16,1024]{2,1,0:T(8,128)}), f32[8,16,1024]{2,1,0:T(8,128)S(1)}, u32[]{:S(2)}, u32[]{:S(2)}) %all-to-all-start) | async-done | bytes 524320 | tf_op jit(solution)/shard_map/all_to_all | solution.py:261
  42.9 2.4 collective-permute-start.3
  45.2 9.5 %collective-permute-done.3.refs_1_ = f32[8,16,1024]{2,1,0:T(8,128)S(1)} collective-permute-done((f32[8,16,1024]{2,1,0:T(8,128)S(1)}, f32[8,16,1024]{2,1,0:T(8,128)S(1)}, u32[]{:S(2)}, u32[]{:S(2)}) %collective-permute-start.3) | collective-permute-done | bytes 524320 | tf_op jit(solution)/shard_map/ppermute | solution.py:23
  54.8 2.5 collective-permute-start.4
  57.3 3.9 %collective-permute-done.4.refs_2_ = f32[4,16,1024]{2,1,0:T(8,128)S(1)} collective-permute-done((f32[4,16,1024]{2,1,0:T(8,128)S(1)}, f32[4,16,1024]{2,1,0:T(8,128)S(1)}, u32[]{:S(2)}, u32[]{:S(2)}) %collective-permute-start.4) | collective-permute-done | bytes 262176 | tf_op jit(solution)/shard_map/ppermute | solution.py:23
  61.2 3.7 %collective-permute-done.6.refs_3_ = f32[4,16,1024]{2,1,0:T(8,128)S(1)} collective-permute-done((f32[4,16,1024]{2,1,0:T(8,128)S(1)}, f32[4,16,1024]{2,1,0:T(8,128)S(1)}, u32[]{:S(2)}, u32[]{:S(2)}) %collective-permute-start.6) | collective-permute-done | bytes 262176 | tf_op jit(solution)/shard_map/ppermute | solution.py:23
  64.9 14.1 %collective-permute-done.7.refs_6_ = f32[1400,512]{1,0:T(8,128)} collective-permute-done((f32[1400,512]{1,0:T(8,128)}, f32[1400,512]{1,0:T(8,128)}, u32[]{:S(2)}, u32[]{:S(2)}) %collective-permute-start.7) | collective-permute-done | bytes 2867232 | tf_op jit(solution)/shard_map/ppermute | solution.py:31
  79.0 1.7 collective-permute-done.8.refs_8_
  81.3 1.5 slice.25
  86.3 4.1 %collective-permute-done.10.refs_9_ = f32[1400,512]{1,0:T(8,128)} collective-permute-done((f32[1400,512]{1,0:T(8,128)}, f32[1400,512]{1,0:T(8,128)}, u32[]{:S(2)}, u32[]{:S(2)}) %collective-permute-start.10) | collective-permute-done | bytes 2867232 | tf_op jit(solution)/shard_map/ppermute | solution.py:19
  90.4 17.5 %shard_map.28 = (f32[64,1400]{1,0:T(8,128)}, f32[64,1400]{1,0:T(8,128)}, f32[64,1400]{1,0:T(8,128)}, f32[64,1400]{1,0:T(8,128)}, f32[64,1400]{1,0:T(8,128)}, /*i...) custom-call(s32[3]{0:T(128)} %pad_add_fusion.place_ref, f32[8,16,1024]{2,1,0:T(8,128)} %copy-done.17, ...), custom_call_target="tpu_custom_call" | custom-call | flops 8808038400 | bytes 18530304 | tf_op jit(solution)/shard_map/pallas_call | solution.py:127
  107.8 4.9 %collective-permute-start.11 = (f32[64,1400]{1,0:T(8,128)}, f32[64,1400]{1,0:T(8,128)S(1)}, u32[]{:S(2)}, u32[]{:S(2)}) collective-permute-start(f32[64,1400]{1,0:T(8,128)} %get-tuple-element.37), channel_id=1, source_target_pairs={{0,12},{4,16},{8,20},{12,24},{16,28},{20,0},{24,4},{28,8},{1,13},{... | collective-permute-start | bytes 1075208 | tf_op jit(solution)/shard_map/ppermute | solution.py:27
  112.7 2.2 collective-permute-start.12
  116.4 4.1 %collective-permute-done.14.refs_8_ = f32[768,512]{1,0:T(8,128)} collective-permute-done((f32[768,512]{1,0:T(8,128)S(1)}, f32[768,512]{1,0:T(8,128)}, u32[]{:S(2)}, u32[]{:S(2)}) %collective-permute-start.14) | collective-permute-done | bytes 1572896 | tf_op jit(solution)/shard_map/ppermute | solution.py:35
  120.5 16.3 %collective-permute-done.11 = f32[64,1400]{1,0:T(8,128)S(1)} collective-permute-done((f32[64,1400]{1,0:T(8,128)}, f32[64,1400]{1,0:T(8,128)S(1)}, u32[]{:S(2)}, u32[]{:S(2)}) %collective-permute-start.11) | collective-permute-done | bytes 358432 | tf_op jit(solution)/shard_map/ppermute | solution.py:27
  138.9 6.1 %collective-permute-start.18 = (f32[64,1400]{1,0:T(8,128)}, f32[64,1400]{1,0:T(8,128)S(1)}, u32[]{:S(2)}, u32[]{:S(2)}) collective-permute-start(f32[64,1400]{1,0:T(8,128)} %get-tuple-element.48), channel_id=1, source_target_pairs={{0,4},{4,8},{8,12},{12,16},{16,20},{20,24},{24,28},{28,0},{1,5},{5... | collective-permute-start | bytes 1075208 | tf_op jit(solution)/shard_map/ppermute | solution.py:27
  145.0 1.8 collective-permute-start.20
  146.8 3.7 %collective-permute-start.21 = (f32[64,1400]{1,0:T(8,128)}, f32[64,1400]{1,0:T(8,128)S(1)}, u32[]{:S(2)}, u32[]{:S(2)}) collective-permute-start(f32[64,1400]{1,0:T(8,128)} %get-tuple-element.51), channel_id=1, source_target_pairs={{0,24},{4,28},{8,0},{12,4},{16,8},{20,12},{24,16},{28,20},{1,25},{... | collective-permute-start | bytes 1075208 | tf_op jit(solution)/shard_map/ppermute | solution.py:27
  150.5 2.7 collective-permute-start.22
  153.2 17.6 %shard_map.29 = f32[512,1400]{1,0:T(8,128)} custom-call(s32[3]{0:T(128)} %pad_add_fusion.place_ref, f32[8,16,1024]{2,1,0:T(8,128)} %copy-done.17, f32[8,16,1024]{2,1,0:T(8,128)} %copy-done.18, f32[4,16,1024]{2,1,0:T(8,128)} %copy-done.22, f32[4,16,1024]{2,1,0:T(8,128)} %copy-done.23, f32[8,16,1024]{2,1,0:T(8,128)} %copy-done.19, ...), custom_call_target="tpu_custom_call" | custom-call | flops 8808038400 | bytes 18530304 | tf_op jit(solution)/shard_map/pallas_call | solution.py:127
  173.1 10.2 %collective-permute-done.21 = f32[64,1400]{1,0:T(8,128)S(1)} collective-permute-done((f32[64,1400]{1,0:T(8,128)}, f32[64,1400]{1,0:T(8,128)S(1)}, u32[]{:S(2)}, u32[]{:S(2)}) %collective-permute-start.21) | collective-permute-done | bytes 358432 | tf_op jit(solution)/shard_map/ppermute | solution.py:27
  184.7 10.2 %all-to-all-start.1 = ((f32[32,16,1400]{2,1,0:T(8,128)}), f32[32,16,1400]{2,1,0:T(8,128)S(1)}, u32[]{:S(2)}, u32[]{:S(2)}) async-start(f32[32,16,1400]{2,1,0:T(8,128)} %bitcast.24), calls=%async_computation.1 | async-start | bytes 5767168 | tf_op jit(solution)/shard_map/all_to_all | solution.py:280
  201.9 1.5 shard_map.30
  204.3 1.8 collective-permute-start.23
  206.1 2.7 collective-permute-start.24
  210.3 28.4 %collective-permute-done.23.refs_1_ = f32[8,16,1400]{2,1,0:T(8,128)} collective-permute-done((f32[8,16,1400]{2,1,0:T(8,128)}, f32[8,16,1400]{2,1,0:T(8,128)}, u32[]{:S(2)}, u32[]{:S(2)}) %collective-permute-start.23) | collective-permute-done | bytes 716832 | tf_op jit(solution)/shard_map/ppermute | solution.py:23
  238.7 25.6 %collective-permute-done.24.refs_2_ = f32[8,16,1400]{2,1,0:T(8,128)} collective-permute-done((f32[8,16,1400]{2,1,0:T(8,128)}, f32[8,16,1400]{2,1,0:T(8,128)}, u32[]{:S(2)}, u32[]{:S(2)}) %collective-permute-start.24) | collective-permute-done | bytes 716832 | tf_op jit(solution)/shard_map/ppermute | solution.py:23
  265.4 4.4 %shard_map.31._ = f32[16,89600]{1,0:T(8,128)} custom-call(s32[2]{0:T(128)S(1)} %pad_add_fusion.1.at_ref, f32[8,16,1400]{2,1,0:T(8,128)S(1)} %copy-done.1, f32[8,16,1400]{2,1,0:T(8,128)} %collective-permute-done.23.refs_1_, f32[8,16,1400]{2,1,0:T(8,128)} %collective-permute-done.24.refs_2_, f32[8,16,1400]{2,1,0:T(8,128)} %collective-permute-done.25.refs_3_), custom_call_target="tpu_custom_call" | custom-call | bytes 5734400 | tf_op jit(solution)/shard_map/pallas_call | solution.py:230
  269.8 2.0 shard_map.32
  (89 shorter events, 30.3 us)
Async XLA Ops:
  7.4 6.1 %collective-permute-start = (f32[16,1024]{1,0:T(8,128)S(1)}, f32[16,1024]{1,0:T(8,128)S(1)}, u32[]{:S(2)}, u32[]{:S(2)}) collective-permute-start(f32[16,1024]{1,0:T(8,128)S(1)} %get-tuple-element.59), channel_id=1, source_target_pairs={{0,32},{32,64},{64,96},{96,0},{1,33},{33,65},{65,97},{97,1},{2,34}... | collective-permute-start | bytes 196616 | tf_op jit(solution)/shard_map/ppermute | solution.py:23
  9.0 5.9 %collective-permute-start.2 = (f32[16,1024]{1,0:T(8,128)S(1)}, f32[16,1024]{1,0:T(8,128)S(1)}, u32[]{:S(2)}, u32[]{:S(2)}) collective-permute-start(f32[16,1024]{1,0:T(8,128)S(1)} %get-tuple-element.59), channel_id=1, source_target_pairs={{0,64},{32,96},{64,0},{96,32},{1,65},{33,97},{65,1},{97,33},{2,66}... | collective-permute-start | bytes 196616 | tf_op jit(solution)/shard_map/ppermute | solution.py:23
  11.7 4.3 %collective-permute-start.1 = (f32[16,1024]{1,0:T(8,128)S(1)}, f32[16,1024]{1,0:T(8,128)S(1)}, u32[]{:S(2)}, u32[]{:S(2)}) collective-permute-start(f32[16,1024]{1,0:T(8,128)S(1)} %get-tuple-element.59), channel_id=1, source_target_pairs={{0,96},{32,0},{64,32},{96,64},{1,97},{33,1},{65,33},{97,65},{2,98}... | collective-permute-start | bytes 196616 | tf_op jit(solution)/shard_map/ppermute | solution.py:23
  16.0 63.0 %collective-permute-start.7 = (f32[1400,512]{1,0:T(8,128)}, f32[1400,512]{1,0:T(8,128)}, u32[]{:S(2)}, u32[]{:S(2)}) collective-permute-start(f32[1400,512]{1,0:T(8,128)} %bitcast.25), channel_id=1, source_target_pairs={{0,128},{128,0},{1,129},{129,1},{2,130},{130,2},{3,131},{131,3},{4... | collective-permute-start | bytes 8601608 | tf_op jit(solution)/shard_map/ppermute | solution.py:31
  16.7 63.9 %collective-permute-start.8 = (f32[1400,512]{1,0:T(8,128)}, f32[1400,512]{1,0:T(8,128)}, u32[]{:S(2)}, u32[]{:S(2)}) collective-permute-start(f32[1400,512]{1,0:T(8,128)} %bitcast.26), channel_id=1, source_target_pairs={{128,2},{2,128},{130,0},{0,130},{129,3},{3,129},{131,1},{1,131},{1... | collective-permute-start | bytes 8601608 | tf_op jit(solution)/shard_map/ppermute | solution.py:35
  18.6 24.2 %all-to-all-start = ((f32[8,16,1024]{2,1,0:T(8,128)}), f32[8,16,1024]{2,1,0:T(8,128)S(1)}, u32[]{:S(2)}, u32[]{:S(2)}) async-start(f32[8,16,1024]{2,1,0:T(8,128)} %broadcast_in_dim.2), calls=%async_computation | async-start | bytes 1048576 | tf_op jit(solution)/shard_map/all_to_all | solution.py:261
  27.1 59.0 %all-gather.3.cloned.1.call-start = ((), (), s32[]{:S(2)}) async-start(), calls=%async_computation.2 | async-start | bytes 2359296 | tf_op jit(solution)/shard_map/all_gather | solution.py:263
  42.9 42.5 %copy-start.17 = (f32[8,16,1024]{2,1,0:T(8,128)}, f32[8,16,1024]{2,1,0:T(8,128)S(1)}, u32[]{:S(2)}) copy-start(f32[8,16,1024]{2,1,0:T(8,128)S(1)} %all-to-all-done.refs_0_) | copy-start | bytes 1572868
  42.9 11.9 %collective-permute-start.3 = (f32[8,16,1024]{2,1,0:T(8,128)S(1)}, f32[8,16,1024]{2,1,0:T(8,128)S(1)}, u32[]{:S(2)}, u32[]{:S(2)}) collective-permute-start(f32[8,16,1024]{2,1,0:T(8,128)S(1)} %all-to-all-done.refs_0_), channel_id=1, source_target_pairs={{0,96},{32,0},{64,32},{96,64},{1,97},{33,1},{65,33},{97,65},{2,98}... | collective-permute-start | bytes 1572872 | tf_op jit(solution)/shard_map/ppermute | solution.py:23
  45.2 12.0 %collective-permute-start.5 = (f32[8,16,1024]{2,1,0:T(8,128)S(1)}, f32[8,16,1024]{2,1,0:T(8,128)S(1)}, u32[]{:S(2)}, u32[]{:S(2)}) collective-permute-start(f32[8,16,1024]{2,1,0:T(8,128)S(1)} %all-to-all-done.refs_0_), channel_id=1, source_target_pairs={{0,32},{32,64},{64,96},{96,0},{1,33},{33,65},{65,97},{97,1},{2,34}... | collective-permute-start | bytes 1572872 | tf_op jit(solution)/shard_map/ppermute | solution.py:23
  54.8 6.4 %collective-permute-start.4 = (f32[4,16,1024]{2,1,0:T(8,128)S(1)}, f32[4,16,1024]{2,1,0:T(8,128)S(1)}, u32[]{:S(2)}, u32[]{:S(2)}) collective-permute-start(f32[4,16,1024]{2,1,0:T(8,128)S(1)} %slice.27), channel_id=1, source_target_pairs={{0,96},{32,0},{64,32},{96,64},{1,97},{33,1},{65,33},{97,65},{2,98}... | collective-permute-start | bytes 786440 | tf_op jit(solution)/shard_map/ppermute | solution.py:23
  57.2 23.5 %copy-start.19 = (f32[8,16,1024]{2,1,0:T(8,128)}, f32[8,16,1024]{2,1,0:T(8,128)S(1)}, u32[]{:S(2)}) copy-start(f32[8,16,1024]{2,1,0:T(8,128)S(1)} %collective-permute-done.5.refs_4_) | copy-start | bytes 1572868
  57.3 7.7 %collective-permute-start.6 = (f32[4,16,1024]{2,1,0:T(8,128)S(1)}, f32[4,16,1024]{2,1,0:T(8,128)S(1)}, u32[]{:S(2)}, u32[]{:S(2)}) collective-permute-start(f32[4,16,1024]{2,1,0:T(8,128)S(1)} %slice.28), channel_id=1, source_target_pairs={{0,32},{32,64},{64,96},{96,0},{1,33},{33,65},{65,97},{97,1},{2,34}... | collective-permute-start | bytes 786440 | tf_op jit(solution)/shard_map/ppermute | solution.py:23
  61.2 19.5 %copy-start.22 = (f32[4,16,1024]{2,1,0:T(8,128)}, f32[4,16,1024]{2,1,0:T(8,128)S(1)}, u32[]{:S(2)}) copy-start(f32[4,16,1024]{2,1,0:T(8,128)S(1)} %collective-permute-done.4.refs_2_) | copy-start | bytes 786436
  80.7 5.6 %collective-permute-start.9 = (f32[1400,512]{1,0:T(8,128)}, f32[1400,512]{1,0:T(8,128)}, u32[]{:S(2)}, u32[]{:S(2)}) collective-permute-start(f32[1400,512]{1,0:T(8,128)} %collective-permute-done.7.refs_6_), channel_id=1, source_target_pairs={{0,1},{1,0},{2,3},{3,2},{4,5},{5,4},{6,7},{7,6},{8,9},{9,8},{10,11... | collective-permute-start | bytes 8601608 | tf_op jit(solution)/shard_map/ppermute | solution.py:19
  80.7 9.7 %collective-permute-start.10 = (f32[1400,512]{1,0:T(8,128)}, f32[1400,512]{1,0:T(8,128)}, u32[]{:S(2)}, u32[]{:S(2)}) collective-permute-start(f32[1400,512]{1,0:T(8,128)} %collective-permute-done.8.refs_8_), channel_id=1, source_target_pairs={{0,1},{1,0},{2,3},{3,2},{4,5},{5,4},{6,7},{7,6},{8,9},{9,8},{10,11... | collective-permute-start | bytes 8601608 | tf_op jit(solution)/shard_map/ppermute | solution.py:19
  82.8 37.7 %collective-permute-start.14 = (f32[768,512]{1,0:T(8,128)S(1)}, f32[768,512]{1,0:T(8,128)}, u32[]{:S(2)}, u32[]{:S(2)}) collective-permute-start(f32[768,512]{1,0:T(8,128)S(1)} %slice.25), channel_id=1, source_target_pairs={{128,2},{2,128},{130,0},{0,130},{129,3},{3,129},{131,1},{1,131},{1... | collective-permute-start | bytes 4718600 | tf_op jit(solution)/shard_map/ppermute | solution.py:35
  83.9 61.1 %collective-permute-start.13 = (f32[1400,512]{1,0:T(8,128)}, f32[1400,512]{1,0:T(8,128)}, u32[]{:S(2)}, u32[]{:S(2)}) collective-permute-start(f32[1400,512]{1,0:T(8,128)} %bitcast.27), channel_id=1, source_target_pairs={{0,1},{1,0},{2,3},{3,2},{4,5},{5,4},{6,7},{7,6},{8,9},{9,8},{10,11... | collective-permute-start | bytes 8601608 | tf_op jit(solution)/shard_map/ppermute | solution.py:19
  85.4 31.0 %collective-permute-start.15 = (f32[632,512]{1,0:T(8,128)S(1)}, f32[632,512]{1,0:T(8,128)}, u32[]{:S(2)}, u32[]{:S(2)}) collective-permute-start(f32[632,512]{1,0:T(8,128)S(1)} %slice.26), channel_id=1, source_target_pairs={{0,128},{128,0},{1,129},{129,1},{2,130},{130,2},{3,131},{131,3},{4... | collective-permute-start | bytes 3883016 | tf_op jit(solution)/shard_map/ppermute | solution.py:31
  107.8 29.0 %collective-permute-start.11 = (f32[64,1400]{1,0:T(8,128)}, f32[64,1400]{1,0:T(8,128)S(1)}, u32[]{:S(2)}, u32[]{:S(2)}) collective-permute-start(f32[64,1400]{1,0:T(8,128)} %get-tuple-element.37), channel_id=1, source_target_pairs={{0,12},{4,16},{8,20},{12,24},{16,28},{20,0},{24,4},{28,8},{1,13},{... | collective-permute-start | bytes 1075208 | tf_op jit(solution)/shard_map/ppermute | solution.py:27
  112.7 24.9 %collective-permute-start.12 = (f32[64,1400]{1,0:T(8,128)}, f32[64,1400]{1,0:T(8,128)S(1)}, u32[]{:S(2)}, u32[]{:S(2)}) collective-permute-start(f32[64,1400]{1,0:T(8,128)} %get-tuple-element.38), channel_id=1, source_target_pairs={{0,20},{4,24},{8,28},{12,0},{16,4},{20,8},{24,12},{28,16},{1,21},{... | collective-permute-start | bytes 1075208 | tf_op jit(solution)/shard_map/ppermute | solution.py:27
  138.4 12.2 %collective-permute-start.16 = (f32[768,512]{1,0:T(8,128)}, f32[768,512]{1,0:T(8,128)S(1)}, u32[]{:S(2)}, u32[]{:S(2)}) collective-permute-start(f32[768,512]{1,0:T(8,128)} %collective-permute-done.14.refs_8_), channel_id=1, source_target_pairs={{0,1},{1,0},{2,3},{3,2},{4,5},{5,4},{6,7},{7,6},{8,9},{9,8},{10,11... | collective-permute-start | bytes 4718600 | tf_op jit(solution)/shard_map/ppermute | solution.py:19
  138.4 8.5 %collective-permute-start.17 = (f32[632,512]{1,0:T(8,128)}, f32[632,512]{1,0:T(8,128)S(1)}, u32[]{:S(2)}, u32[]{:S(2)}) collective-permute-start(f32[632,512]{1,0:T(8,128)} %collective-permute-done.15.refs_9_), channel_id=1, source_target_pairs={{0,1},{1,0},{2,3},{3,2},{4,5},{5,4},{6,7},{7,6},{8,9},{9,8},{10,11... | collective-permute-start | bytes 3883016 | tf_op jit(solution)/shard_map/ppermute | solution.py:19
  138.9 32.0 %collective-permute-start.18 = (f32[64,1400]{1,0:T(8,128)}, f32[64,1400]{1,0:T(8,128)S(1)}, u32[]{:S(2)}, u32[]{:S(2)}) collective-permute-start(f32[64,1400]{1,0:T(8,128)} %get-tuple-element.48), channel_id=1, source_target_pairs={{0,4},{4,8},{8,12},{12,16},{16,20},{20,24},{24,28},{28,0},{1,5},{5... | collective-permute-start | bytes 1075208 | tf_op jit(solution)/shard_map/ppermute | solution.py:27
  145.0 26.6 %collective-permute-start.19 = (f32[64,1400]{1,0:T(8,128)}, f32[64,1400]{1,0:T(8,128)S(1)}, u32[]{:S(2)}, u32[]{:S(2)}) collective-permute-start(f32[64,1400]{1,0:T(8,128)} %get-tuple-element.49), channel_id=1, source_target_pairs={{0,28},{4,0},{8,4},{12,8},{16,12},{20,16},{24,20},{28,24},{1,29},{... | collective-permute-start | bytes 1075208 | tf_op jit(solution)/shard_map/ppermute | solution.py:27
  145.0 27.3 %collective-permute-start.20 = (f32[64,1400]{1,0:T(8,128)}, f32[64,1400]{1,0:T(8,128)S(1)}, u32[]{:S(2)}, u32[]{:S(2)}) collective-permute-start(f32[64,1400]{1,0:T(8,128)} %get-tuple-element.50), channel_id=1, source_target_pairs={{0,8},{4,12},{8,16},{12,20},{16,24},{20,28},{24,0},{28,4},{1,9},{5... | collective-permute-start | bytes 1075208 | tf_op jit(solution)/shard_map/ppermute | solution.py:27
  146.8 36.4 %collective-permute-start.21 = (f32[64,1400]{1,0:T(8,128)}, f32[64,1400]{1,0:T(8,128)S(1)}, u32[]{:S(2)}, u32[]{:S(2)}) collective-permute-start(f32[64,1400]{1,0:T(8,128)} %get-tuple-element.51), channel_id=1, source_target_pairs={{0,24},{4,28},{8,0},{12,4},{16,8},{20,12},{24,16},{28,20},{1,25},{... | collective-permute-start | bytes 1075208 | tf_op jit(solution)/shard_map/ppermute | solution.py:27
  150.5 33.5 %collective-permute-start.22 = (f32[64,1400]{1,0:T(8,128)}, f32[64,1400]{1,0:T(8,128)S(1)}, u32[]{:S(2)}, u32[]{:S(2)}) collective-permute-start(f32[64,1400]{1,0:T(8,128)} %get-tuple-element.52), channel_id=1, source_target_pairs={{0,16},{4,20},{8,24},{12,28},{16,0},{20,4},{24,8},{28,12},{1,17},{... | collective-permute-start | bytes 1075208 | tf_op jit(solution)/shard_map/ppermute | solution.py:27
  184.7 85.1 %all-to-all-start.1 = ((f32[32,16,1400]{2,1,0:T(8,128)}), f32[32,16,1400]{2,1,0:T(8,128)S(1)}, u32[]{:S(2)}, u32[]{:S(2)}) async-start(f32[32,16,1400]{2,1,0:T(8,128)} %bitcast.24), calls=%async_computation.1 | async-start | bytes 5767168 | tf_op jit(solution)/shard_map/all_to_all | solution.py:280
  204.3 34.4 %collective-permute-start.23 = (f32[8,16,1400]{2,1,0:T(8,128)}, f32[8,16,1400]{2,1,0:T(8,128)}, u32[]{:S(2)}, u32[]{:S(2)}) collective-permute-start(f32[8,16,1400]{2,1,0:T(8,128)} %get-tuple-element.56), channel_id=1, source_target_pairs={{0,32},{32,64},{64,96},{96,0},{1,33},{33,65},{65,97},{97,1},{2,34}... | collective-permute-start | bytes 2150408 | tf_op jit(solution)/shard_map/ppermute | solution.py:23
  206.1 58.2 %collective-permute-start.24 = (f32[8,16,1400]{2,1,0:T(8,128)}, f32[8,16,1400]{2,1,0:T(8,128)}, u32[]{:S(2)}, u32[]{:S(2)}) collective-permute-start(f32[8,16,1400]{2,1,0:T(8,128)} %get-tuple-element.57), channel_id=1, source_target_pairs={{0,64},{32,96},{64,0},{96,32},{1,65},{33,97},{65,1},{97,33},{2,66}... | collective-permute-start | bytes 2150408 | tf_op jit(solution)/shard_map/ppermute | solution.py:23
  208.8 55.5 %collective-permute-start.25 = (f32[8,16,1400]{2,1,0:T(8,128)}, f32[8,16,1400]{2,1,0:T(8,128)}, u32[]{:S(2)}, u32[]{:S(2)}) collective-permute-start(f32[8,16,1400]{2,1,0:T(8,128)} %get-tuple-element.58), channel_id=1, source_target_pairs={{0,96},{32,0},{64,32},{96,64},{1,97},{33,1},{65,33},{97,65},{2,98}... | collective-permute-start | bytes 2150408 | tf_op jit(solution)/shard_map/ppermute | solution.py:23
  (21 other events, 49.0 us)
Sparse Core Ops, SparseCore 0:
  29.7 42.1 all-gather.2

commit v4 on v2

--- a/solution.py
+++ b/solution.py
@@ -10,7 +10,7 @@
 
 AXES = ("yl", "x", "z", "yh", "core")
 TILE = 256
-CUT = 768
+CUT = 1024
 GROUP = 16
 
 
@@ -36,36 +36,42 @@
     return top, rest
 
 
-def load_amplitudes(place_ref, pieces, last_ref, top_ref, rest_ref):
-    own, x = place_ref[0], place_ref[1]
-    part = last_ref.shape[3]
-
-    @pl.loop(0, 4)
-    def _(q):
+def load_amplitudes(place_ref, around, first_refs, last_ref, top_ref, rest_ref):
+    here_ref, ahead_ref, low_ref, high_ref, behind_ref = first_refs
+    own, x, z = place_ref[0], place_ref[1], place_ref[2]
+    heights, _, rows, half = last_ref.shape
+    part = half // 2
+
+    @pl.loop(0, 4 * heights)
+    def _(i):
+        q, there = i // heights, lax.rem(i, heights)
         source = own ^ q
-        take = pl.ds(pl.multiple_of(jnp.minimum(source, 2) * part, part), part)
+        take = pl.ds(pl.multiple_of((source & 1) * part, part), part)
         into = pl.ds(pl.multiple_of(q * part, part), part)
-        for d, refs in enumerate(pieces):
-            last = last_ref[:, d].reshape(-1, part)
-            row = lax.rem(x + d, 4) * last.shape[0]
-            at = 0
-            for ref in refs:
-                count = ref.shape[0]
-                value = jnp.where(source < 3, ref[:, take], last[at : at + count])
-                rows = pl.ds(pl.multiple_of(row + at, count), count)
-                top_ref[rows, into], rest_ref[rows, into] = halves(value)
-                at += count
-
-
-def product_kernel(counts, place_ref, *refs):
-    pieces, (out_ref, top_ref, rest_ref) = refs[6:-3], refs[-3:]
+        below = there < heights // 2
+        opposite = jnp.where(
+            below,
+            low_ref[jnp.minimum(there, heights // 2 - 1), :, take],
+            high_ref[jnp.maximum(there - heights // 2, 0), :, take],
+        )
+        first = [here_ref[there, :, take], ahead_ref[there, :, take], opposite, behind_ref[there, :, take]]
+        for d in range(4):
+            value = jnp.where(source < 2, first[d], last_ref[there, d, :, take])
+            if around:
+                row = lax.rem(there - z + heights, heights) * (4 * rows) + d * rows
+            else:
+                row = lax.rem(x + d, 4) * (heights * rows) + there * rows
+            into_rows = pl.ds(pl.multiple_of(row, rows), rows)
+            top_ref[into_rows, into], rest_ref[into_rows, into] = halves(value)
+
+
+def product_kernel(around, counts, place_ref, *refs):
+    pieces = refs[6 : 6 + sum(len(tiles) for tiles in counts)]
+    outs, (top_ref, rest_ref) = refs[6 + len(pieces) : -2], refs[-2:]
 
     @pl.when(pl.program_id(0) == 0)
     def _():
-        here, ahead, behind, low, high, last_ref = refs[:6]
-        load_amplitudes(
-            place_ref, [[here], [ahead], [low, high], [behind]], last_ref, top_ref, rest_ref
-        )
+        load_amplitudes(place_ref, around, refs[:5], refs[5], top_ref, rest_ref)
 
     dot = functools.partial(
         lax.dot_general,
@@ -84,13 +90,16 @@
         t_top, t_rest = top_ref[:, depth], rest_ref[:, depth]
         term = dot(t_top, rest) + dot(t_rest, top) + dot(t_top, top)
         total = term if total is None else total + term
-    out_ref[...] = 0.5 * total
-
-
-def product(place, amplitudes, quarters):
+    count = total.shape[0] // len(outs)
+    for i, out_ref in enumerate(outs):
+        out_ref[...] = 0.5 * total[i * count : (i + 1) * count]
+
+
+def product(place, amplitudes, quarters, around=False):
     last = amplitudes[-1]
-    rows, part = math.prod(last.shape[:3]), last.shape[3]
-    depth = 4 * part
+    rows, depth = math.prod(last.shape[:3]), 2 * last.shape[3]
+    part = depth // 4
+    outs = last.shape[0] if around else 1
     columns = sum(piece.shape[0] for piece in quarters[0])
     specs, counts = [], []
     for quarter in quarters:
@@ -111,15 +120,15 @@
         for v in amplitudes
     ]
     return pl.pallas_call(
-        functools.partial(product_kernel, counts),
+        functools.partial(product_kernel, around, counts),
         grid_spec=pltpu.PrefetchScalarGridSpec(
             num_scalar_prefetch=1,
             grid=(pl.cdiv(columns, TILE),),
             in_specs=whole + specs,
-            out_specs=pl.BlockSpec((rows, TILE), lambda n, place: (0, n)),
+            out_specs=[pl.BlockSpec((rows // outs, TILE), lambda n, place: (0, n))] * outs,
             scratch_shapes=[pltpu.VMEM((rows, depth), jnp.bfloat16)] * 2,
         ),
-        out_shape=jax.ShapeDtypeStruct((rows, columns), jnp.float32),
+        out_shape=[jax.ShapeDtypeStruct((rows // outs, columns), jnp.float32)] * outs,
         compiler_params=pltpu.CompilerParams(vmem_limit_bytes=60 << 20),
         cost_estimate=pl.CostEstimate(
             flops=6 * rows * depth * columns,
@@ -165,42 +174,50 @@
     )(at, *blocks, *([] if out is None else [out]))
 
 
-def gather_amplitudes(amplitudes):
+def after(value, *others):
+    return lax.optimization_barrier((value, *others))[0]
+
+
+def on_device(amplitudes, integrals):
+    x, z, yl, yh, core = (lax.axis_index(name) for name in ("x", "z", "yl", "yh", "core"))
     rows, depth = amplitudes.shape
-    part = depth // 4
-    last = amplitudes[:, 3 * part :]
-    last = jnp.concatenate([last] + [shift_x(last, -d) for d in (1, 2, 3)])
-    last = lax.all_gather(last, "z", axis=0).reshape(8, 4, rows, part)
-    here = jnp.broadcast_to(amplitudes[None, :, : 3 * part], (8, rows, 3 * part))
-    here = lax.all_to_all(here, "z", split_axis=0, concat_axis=0, tiled=True).reshape(-1, 3 * part)
+    columns = integrals.shape[1]
+    half = depth // 2
+    spot = jnp.stack([2 * yh + core, x, z])
+
+    turns = [shift_x(amplitudes[:, half:], -d) for d in (1, 2, 3)]
+    last = jnp.concatenate([amplitudes[:, half:]] + turns)
+    here = jnp.broadcast_to(after(amplitudes[:, :half], last)[None], (8, rows, half))
+    here = lax.all_to_all(here, "z", split_axis=0, concat_axis=0, tiled=True)
+    last = lax.all_gather(last, "z", axis=0).reshape(8, 4, rows, half)
     ahead, behind = shift_x(here, -1), shift_x(here, 1)
-    half = here.shape[0] // 2
-    low, high = shift_x(ahead[:half], -1), shift_x(behind[half:], 1)
-    return [here, ahead, behind, low, high, last]
-
-
-def on_device(amplitudes, integrals):
-    x, yl, yh, core = (lax.axis_index(name) for name in ("x", "yl", "yh", "core"))
-    rows = amplitudes.shape[0]
-    columns = integrals.shape[1]
-    spot = jnp.stack([2 * yh + core, x])
-    t = gather_amplitudes(amplitudes)
-
-    own = [integrals.T[:CUT], integrals.T[CUT:]]
-    near, far = [swap_near(v) for v in own], [swap_far(v) for v in own]
-    across = [swap_far(near[0]), swap_near(far[1])]
+    low, high = shift_x(ahead[:4], -1), shift_x(behind[4:], 1)
+    t = (here, ahead, low, high, behind, last)
+
+    first, second = after(integrals.T[:CUT], *turns), after(integrals.T[CUT:], ahead, behind)
+    near, far = after((swap_near(first), swap_far(first)), low, high)
+    near_next, far_next = swap_near(second), swap_far(second)
 
     def exchange(v):
         return lax.all_to_all(
             v.reshape(-1, rows, v.shape[1]), ("x", "z"), split_axis=0, concat_axis=0, tiled=True
         )
 
-    other_block = [
-        exchange(product(spot, t, [[n], [swap_core(n)], [f], [swap_core(f)]]))
-        for n, f in zip(near, far)
-    ]
-    own2, across2 = [swap_core(v) for v in own], [swap_core(v) for v in across]
-    own_block = exchange(product(spot, t, [own, own2, across, across2]))
+    (result,) = product(spot, t, [[near], [swap_core(near)], [far], [swap_core(far)]])
+    t = after(t, result)
+    near_next, far_next = after((near_next, far_next), result)
+    across = [swap_far(after(near, low, high)), swap_near(far_next)]
+    own = [first, second]
+    own2 = [swap_core(v) for v in after((first, second), result)]
+    (result_next,) = product(
+        spot, t, [[near_next], [swap_core(near_next)], [far_next], [swap_core(far_next)]]
+    )
+    t = after(t, result_next)
+    other_block = [exchange(result)]
+    other_block.append(exchange(after(result_next, other_block[0])))
+    across2 = [swap_core(v) for v in after(across, result_next)]
+    (own_block,) = product(spot, t, [own, own2, across, across2])
+    own_block = exchange(after(own_block, other_block[1]))
     out = place((1 - yl).reshape(1), other_block)
     return place(yl.reshape(1), [own_block], out)
 

time: 258 us -> 299 us (1.16)
  waiting for transfers between devices: 141 us -> 178 us
  starting transfers between devices: 40.6 us -> 50.1 us
  local copies, waits for them, and re-layouts: 17.7 us -> 10.1 us
    ppermute x3, waiting for transfers between devices: 6.91 us -> 43.3 us  [swap_far(): return lax.ppermute(value, ('yl', 'yh'), [(2, 1), (1, 2), (3, 0), (0, 3)])]
    ppermute x3, waiting for transfers between devices: 9.2 us -> 22.7 us  [swap_near(): return lax.ppermute(value, 'yl', [(0, 1), (1, 0)])]
    all_to_all x3, waiting for transfers between devices: 82.1 us -> 68.9 us  [exchange(): lax.all_to_all(v.reshape(-1, rows, v.shape[1]), ('x', 'z'), split_axis=0,...]
    all_to_all x3, starting transfers between devices: 14.6 us -> 24.1 us  [exchange(): lax.all_to_all(v.reshape(-1, rows, v.shape[1]), ('x', 'z'), split_axis=0,...]
    ppermute x7, waiting for transfers between devices: 26.4 us -> 18.1 us  [shift_x(): return lax.ppermute(value, 'x', [(i, (i + by) % 4) for i in range(4)])]
    unnamed x28 -> x26, local copies, waits for them, and re-layouts: 11.1 us -> 4.52 us
    all_to_all x1, waiting for transfers between devices: 9.16 us -> 15 us  [on_device(): here = lax.all_to_all(here, 'z', split_axis=0, concat_axis=0, tiled=True)]
    all_gather x1, waiting for transfers between devices: 0.01 us -> 5.83 us  [on_device(): last = lax.all_gather(last, 'z', axis=0).reshape(8, 4, rows, half)]
  transfers between devices with their start and end apart: 26 -> 26, of which waited for: 18 -> 14; matrix products, arithmetic and copies ran while one was open for 2% -> 2% of each run, Pallas kernels for 16% -> 10%
where the time goes in v4:
time: 299 us; the launch traced here: 298 us
  waiting for transfers between devices  178 us (60%)
  starting transfers between devices  50.1 us (17%)
  Pallas kernels  44.8 us (15%)
  between operations  13.6 us (5%)
  local copies, waits for them, and re-layouts  10.1 us (3%)
    all_to_all x3, waiting for transfers between devices, exchange(): lax.all_to_all(v.reshape(-1, rows, v.shape[1]), ('x', 'z'), split_axis=0,...  68.9 us
    ppermute x3, waiting for transfers between devices, swap_far(): return lax.ppermute(value, ('yl', 'yh'), [(2, 1), (1, 2), (3, 0), (0, 3)])  43.3 us
    pallas_call x3, Pallas kernels, product(): pl.pallas_call(functools.partial(product_kernel, around, counts), grid_sp...  40.8 us
    all_to_all x3, starting transfers between devices, exchange(): lax.all_to_all(v.reshape(-1, rows, v.shape[1]), ('x', 'z'), split_axis=0,...  24.1 us
    ppermute x3, waiting for transfers between devices, swap_near(): return lax.ppermute(value, 'yl', [(0, 1), (1, 0)])  22.7 us
    ppermute x7, waiting for transfers between devices, shift_x(): return lax.ppermute(value, 'x', [(i, (i + by) % 4) for i in range(4)])  18.1 us
    all_to_all x1, waiting for transfers between devices, on_device(): here = lax.all_to_all(here, 'z', split_axis=0, concat_axis=0, tiled=True)  15 us
    ppermute x7, starting transfers between devices, shift_x(): return lax.ppermute(value, 'x', [(i, (i + by) % 4) for i in range(4)])  10.6 us
  transfers between devices with their start and end apart: 26, of which 14 were waited for; matrix products, arithmetic and copies ran while one was open for 2% of the time, Pallas kernels for 10%

profile of v4, /device:TPU:24, one launch (start us, length us, event | category | flops | bytes accessed | tf_op | source)
XLA Modules:
  0.0 298.0 jit_solution(14647529975179941356)
XLA Ops:
  7.4 1.6 collective-permute-start.2
  9.0 2.7 collective-permute-start.1
  11.7 1.4 collective-permute-start
  13.2 1.8 slice.29.refs_6_
  19.4 8.5 %all-to-all-start = ((f32[8,16,1024]{2,1,0:T(8,128)}), f32[8,16,1024]{2,1,0:T(8,128)S(1)}, u32[]{:S(2)}, u32[]{:S(2)}) async-start(f32[8,16,1024]{2,1,0:T(8,128)} %broadcast_in_dim.2), calls=%async_computation | async-start | bytes 1048576 | tf_op jit(solution)/shard_map/all_to_all | solution.py:191
  28.6 15.0 %all-to-all-done.refs_0_ = f32[8,16,1024]{2,1,0:T(8,128)S(1)} async-done(((f32[8,16,1024]{2,1,0:T(8,128)}), f32[8,16,1024]{2,1,0:T(8,128)S(1)}, u32[]{:S(2)}, u32[]{:S(2)}) %all-to-all-start) | async-done | bytes 524320 | tf_op jit(solution)/shard_map/all_to_all | solution.py:191
  43.6 2.4 collective-permute-start.3
  46.0 9.5 %collective-permute-done.3.refs_1_ = f32[8,16,1024]{2,1,0:T(8,128)S(1)} collective-permute-done((f32[8,16,1024]{2,1,0:T(8,128)S(1)}, f32[8,16,1024]{2,1,0:T(8,128)S(1)}, u32[]{:S(2)}, u32[]{:S(2)}) %collective-permute-start.3) | collective-permute-done | bytes 524320 | tf_op jit(solution)/shard_map/ppermute | solution.py:22
  55.5 2.5 collective-permute-start.4
  58.1 3.9 %collective-permute-done.4.refs_2_ = f32[4,16,1024]{2,1,0:T(8,128)S(1)} collective-permute-done((f32[4,16,1024]{2,1,0:T(8,128)S(1)}, f32[4,16,1024]{2,1,0:T(8,128)S(1)}, u32[]{:S(2)}, u32[]{:S(2)}) %collective-permute-start.4) | collective-permute-done | bytes 262176 | tf_op jit(solution)/shard_map/ppermute | solution.py:22
  61.9 3.7 %collective-permute-done.6.refs_3_ = f32[4,16,1024]{2,1,0:T(8,128)S(1)} collective-permute-done((f32[4,16,1024]{2,1,0:T(8,128)S(1)}, f32[4,16,1024]{2,1,0:T(8,128)S(1)}, u32[]{:S(2)}, u32[]{:S(2)}) %collective-permute-start.6) | collective-permute-done | bytes 262176 | tf_op jit(solution)/shard_map/ppermute | solution.py:22
  66.8 5.8 %all-gather.3.cloned.1.call-done = f32[512,1024]{1,0:T(8,128)} async-done(((f32[64,1024]{1,0:T(8,128)}), f32[512,1024]{1,0:T(8,128)}) %all-gather.3.cloned.1.call-update) | async-done | bytes 2097168 | tf_op jit(solution)/shard_map/all_gather | solution.py:192
  73.3 13.4 %shard_map.28 = f32[512,1024]{1,0:T(8,128)} custom-call(s32[3]{0:T(128)} %pad_add_fusion.place_ref, f32[8,16,1024]{2,1,0:T(8,128)} %copy-done.5, f32[8,16,1024]{2,1,0:T(8,128)} %copy-done.6, f32[4,16,1024]{2,1,0:T(8,128)} %copy-done.11, f32[4,16,1024]{2,1,0:T(8,128)} %copy-done.12, f32[8,16,1024]{2,1,0:T(8,128)} %copy-done.7, f32[8,4,16,1024]{3,2,1,0:T(8,128)} %bitcast.15, ...), custom_call_target="tpu_custom_call" | custom-call | flops 6442450944 | bytes 14680064 | tf_op jit(solution)/shard_map/pallas_call | solution.py:122
  86.7 8.9 %all-to-all-start.1 = ((f32[32,16,1024]{2,1,0:T(8,128)}), f32[32,16,1024]{2,1,0:T(8,128)S(1)}, u32[]{:S(2)}, u32[]{:S(2)}) async-start(f32[32,16,1024]{2,1,0:T(8,128)} %bitcast.13), calls=%async_computation.1 | async-start | bytes 4194304 | tf_op jit(solution)/shard_map/all_to_all | solution.py:202
  95.6 1.1 collective-permute-start.17
  96.7 2.1 slice.30.refs_7_
  98.8 2.2 collective-permute-start.12
  101.0 16.7 %collective-permute-done.11.refs_6_ = f32[376,512]{1,0:T(8,128)S(1)} collective-permute-done((f32[376,512]{1,0:T(8,128)}, f32[376,512]{1,0:T(8,128)S(1)}, u32[]{:S(2)}, u32[]{:S(2)}) %collective-permute-start.11) | collective-permute-done | bytes 770080 | tf_op jit(solution)/shard_map/ppermute | solution.py:26
  117.7 43.3 %collective-permute-done.12.refs_8_ = f32[376,512]{1,0:T(8,128)S(1)} collective-permute-done((f32[376,512]{1,0:T(8,128)}, f32[376,512]{1,0:T(8,128)S(1)}, u32[]{:S(2)}, u32[]{:S(2)}) %collective-permute-start.12) | collective-permute-done | bytes 770080 | tf_op jit(solution)/shard_map/ppermute | solution.py:30
  161.6 1.8 collective-permute-done.13.refs_7_
  164.3 1.1 collective-permute-done.14.refs_9_
  165.4 9.4 %shard_map.29 = f32[512,376]{1,0:T(8,128)} custom-call(s32[3]{0:T(128)} %pad_add_fusion.place_ref, f32[8,16,1024]{2,1,0:T(8,128)} %copy-done.5, f32[8,16,1024]{2,1,0:T(8,128)} %copy-done.6, f32[4,16,1024]{2,1,0:T(8,128)} %copy-done.11, f32[4,16,1024]{2,1,0:T(8,128)} %copy-done.12, f32[8,16,1024]{2,1,0:T(8,128)} %copy-done.7, f32[8,4,16,1024]{3,2,1,0:T(8,128)} %bitcast.16, ...), custom_call_target="tpu_custom_call" | custom-call | flops 2365587456 | bytes 8044544 | tf_op jit(solution)/shard_map/pallas_call | solution.py:122
  174.9 5.9 %collective-permute-done.18.refs_11_ = f32[376,512]{1,0:T(8,128)} collective-permute-done((f32[376,512]{1,0:T(8,128)S(1)}, f32[376,512]{1,0:T(8,128)}, u32[]{:S(2)}, u32[]{:S(2)}) %collective-permute-start.18) | collective-permute-done | bytes 770080 | tf_op jit(solution)/shard_map/ppermute | solution.py:26
  181.3 9.5 %all-to-all-start.2 = ((f32[32,16,376]{2,1,0:T(8,128)}), f32[32,16,376]{2,1,0:T(8,128)S(1)}, u32[]{:S(2)}, u32[]{:S(2)}) async-start(f32[32,16,376]{2,1,0:T(8,128)} %bitcast.14), calls=%async_computation.2 | async-start | bytes 1572864 | tf_op jit(solution)/shard_map/all_to_all | solution.py:202
  190.9 18.0 %shard_map.30 = f32[512,1400]{1,0:T(8,128)} custom-call(s32[3]{0:T(128)} %pad_add_fusion.place_ref, f32[8,16,1024]{2,1,0:T(8,128)} %copy-done.5, f32[8,16,1024]{2,1,0:T(8,128)} %copy-done.6, f32[4,16,1024]{2,1,0:T(8,128)} %copy-done.11, f32[4,16,1024]{2,1,0:T(8,128)} %copy-done.12, f32[8,16,1024]{2,1,0:T(8,128)} %copy-done.7, f32[8,4,16,1024]{3,2,1,0:T(8,128)} %bitcast.17, ...), custom_call_target="tpu_custom_call" | custom-call | flops 8808038400 | bytes 18530304 | tf_op jit(solution)/shard_map/pallas_call | solution.py:122
  208.9 5.0 %all-to-all-done.2.refs_1_ = f32[32,16,376]{2,1,0:T(8,128)S(1)} async-done(((f32[32,16,376]{2,1,0:T(8,128)}), f32[32,16,376]{2,1,0:T(8,128)S(1)}, u32[]{:S(2)}, u32[]{:S(2)}) %all-to-all-start.2) | async-done | bytes 770080 | tf_op jit(solution)/shard_map/all_to_all | solution.py:202
  214.8 5.7 %all-to-all-start.3 = ((f32[32,16,1400]{2,1,0:T(8,128)}), f32[32,16,1400]{2,1,0:T(8,128)S(1)}, u32[]{:S(2)}, u32[]{:S(2)}) async-start(f32[32,16,1400]{2,1,0:T(8,128)} %bitcast.10), calls=%async_computation.3 | async-start | bytes 5767168 | tf_op jit(solution)/shard_map/all_to_all | solution.py:202
  220.5 1.6 copy-done.1
  222.1 1.1 copy-done.3
  223.2 2.0 shard_map.31.refs_1_
  225.2 63.9 %all-to-all-done.3.refs_0_ = f32[32,16,1400]{2,1,0:T(8,128)S(1)} async-done(((f32[32,16,1400]{2,1,0:T(8,128)}), f32[32,16,1400]{2,1,0:T(8,128)S(1)}, u32[]{:S(2)}, u32[]{:S(2)}) %all-to-all-start.3) | async-done | bytes 2867232 | tf_op jit(solution)/shard_map/all_to_all | solution.py:202
  289.1 2.0 shard_map.32
  (60 shorter events, 10.8 us)
Async XLA Ops:
  7.4 7.5 %collective-permute-start.2 = (f32[16,1024]{1,0:T(8,128)S(1)}, f32[16,1024]{1,0:T(8,128)S(1)}, u32[]{:S(2)}, u32[]{:S(2)}) collective-permute-start(f32[16,1024]{1,0:T(8,128)S(1)} %get-tuple-element.57), channel_id=1, source_target_pairs={{0,32},{32,64},{64,96},{96,0},{1,33},{33,65},{65,97},{97,1},{2,34}... | collective-permute-start | bytes 196616 | tf_op jit(solution)/shard_map/ppermute | solution.py:22
  9.0 6.0 %collective-permute-start.1 = (f32[16,1024]{1,0:T(8,128)S(1)}, f32[16,1024]{1,0:T(8,128)S(1)}, u32[]{:S(2)}, u32[]{:S(2)}) collective-permute-start(f32[16,1024]{1,0:T(8,128)S(1)} %get-tuple-element.57), channel_id=1, source_target_pairs={{0,64},{32,96},{64,0},{96,32},{1,65},{33,97},{65,1},{97,33},{2,66}... | collective-permute-start | bytes 196616 | tf_op jit(solution)/shard_map/ppermute | solution.py:22
  11.7 4.3 %collective-permute-start = (f32[16,1024]{1,0:T(8,128)S(1)}, f32[16,1024]{1,0:T(8,128)S(1)}, u32[]{:S(2)}, u32[]{:S(2)}) collective-permute-start(f32[16,1024]{1,0:T(8,128)S(1)} %get-tuple-element.57), channel_id=1, source_target_pairs={{0,96},{32,0},{64,32},{96,64},{1,97},{33,1},{65,33},{97,65},{2,98}... | collective-permute-start | bytes 196616 | tf_op jit(solution)/shard_map/ppermute | solution.py:22
  14.9 71.8 %copy-start.4 = (f32[1024,512]{1,0:T(8,128)}, f32[1024,512]{1,0:T(8,128)S(1)}, u32[]{:S(2)}) copy-start(f32[1024,512]{1,0:T(8,128)S(1)} %slice.29.refs_6_) | copy-start | bytes 6291460
  16.0 49.7 %collective-permute-start.7 = (f32[1024,512]{1,0:T(8,128)S(1)}, f32[1024,512]{1,0:T(8,128)}, u32[]{:S(2)}, u32[]{:S(2)}) collective-permute-start(f32[1024,512]{1,0:T(8,128)S(1)} %slice.29.refs_6_), channel_id=1, source_target_pairs={{0,128},{128,0},{1,129},{129,1},{2,130},{130,2},{3,131},{131,3},{4... | collective-permute-start | bytes 6291464 | tf_op jit(solution)/shard_map/ppermute | solution.py:26
  16.7 48.9 %collective-permute-start.8 = (f32[1024,512]{1,0:T(8,128)S(1)}, f32[1024,512]{1,0:T(8,128)}, u32[]{:S(2)}, u32[]{:S(2)}) collective-permute-start(f32[1024,512]{1,0:T(8,128)S(1)} %slice.29.refs_6_), channel_id=1, source_target_pairs={{128,2},{2,128},{130,0},{0,130},{129,3},{3,129},{131,1},{1,131},{1... | collective-permute-start | bytes 6291464 | tf_op jit(solution)/shard_map/ppermute | solution.py:30
  19.4 24.2 %all-to-all-start = ((f32[8,16,1024]{2,1,0:T(8,128)}), f32[8,16,1024]{2,1,0:T(8,128)S(1)}, u32[]{:S(2)}, u32[]{:S(2)}) async-start(f32[8,16,1024]{2,1,0:T(8,128)} %broadcast_in_dim.2), calls=%async_computation | async-start | bytes 1048576 | tf_op jit(solution)/shard_map/all_to_all | solution.py:191
  27.8 44.9 %all-gather.3.cloned.1.call-start = ((), (), s32[]{:S(2)}) async-start(), calls=%async_computation.4 | async-start | bytes 2359296 | tf_op jit(solution)/shard_map/all_gather | solution.py:192
  43.6 29.7 %copy-start.5 = (f32[8,16,1024]{2,1,0:T(8,128)}, f32[8,16,1024]{2,1,0:T(8,128)S(1)}, u32[]{:S(2)}) copy-start(f32[8,16,1024]{2,1,0:T(8,128)S(1)} %all-to-all-done.refs_0_) | copy-start | bytes 1572868
  43.6 11.9 %collective-permute-start.3 = (f32[8,16,1024]{2,1,0:T(8,128)S(1)}, f32[8,16,1024]{2,1,0:T(8,128)S(1)}, u32[]{:S(2)}, u32[]{:S(2)}) collective-permute-start(f32[8,16,1024]{2,1,0:T(8,128)S(1)} %all-to-all-done.refs_0_), channel_id=1, source_target_pairs={{0,96},{32,0},{64,32},{96,64},{1,97},{33,1},{65,33},{97,65},{2,98}... | collective-permute-start | bytes 1572872 | tf_op jit(solution)/shard_map/ppermute | solution.py:22
  46.0 12.0 %collective-permute-start.5 = (f32[8,16,1024]{2,1,0:T(8,128)S(1)}, f32[8,16,1024]{2,1,0:T(8,128)S(1)}, u32[]{:S(2)}, u32[]{:S(2)}) collective-permute-start(f32[8,16,1024]{2,1,0:T(8,128)S(1)} %all-to-all-done.refs_0_), channel_id=1, source_target_pairs={{0,32},{32,64},{64,96},{96,0},{1,33},{33,65},{65,97},{97,1},{2,34}... | collective-permute-start | bytes 1572872 | tf_op jit(solution)/shard_map/ppermute | solution.py:22
  55.5 6.4 %collective-permute-start.4 = (f32[4,16,1024]{2,1,0:T(8,128)S(1)}, f32[4,16,1024]{2,1,0:T(8,128)S(1)}, u32[]{:S(2)}, u32[]{:S(2)}) collective-permute-start(f32[4,16,1024]{2,1,0:T(8,128)S(1)} %slice.27), channel_id=1, source_target_pairs={{0,96},{32,0},{64,32},{96,64},{1,97},{33,1},{65,33},{97,65},{2,98}... | collective-permute-start | bytes 786440 | tf_op jit(solution)/shard_map/ppermute | solution.py:22
  58.0 7.7 %copy-start.7 = (f32[8,16,1024]{2,1,0:T(8,128)}, f32[8,16,1024]{2,1,0:T(8,128)S(1)}, u32[]{:S(2)}) copy-start(f32[8,16,1024]{2,1,0:T(8,128)S(1)} %collective-permute-done.5.refs_4_) | copy-start | bytes 1572868
  58.0 7.7 %collective-permute-start.6 = (f32[4,16,1024]{2,1,0:T(8,128)S(1)}, f32[4,16,1024]{2,1,0:T(8,128)S(1)}, u32[]{:S(2)}, u32[]{:S(2)}) collective-permute-start(f32[4,16,1024]{2,1,0:T(8,128)S(1)} %slice.28), channel_id=1, source_target_pairs={{0,32},{32,64},{64,96},{96,0},{1,33},{33,65},{65,97},{97,1},{2,34}... | collective-permute-start | bytes 786440 | tf_op jit(solution)/shard_map/ppermute | solution.py:22
  65.6 7.6 %copy-start.12 = (f32[4,16,1024]{2,1,0:T(8,128)}, f32[4,16,1024]{2,1,0:T(8,128)S(1)}, u32[]{:S(2)}) copy-start(f32[4,16,1024]{2,1,0:T(8,128)S(1)} %collective-permute-done.6.refs_3_) | copy-start | bytes 786436
  65.7 7.0 %collective-permute-start.9 = (f32[1024,512]{1,0:T(8,128)}, f32[1024,512]{1,0:T(8,128)}, u32[]{:S(2)}, u32[]{:S(2)}) collective-permute-start(f32[1024,512]{1,0:T(8,128)} %collective-permute-done.7.refs_6_), channel_id=1, source_target_pairs={{0,1},{1,0},{2,3},{3,2},{4,5},{5,4},{6,7},{7,6},{8,9},{9,8},{10,11... | collective-permute-start | bytes 6291464 | tf_op jit(solution)/shard_map/ppermute | solution.py:18
  65.8 7.5 %collective-permute-start.10 = (f32[1024,512]{1,0:T(8,128)}, f32[1024,512]{1,0:T(8,128)}, u32[]{:S(2)}, u32[]{:S(2)}) collective-permute-start(f32[1024,512]{1,0:T(8,128)} %collective-permute-done.8.refs_8_), channel_id=1, source_target_pairs={{0,1},{1,0},{2,3},{3,2},{4,5},{5,4},{6,7},{7,6},{8,9},{9,8},{10,11... | collective-permute-start | bytes 6291464 | tf_op jit(solution)/shard_map/ppermute | solution.py:18
  86.7 94.6 %all-to-all-start.1 = ((f32[32,16,1024]{2,1,0:T(8,128)}), f32[32,16,1024]{2,1,0:T(8,128)S(1)}, u32[]{:S(2)}, u32[]{:S(2)}) async-start(f32[32,16,1024]{2,1,0:T(8,128)} %bitcast.13), calls=%async_computation.1 | async-start | bytes 4194304 | tf_op jit(solution)/shard_map/all_to_all | solution.py:202
  95.6 79.3 %collective-permute-start.17 = (f32[1024,512]{1,0:T(8,128)}, f32[1024,512]{1,0:T(8,128)}, u32[]{:S(2)}, u32[]{:S(2)}) collective-permute-start(f32[1024,512]{1,0:T(8,128)} %collective-permute-done.7.refs_6_), channel_id=1, source_target_pairs={{128,2},{2,128},{130,0},{0,130},{129,3},{3,129},{131,1},{1,131},{1... | collective-permute-start | bytes 6291464 | tf_op jit(solution)/shard_map/ppermute | solution.py:30
  98.8 18.9 %collective-permute-start.11 = (f32[376,512]{1,0:T(8,128)}, f32[376,512]{1,0:T(8,128)S(1)}, u32[]{:S(2)}, u32[]{:S(2)}) collective-permute-start(f32[376,512]{1,0:T(8,128)} %slice.30.refs_7_), channel_id=1, source_target_pairs={{0,128},{128,0},{1,129},{129,1},{2,130},{130,2},{3,131},{131,3},{4... | collective-permute-start | bytes 2310152 | tf_op jit(solution)/shard_map/ppermute | solution.py:26
  98.8 62.2 %collective-permute-start.12 = (f32[376,512]{1,0:T(8,128)}, f32[376,512]{1,0:T(8,128)S(1)}, u32[]{:S(2)}, u32[]{:S(2)}) collective-permute-start(f32[376,512]{1,0:T(8,128)} %slice.30.refs_7_), channel_id=1, source_target_pairs={{128,2},{2,128},{130,0},{0,130},{129,3},{3,129},{131,1},{1,131},{1... | collective-permute-start | bytes 2310152 | tf_op jit(solution)/shard_map/ppermute | solution.py:30
  117.7 43.3 %copy-start.9 = (f32[376,512]{1,0:T(8,128)}, f32[376,512]{1,0:T(8,128)S(1)}, u32[]{:S(2)}) copy-start(f32[376,512]{1,0:T(8,128)S(1)} %collective-permute-done.11.refs_6_) | copy-start | bytes 2310148
  161.0 2.4 collective-permute-start.13
  161.0 4.4 %collective-permute-start.14 = (f32[376,512]{1,0:T(8,128)S(1)}, f32[376,512]{1,0:T(8,128)}, u32[]{:S(2)}, u32[]{:S(2)}) collective-permute-start(f32[376,512]{1,0:T(8,128)S(1)} %collective-permute-done.12.refs_8_), channel_id=1, source_target_pairs={{0,1},{1,0},{2,3},{3,2},{4,5},{5,4},{6,7},{7,6},{8,9},{9,8},{10,11... | collective-permute-start | bytes 2310152 | tf_op jit(solution)/shard_map/ppermute | solution.py:18
  161.5 19.3 %collective-permute-start.18 = (f32[376,512]{1,0:T(8,128)S(1)}, f32[376,512]{1,0:T(8,128)}, u32[]{:S(2)}, u32[]{:S(2)}) collective-permute-start(f32[376,512]{1,0:T(8,128)S(1)} %collective-permute-done.12.refs_8_), channel_id=1, source_target_pairs={{0,128},{128,0},{1,129},{129,1},{2,130},{130,2},{3,131},{131,3},{4... | collective-permute-start | bytes 2310152 | tf_op jit(solution)/shard_map/ppermute | solution.py:26
  161.5 29.4 %collective-permute-start.15 = (f32[1024,512]{1,0:T(8,128)}, f32[1024,512]{1,0:T(8,128)}, u32[]{:S(2)}, u32[]{:S(2)}) collective-permute-start(f32[1024,512]{1,0:T(8,128)} %copy-done.4), channel_id=1, source_target_pairs={{0,1},{1,0},{2,3},{3,2},{4,5},{5,4},{6,7},{7,6},{8,9},{9,8},{10,11... | collective-permute-start | bytes 6291464 | tf_op jit(solution)/shard_map/ppermute | solution.py:18
  180.8 10.1 %collective-permute-start.19 = (f32[1024,512]{1,0:T(8,128)}, f32[1024,512]{1,0:T(8,128)}, u32[]{:S(2)}, u32[]{:S(2)}) collective-permute-start(f32[1024,512]{1,0:T(8,128)} %collective-permute-done.17.refs_10_), channel_id=1, source_target_pairs={{0,1},{1,0},{2,3},{3,2},{4,5},{5,4},{6,7},{7,6},{8,9},{9,8},{10,11... | collective-permute-start | bytes 6291464 | tf_op jit(solution)/shard_map/ppermute | solution.py:18
  180.8 10.0 %collective-permute-start.16 = (f32[376,512]{1,0:T(8,128)}, f32[376,512]{1,0:T(8,128)}, u32[]{:S(2)}, u32[]{:S(2)}) collective-permute-start(f32[376,512]{1,0:T(8,128)} %slice.30.refs_7_), channel_id=1, source_target_pairs={{0,1},{1,0},{2,3},{3,2},{4,5},{5,4},{6,7},{7,6},{8,9},{9,8},{10,11... | collective-permute-start | bytes 2310152 | tf_op jit(solution)/shard_map/ppermute | solution.py:18
  181.3 9.6 %collective-permute-start.20 = (f32[376,512]{1,0:T(8,128)}, f32[376,512]{1,0:T(8,128)}, u32[]{:S(2)}, u32[]{:S(2)}) collective-permute-start(f32[376,512]{1,0:T(8,128)} %collective-permute-done.18.refs_11_), channel_id=1, source_target_pairs={{0,1},{1,0},{2,3},{3,2},{4,5},{5,4},{6,7},{7,6},{8,9},{9,8},{10,11... | collective-permute-start | bytes 2310152 | tf_op jit(solution)/shard_map/ppermute | solution.py:18
  181.3 27.6 %copy-start = (f32[32,16,1024]{2,1,0:T(8,128)}, f32[32,16,1024]{2,1,0:T(8,128)S(1)}, u32[]{:S(2)}) copy-start(f32[32,16,1024]{2,1,0:T(8,128)S(1)} %all-to-all-done.1.refs_0_) | copy-start | bytes 6291460
  181.3 32.6 %all-to-all-start.2 = ((f32[32,16,376]{2,1,0:T(8,128)}), f32[32,16,376]{2,1,0:T(8,128)S(1)}, u32[]{:S(2)}, u32[]{:S(2)}) async-start(f32[32,16,376]{2,1,0:T(8,128)} %bitcast.14), calls=%async_computation.2 | async-start | bytes 1572864 | tf_op jit(solution)/shard_map/all_to_all | solution.py:202
  214.8 74.4 %all-to-all-start.3 = ((f32[32,16,1400]{2,1,0:T(8,128)}), f32[32,16,1400]{2,1,0:T(8,128)S(1)}, u32[]{:S(2)}, u32[]{:S(2)}) async-start(f32[32,16,1400]{2,1,0:T(8,128)} %bitcast.10), calls=%async_computation.3 | async-start | bytes 5767168 | tf_op jit(solution)/shard_map/all_to_all | solution.py:202
  (7 other events, 15.2 us)
Sparse Core Ops, SparseCore 0:
  30.4 42.1 all-gather.2

commit v5 on v4

--- a/solution.py
+++ b/solution.py
@@ -10,7 +10,7 @@
 
 AXES = ("yl", "x", "z", "yh", "core")
 TILE = 256
-CUT = 1024
+CUT = 768
 GROUP = 16
 
 
@@ -194,9 +194,9 @@
     low, high = shift_x(ahead[:4], -1), shift_x(behind[4:], 1)
     t = (here, ahead, low, high, behind, last)
 
-    first, second = after(integrals.T[:CUT], *turns), after(integrals.T[CUT:], ahead, behind)
-    near, far = after((swap_near(first), swap_far(first)), low, high)
-    near_next, far_next = swap_near(second), swap_far(second)
+    first, second = after(integrals.T[:CUT], low, high), integrals.T[CUT:]
+    near, far = after((swap_near(first), swap_far(first)), ahead, behind)
+    near_next, far_next = after((swap_near(second), swap_far(second)), ahead, behind)
 
     def exchange(v):
         return lax.all_to_all(
@@ -204,18 +204,12 @@
         )
 
     (result,) = product(spot, t, [[near], [swap_core(near)], [far], [swap_core(far)]])
-    t = after(t, result)
-    near_next, far_next = after((near_next, far_next), result)
-    across = [swap_far(after(near, low, high)), swap_near(far_next)]
-    own = [first, second]
-    own2 = [swap_core(v) for v in after((first, second), result)]
     (result_next,) = product(
         spot, t, [[near_next], [swap_core(near_next)], [far_next], [swap_core(far_next)]]
     )
-    t = after(t, result_next)
-    other_block = [exchange(result)]
-    other_block.append(exchange(after(result_next, other_block[0])))
-    across2 = [swap_core(v) for v in after(across, result_next)]
+    other_block = [exchange(result), exchange(result_next)]
+    across = [swap_far(near), swap_near(far_next)]
+    own, own2, across2 = [first, second], [swap_core(first), swap_core(second)], [swap_core(v) for v in across]
     (own_block,) = product(spot, t, [own, own2, across, across2])
     own_block = exchange(after(own_block, other_block[1]))
     out = place((1 - yl).reshape(1), other_block)

time: 299 us -> 262 us (0.88)
  waiting for transfers between devices: 178 us -> 135 us
  local copies, waits for them, and re-layouts: 10.1 us -> 14.9 us
    ppermute x3, waiting for transfers between devices: 22.7 us -> 0.15 us  [swap_near(): return lax.ppermute(value, 'yl', [(0, 1), (1, 0)])]
    ppermute x7, waiting for transfers between devices: 18.1 us -> 7.74 us  [shift_x(): return lax.ppermute(value, 'x', [(i, (i + by) % 4) for i in range(4)])]
    ppermute x3, waiting for transfers between devices: 43.3 us -> 34.4 us  [swap_far(): return lax.ppermute(value, ('yl', 'yh'), [(2, 1), (1, 2), (3, 0), (0, 3)])]
    ppermute x8, waiting for transfers between devices: 3.53 us -> 9.4 us  [swap_core(): return lax.ppermute(value, 'core', [(0, 1), (1, 0)])]
    all_gather x1, waiting for transfers between devices: 5.83 us -> 0.01 us  [on_device(): last = lax.all_gather(last, 'z', axis=0).reshape(8, 4, rows, half)]
    unnamed x26 -> x28, local copies, waits for them, and re-layouts: 4.52 us -> 9.26 us
  transfers between devices with their start and end apart: 26 -> 26, of which waited for: 14 -> 16; matrix products, arithmetic and copies ran while one was open for 2% -> 2% of each run, Pallas kernels for 10% -> 16%
where the time goes in v5:
time: 262 us; the launch traced here: 261 us
  waiting for transfers between devices  135 us (52%)
  starting transfers between devices  51.4 us (20%)
  Pallas kernels  44.9 us (17%)
  local copies, waits for them, and re-layouts  14.9 us (6%)
  between operations  13.5 us (5%)
    all_to_all x3, waiting for transfers between devices, exchange(): lax.all_to_all(v.reshape(-1, rows, v.shape[1]), ('x', 'z'), split_axis=0,...  66.8 us
    pallas_call x3, Pallas kernels, product(): pl.pallas_call(functools.partial(product_kernel, around, counts), grid_sp...  41 us
    ppermute x3, waiting for transfers between devices, swap_far(): return lax.ppermute(value, ('yl', 'yh'), [(2, 1), (1, 2), (3, 0), (0, 3)])  34.4 us
    all_to_all x3, starting transfers between devices, exchange(): lax.all_to_all(v.reshape(-1, rows, v.shape[1]), ('x', 'z'), split_axis=0,...  24.5 us
    all_to_all x1, waiting for transfers between devices, on_device(): here = lax.all_to_all(here, 'z', split_axis=0, concat_axis=0, tiled=True)  16.5 us
    ppermute x7, starting transfers between devices, shift_x(): return lax.ppermute(value, 'x', [(i, (i + by) % 4) for i in range(4)])  12.2 us
    ppermute x8, waiting for transfers between devices, swap_core(): return lax.ppermute(value, 'core', [(0, 1), (1, 0)])  9.4 us
    unnamed x28, local copies, waits for them, and re-layouts  9.26 us
  transfers between devices with their start and end apart: 26, of which 16 were waited for; matrix products, arithmetic and copies ran while one was open for 2% of the time, Pallas kernels for 16%

profile of v5, /device:TPU:24, one launch (start us, length us, event | category | flops | bytes accessed | tf_op | source)
XLA Modules:
  0.0 261.2 jit_solution(5732077029867261929)
XLA Ops:
  7.4 1.6 collective-permute-start.2
  9.0 2.7 %collective-permute-start.1 = (f32[16,1024]{1,0:T(8,128)S(1)}, f32[16,1024]{1,0:T(8,128)S(1)}, u32[]{:S(2)}, u32[]{:S(2)}) collective-permute-start(f32[16,1024]{1,0:T(8,128)S(1)} %get-tuple-element.19), channel_id=1, source_target_pairs={{0,64},{32,96},{64,0},{96,32},{1,65},{33,97},{65,1},{97,33},{2,66}... | collective-permute-start | bytes 196616 | tf_op jit(solution)/shard_map/ppermute | solution.py:22
  11.7 1.4 collective-permute-start
  13.6 1.4 collective-permute-done.1
  17.6 8.5 %all-to-all-start = ((f32[8,16,1024]{2,1,0:T(8,128)}), f32[8,16,1024]{2,1,0:T(8,128)S(1)}, u32[]{:S(2)}, u32[]{:S(2)}) async-start(f32[8,16,1024]{2,1,0:T(8,128)} %broadcast_in_dim.2), calls=%async_computation | async-start | bytes 1048576 | tf_op jit(solution)/shard_map/all_to_all | solution.py:191
  26.1 2.6 %slice.30.refs_7_ = f32[632,512]{1,0:T(8,128)} slice(f32[1400,512]{1,0:T(8,128)} %bitcast.11), slice={[768:1400], [0:512]} | slice | bytes 2588672 | tf_op jit(solution)/shard_map/slice | solution.py:197
  29.9 16.5 %all-to-all-done.refs_0_ = f32[8,16,1024]{2,1,0:T(8,128)S(1)} async-done(((f32[8,16,1024]{2,1,0:T(8,128)}), f32[8,16,1024]{2,1,0:T(8,128)S(1)}, u32[]{:S(2)}, u32[]{:S(2)}) %all-to-all-start) | async-done | bytes 524320 | tf_op jit(solution)/shard_map/all_to_all | solution.py:191
  46.9 2.7 %collective-permute-start.3 = (f32[8,16,1024]{2,1,0:T(8,128)S(1)}, f32[8,16,1024]{2,1,0:T(8,128)S(1)}, u32[]{:S(2)}, u32[]{:S(2)}) collective-permute-start(f32[8,16,1024]{2,1,0:T(8,128)S(1)} %all-to-all-done.refs_0_), channel_id=1, source_target_pairs={{0,96},{32,0},{64,32},{96,64},{1,97},{33,1},{65,33},{97,65},{2,98}... | collective-permute-start | bytes 1572872 | tf_op jit(solution)/shard_map/ppermute | solution.py:22
  49.7 9.3 %collective-permute-done.13.refs_8_ = f32[632,512]{1,0:T(8,128)} collective-permute-done((f32[632,512]{1,0:T(8,128)}, f32[632,512]{1,0:T(8,128)}, u32[]{:S(2)}, u32[]{:S(2)}) %collective-permute-start.13) | collective-permute-done | bytes 1294368 | tf_op jit(solution)/shard_map/ppermute | solution.py:30
  59.9 3.1 %collective-permute-start.4 = (f32[4,16,1024]{2,1,0:T(8,128)S(1)}, f32[4,16,1024]{2,1,0:T(8,128)S(1)}, u32[]{:S(2)}, u32[]{:S(2)}) collective-permute-start(f32[4,16,1024]{2,1,0:T(8,128)S(1)} %slice.27), channel_id=1, source_target_pairs={{0,96},{32,0},{64,32},{96,64},{1,97},{33,1},{65,33},{97,65},{2,98}... | collective-permute-start | bytes 786440 | tf_op jit(solution)/shard_map/ppermute | solution.py:22
  63.0 1.3 slice.29.refs_6_
  64.3 4.9 %collective-permute-done.6.refs_3_ = f32[4,16,1024]{2,1,0:T(8,128)S(1)} collective-permute-done((f32[4,16,1024]{2,1,0:T(8,128)S(1)}, f32[4,16,1024]{2,1,0:T(8,128)S(1)}, u32[]{:S(2)}, u32[]{:S(2)}) %collective-permute-start.6) | collective-permute-done | bytes 262176 | tf_op jit(solution)/shard_map/ppermute | solution.py:22
  69.9 1.7 collective-permute-start.10
  72.2 11.4 %shard_map.29 = f32[512,632]{1,0:T(8,128)} custom-call(s32[3]{0:T(128)} %pad_add_fusion.place_ref, f32[8,16,1024]{2,1,0:T(8,128)} %copy-done.5, f32[8,16,1024]{2,1,0:T(8,128)} %copy-done.7, f32[4,16,1024]{2,1,0:T(8,128)} %copy-done.13, f32[4,16,1024]{2,1,0:T(8,128)} %copy-done.12, f32[8,16,1024]{2,1,0:T(8,128)} %copy-done.6, f32[8,4,16,1024]{3,2,1,0:T(8,128)} %bitcast.15, ...), custom_call_target="tpu_custom_call" | custom-call | flops 3976200192 | bytes 10665984 | tf_op jit(solution)/shard_map/pallas_call | solution.py:122
  83.5 9.1 %all-to-all-start.1 = ((f32[32,16,632]{2,1,0:T(8,128)}), f32[32,16,632]{2,1,0:T(8,128)S(1)}, u32[]{:S(2)}, u32[]{:S(2)}) async-start(f32[32,16,632]{2,1,0:T(8,128)} %bitcast.14), calls=%async_computation.1 | async-start | bytes 2621440 | tf_op jit(solution)/shard_map/all_to_all | solution.py:202
  92.7 14.3 %collective-permute-done.10.refs_8_ = f32[768,512]{1,0:T(8,128)} collective-permute-done((f32[768,512]{1,0:T(8,128)}, f32[768,512]{1,0:T(8,128)}, u32[]{:S(2)}, u32[]{:S(2)}) %collective-permute-start.10) | collective-permute-done | bytes 1572896 | tf_op jit(solution)/shard_map/ppermute | solution.py:30
  107.6 1.6 collective-permute-start.11
  109.2 2.6 collective-permute-done.20.refs_9_
  112.9 11.6 %shard_map.30 = f32[512,768]{1,0:T(8,128)} custom-call(s32[3]{0:T(128)} %pad_add_fusion.place_ref, f32[8,16,1024]{2,1,0:T(8,128)} %copy-done.5, f32[8,16,1024]{2,1,0:T(8,128)} %copy-done.7, f32[4,16,1024]{2,1,0:T(8,128)} %copy-done.13, f32[4,16,1024]{2,1,0:T(8,128)} %copy-done.12, f32[8,16,1024]{2,1,0:T(8,128)} %copy-done.6, f32[8,4,16,1024]{3,2,1,0:T(8,128)} %bitcast.16, ...), custom_call_target="tpu_custom_call" | custom-call | flops 4831838208 | bytes 12058624 | tf_op jit(solution)/shard_map/pallas_call | solution.py:122
  124.5 1.1 all-to-all-done.1.refs_1_
  126.8 7.6 %all-to-all-start.3 = ((f32[32,16,768]{2,1,0:T(8,128)}), f32[32,16,768]{2,1,0:T(8,128)S(1)}, u32[]{:S(2)}, u32[]{:S(2)}) async-start(f32[32,16,768]{2,1,0:T(8,128)} %bitcast.13), calls=%async_computation.3 | async-start | bytes 3145728 | tf_op jit(solution)/shard_map/all_to_all | solution.py:202
  134.5 10.9 %collective-permute-done.11.refs_10_ = f32[768,512]{1,0:T(8,128)} collective-permute-done((f32[768,512]{1,0:T(8,128)S(1)}, f32[768,512]{1,0:T(8,128)}, u32[]{:S(2)}, u32[]{:S(2)}) %collective-permute-start.11) | collective-permute-done | bytes 1572896 | tf_op jit(solution)/shard_map/ppermute | solution.py:30
  145.9 5.0 %collective-permute-done.8.refs_9_ = f32[632,512]{1,0:T(8,128)S(1)} collective-permute-done((f32[632,512]{1,0:T(8,128)}, f32[632,512]{1,0:T(8,128)S(1)}, u32[]{:S(2)}, u32[]{:S(2)}) %collective-permute-start.8) | collective-permute-done | bytes 1294368 | tf_op jit(solution)/shard_map/ppermute | solution.py:18
  153.8 1.2 copy-done.9
  155.0 18.0 %shard_map.28 = f32[512,1400]{1,0:T(8,128)} custom-call(s32[3]{0:T(128)} %pad_add_fusion.place_ref, f32[8,16,1024]{2,1,0:T(8,128)} %copy-done.5, f32[8,16,1024]{2,1,0:T(8,128)} %copy-done.7, f32[4,16,1024]{2,1,0:T(8,128)} %copy-done.13, f32[4,16,1024]{2,1,0:T(8,128)} %copy-done.12, f32[8,16,1024]{2,1,0:T(8,128)} %copy-done.6, f32[8,4,16,1024]{3,2,1,0:T(8,128)} %bitcast.17, ...), custom_call_target="tpu_custom_call" | custom-call | flops 8808038400 | bytes 18530304 | tf_op jit(solution)/shard_map/pallas_call | solution.py:122
  174.0 1.1 copy-done
  175.2 7.8 %all-to-all-start.2 = ((f32[32,16,1400]{2,1,0:T(8,128)}), f32[32,16,1400]{2,1,0:T(8,128)S(1)}, u32[]{:S(2)}, u32[]{:S(2)}) async-start(f32[32,16,1400]{2,1,0:T(8,128)} %bitcast.10), calls=%async_computation.2 | async-start | bytes 5767168 | tf_op jit(solution)/shard_map/all_to_all | solution.py:202
  183.0 1.4 copy-done.1
  184.4 1.3 copy-done.3
  185.7 2.0 shard_map.31.refs_1_
  187.7 64.7 %all-to-all-done.2.refs_0_ = f32[32,16,1400]{2,1,0:T(8,128)S(1)} async-done(((f32[32,16,1400]{2,1,0:T(8,128)}), f32[32,16,1400]{2,1,0:T(8,128)S(1)}, u32[]{:S(2)}, u32[]{:S(2)}) %all-to-all-start.2) | async-done | bytes 2867232 | tf_op jit(solution)/shard_map/all_to_all | solution.py:202
  252.3 2.0 shard_map.32
  (62 shorter events, 15.4 us)
Async XLA Ops:
  6.5 65.7 %all-gather.3.cloned.1.call-start = ((), (), s32[]{:S(2)}) async-start(), calls=%async_computation.4 | async-start | bytes 2359296 | tf_op jit(solution)/shard_map/all_gather | solution.py:192
  7.4 6.1 %collective-permute-start.2 = (f32[16,1024]{1,0:T(8,128)S(1)}, f32[16,1024]{1,0:T(8,128)S(1)}, u32[]{:S(2)}, u32[]{:S(2)}) collective-permute-start(f32[16,1024]{1,0:T(8,128)S(1)} %get-tuple-element.19), channel_id=1, source_target_pairs={{0,32},{32,64},{64,96},{96,0},{1,33},{33,65},{65,97},{97,1},{2,34}... | collective-permute-start | bytes 196616 | tf_op jit(solution)/shard_map/ppermute | solution.py:22
  9.0 5.9 %collective-permute-start.1 = (f32[16,1024]{1,0:T(8,128)S(1)}, f32[16,1024]{1,0:T(8,128)S(1)}, u32[]{:S(2)}, u32[]{:S(2)}) collective-permute-start(f32[16,1024]{1,0:T(8,128)S(1)} %get-tuple-element.19), channel_id=1, source_target_pairs={{0,64},{32,96},{64,0},{96,32},{1,65},{33,97},{65,1},{97,33},{2,66}... | collective-permute-start | bytes 196616 | tf_op jit(solution)/shard_map/ppermute | solution.py:22
  11.7 4.3 %collective-permute-start = (f32[16,1024]{1,0:T(8,128)S(1)}, f32[16,1024]{1,0:T(8,128)S(1)}, u32[]{:S(2)}, u32[]{:S(2)}) collective-permute-start(f32[16,1024]{1,0:T(8,128)S(1)} %get-tuple-element.19), channel_id=1, source_target_pairs={{0,96},{32,0},{64,32},{96,64},{1,97},{33,1},{65,33},{97,65},{2,98}... | collective-permute-start | bytes 196616 | tf_op jit(solution)/shard_map/ppermute | solution.py:22
  17.6 28.8 %all-to-all-start = ((f32[8,16,1024]{2,1,0:T(8,128)}), f32[8,16,1024]{2,1,0:T(8,128)S(1)}, u32[]{:S(2)}, u32[]{:S(2)}) async-start(f32[8,16,1024]{2,1,0:T(8,128)} %broadcast_in_dim.2), calls=%async_computation | async-start | bytes 1048576 | tf_op jit(solution)/shard_map/all_to_all | solution.py:191
  26.1 36.9 %copy-start.4 = (f32[512,1400]{0,1:T(8,128)S(1)}, f32[512,1400]{0,1:T(8,128)}, u32[]{:S(2)}) copy-start(f32[512,1400]{0,1:T(8,128)} %param.3) | copy-start | bytes 8601604
  28.7 30.2 %collective-permute-start.13 = (f32[632,512]{1,0:T(8,128)}, f32[632,512]{1,0:T(8,128)}, u32[]{:S(2)}, u32[]{:S(2)}) collective-permute-start(f32[632,512]{1,0:T(8,128)} %slice.30.refs_7_), channel_id=1, source_target_pairs={{128,2},{2,128},{130,0},{0,130},{129,3},{3,129},{131,1},{1,131},{1... | collective-permute-start | bytes 3883016 | tf_op jit(solution)/shard_map/ppermute | solution.py:30
  28.9 30.0 %collective-permute-start.12 = (f32[632,512]{1,0:T(8,128)}, f32[632,512]{1,0:T(8,128)}, u32[]{:S(2)}, u32[]{:S(2)}) collective-permute-start(f32[632,512]{1,0:T(8,128)} %slice.30.refs_7_), channel_id=1, source_target_pairs={{0,128},{128,0},{1,129},{129,1},{2,130},{130,2},{3,131},{131,3},{4... | collective-permute-start | bytes 3883016 | tf_op jit(solution)/shard_map/ppermute | solution.py:26
  46.4 17.8 %copy-start.5 = (f32[8,16,1024]{2,1,0:T(8,128)}, f32[8,16,1024]{2,1,0:T(8,128)S(1)}, u32[]{:S(2)}) copy-start(f32[8,16,1024]{2,1,0:T(8,128)S(1)} %all-to-all-done.refs_0_) | copy-start | bytes 1572868
  46.4 12.5 %collective-permute-start.5 = (f32[8,16,1024]{2,1,0:T(8,128)S(1)}, f32[8,16,1024]{2,1,0:T(8,128)S(1)}, u32[]{:S(2)}, u32[]{:S(2)}) collective-permute-start(f32[8,16,1024]{2,1,0:T(8,128)S(1)} %all-to-all-done.refs_0_), channel_id=1, source_target_pairs={{0,32},{32,64},{64,96},{96,0},{1,33},{33,65},{65,97},{97,1},{2,34}... | collective-permute-start | bytes 1572872 | tf_op jit(solution)/shard_map/ppermute | solution.py:22
  46.9 12.0 %collective-permute-start.3 = (f32[8,16,1024]{2,1,0:T(8,128)S(1)}, f32[8,16,1024]{2,1,0:T(8,128)S(1)}, u32[]{:S(2)}, u32[]{:S(2)}) collective-permute-start(f32[8,16,1024]{2,1,0:T(8,128)S(1)} %all-to-all-done.refs_0_), channel_id=1, source_target_pairs={{0,96},{32,0},{64,32},{96,64},{1,97},{33,1},{65,33},{97,65},{2,98}... | collective-permute-start | bytes 1572872 | tf_op jit(solution)/shard_map/ppermute | solution.py:22
  58.9 13.2 %collective-permute-start.17 = (f32[632,512]{1,0:T(8,128)}, f32[632,512]{1,0:T(8,128)}, u32[]{:S(2)}, u32[]{:S(2)}) collective-permute-start(f32[632,512]{1,0:T(8,128)} %collective-permute-done.12.refs_6_), channel_id=1, source_target_pairs={{0,1},{1,0},{2,3},{3,2},{4,5},{5,4},{6,7},{7,6},{8,9},{9,8},{10,11... | collective-permute-start | bytes 3883016 | tf_op jit(solution)/shard_map/ppermute | solution.py:18
  59.0 13.1 %collective-permute-start.18 = (f32[632,512]{1,0:T(8,128)}, f32[632,512]{1,0:T(8,128)}, u32[]{:S(2)}, u32[]{:S(2)}) collective-permute-start(f32[632,512]{1,0:T(8,128)} %collective-permute-done.13.refs_8_), channel_id=1, source_target_pairs={{0,1},{1,0},{2,3},{3,2},{4,5},{5,4},{6,7},{7,6},{8,9},{9,8},{10,11... | collective-permute-start | bytes 3883016 | tf_op jit(solution)/shard_map/ppermute | solution.py:18
  59.6 9.6 %collective-permute-start.6 = (f32[4,16,1024]{2,1,0:T(8,128)S(1)}, f32[4,16,1024]{2,1,0:T(8,128)S(1)}, u32[]{:S(2)}, u32[]{:S(2)}) collective-permute-start(f32[4,16,1024]{2,1,0:T(8,128)S(1)} %slice.28), channel_id=1, source_target_pairs={{0,32},{32,64},{64,96},{96,0},{1,33},{33,65},{65,97},{97,1},{2,34}... | collective-permute-start | bytes 786440 | tf_op jit(solution)/shard_map/ppermute | solution.py:22
  59.9 9.3 %collective-permute-start.4 = (f32[4,16,1024]{2,1,0:T(8,128)S(1)}, f32[4,16,1024]{2,1,0:T(8,128)S(1)}, u32[]{:S(2)}, u32[]{:S(2)}) collective-permute-start(f32[4,16,1024]{2,1,0:T(8,128)S(1)} %slice.27), channel_id=1, source_target_pairs={{0,96},{32,0},{64,32},{96,64},{1,97},{33,1},{65,33},{97,65},{2,98}... | collective-permute-start | bytes 786440 | tf_op jit(solution)/shard_map/ppermute | solution.py:22
  69.9 1.7 copy-start.13
  69.9 37.1 %collective-permute-start.10 = (f32[768,512]{1,0:T(8,128)}, f32[768,512]{1,0:T(8,128)}, u32[]{:S(2)}, u32[]{:S(2)}) collective-permute-start(f32[768,512]{1,0:T(8,128)} %slice.29.refs_6_), channel_id=1, source_target_pairs={{128,2},{2,128},{130,0},{0,130},{129,3},{3,129},{131,1},{1,131},{1... | collective-permute-start | bytes 4718600 | tf_op jit(solution)/shard_map/ppermute | solution.py:30
  71.6 35.5 %collective-permute-start.9 = (f32[768,512]{1,0:T(8,128)}, f32[768,512]{1,0:T(8,128)S(1)}, u32[]{:S(2)}, u32[]{:S(2)}) collective-permute-start(f32[768,512]{1,0:T(8,128)} %slice.29.refs_6_), channel_id=1, source_target_pairs={{0,128},{128,0},{1,129},{129,1},{2,130},{130,2},{3,131},{131,3},{4... | collective-permute-start | bytes 4718600 | tf_op jit(solution)/shard_map/ppermute | solution.py:26
  83.5 42.1 %all-to-all-start.1 = ((f32[32,16,632]{2,1,0:T(8,128)}), f32[32,16,632]{2,1,0:T(8,128)S(1)}, u32[]{:S(2)}, u32[]{:S(2)}) async-start(f32[32,16,632]{2,1,0:T(8,128)} %bitcast.14), calls=%async_computation.1 | async-start | bytes 2621440 | tf_op jit(solution)/shard_map/all_to_all | solution.py:202
  107.1 5.8 %copy-start.8 = (f32[768,512]{1,0:T(8,128)}, f32[768,512]{1,0:T(8,128)S(1)}, u32[]{:S(2)}) copy-start(f32[768,512]{1,0:T(8,128)S(1)} %collective-permute-done.9.refs_6_) | copy-start | bytes 4718596
  107.1 4.7 %collective-permute-start.20 = (f32[768,512]{1,0:T(8,128)}, f32[768,512]{1,0:T(8,128)}, u32[]{:S(2)}, u32[]{:S(2)}) collective-permute-start(f32[768,512]{1,0:T(8,128)} %collective-permute-done.10.refs_8_), channel_id=1, source_target_pairs={{0,1},{1,0},{2,3},{3,2},{4,5},{5,4},{6,7},{7,6},{8,9},{9,8},{10,11... | collective-permute-start | bytes 4718600 | tf_op jit(solution)/shard_map/ppermute | solution.py:18
  107.1 5.8 %collective-permute-start.19 = (f32[768,512]{1,0:T(8,128)S(1)}, f32[768,512]{1,0:T(8,128)}, u32[]{:S(2)}, u32[]{:S(2)}) collective-permute-start(f32[768,512]{1,0:T(8,128)S(1)} %collective-permute-done.9.refs_6_), channel_id=1, source_target_pairs={{0,1},{1,0},{2,3},{3,2},{4,5},{5,4},{6,7},{7,6},{8,9},{9,8},{10,11... | collective-permute-start | bytes 4718600 | tf_op jit(solution)/shard_map/ppermute | solution.py:18
  107.6 37.7 %collective-permute-start.11 = (f32[768,512]{1,0:T(8,128)S(1)}, f32[768,512]{1,0:T(8,128)}, u32[]{:S(2)}, u32[]{:S(2)}) collective-permute-start(f32[768,512]{1,0:T(8,128)S(1)} %collective-permute-done.9.refs_6_), channel_id=1, source_target_pairs={{128,2},{2,128},{130,0},{0,130},{129,3},{3,129},{131,1},{1,131},{1... | collective-permute-start | bytes 4718600 | tf_op jit(solution)/shard_map/ppermute | solution.py:30
  109.2 36.7 %collective-permute-start.14 = (f32[632,512]{1,0:T(8,128)}, f32[632,512]{1,0:T(8,128)}, u32[]{:S(2)}, u32[]{:S(2)}) collective-permute-start(f32[632,512]{1,0:T(8,128)} %collective-permute-done.13.refs_8_), channel_id=1, source_target_pairs={{0,128},{128,0},{1,129},{129,1},{2,130},{130,2},{3,131},{131,3},{4... | collective-permute-start | bytes 3883016 | tf_op jit(solution)/shard_map/ppermute | solution.py:26
  126.8 47.3 %all-to-all-start.3 = ((f32[32,16,768]{2,1,0:T(8,128)}), f32[32,16,768]{2,1,0:T(8,128)S(1)}, u32[]{:S(2)}, u32[]{:S(2)}) async-start(f32[32,16,768]{2,1,0:T(8,128)} %bitcast.13), calls=%async_computation.3 | async-start | bytes 3145728 | tf_op jit(solution)/shard_map/all_to_all | solution.py:202
  134.4 16.4 %collective-permute-start.7 = (f32[768,512]{1,0:T(8,128)}, f32[768,512]{1,0:T(8,128)}, u32[]{:S(2)}, u32[]{:S(2)}) collective-permute-start(f32[768,512]{1,0:T(8,128)} %slice.29.refs_6_), channel_id=1, source_target_pairs={{0,1},{1,0},{2,3},{3,2},{4,5},{5,4},{6,7},{7,6},{8,9},{9,8},{10,11... | collective-permute-start | bytes 4718600 | tf_op jit(solution)/shard_map/ppermute | solution.py:18
  145.4 8.4 %collective-permute-start.15 = (f32[768,512]{1,0:T(8,128)}, f32[768,512]{1,0:T(8,128)S(1)}, u32[]{:S(2)}, u32[]{:S(2)}) collective-permute-start(f32[768,512]{1,0:T(8,128)} %collective-permute-done.11.refs_10_), channel_id=1, source_target_pairs={{0,1},{1,0},{2,3},{3,2},{4,5},{5,4},{6,7},{7,6},{8,9},{9,8},{10,11... | collective-permute-start | bytes 4718600 | tf_op jit(solution)/shard_map/ppermute | solution.py:18
  145.4 5.5 %collective-permute-start.8 = (f32[632,512]{1,0:T(8,128)}, f32[632,512]{1,0:T(8,128)S(1)}, u32[]{:S(2)}, u32[]{:S(2)}) collective-permute-start(f32[632,512]{1,0:T(8,128)} %slice.30.refs_7_), channel_id=1, source_target_pairs={{0,1},{1,0},{2,3},{3,2},{4,5},{5,4},{6,7},{7,6},{8,9},{9,8},{10,11... | collective-permute-start | bytes 3883016 | tf_op jit(solution)/shard_map/ppermute | solution.py:18
  145.9 6.8 %collective-permute-start.16 = (f32[632,512]{1,0:T(8,128)}, f32[632,512]{1,0:T(8,128)S(1)}, u32[]{:S(2)}, u32[]{:S(2)}) collective-permute-start(f32[632,512]{1,0:T(8,128)} %collective-permute-done.14.refs_11_), channel_id=1, source_target_pairs={{0,1},{1,0},{2,3},{3,2},{4,5},{5,4},{6,7},{7,6},{8,9},{9,8},{10,11... | collective-permute-start | bytes 3883016 | tf_op jit(solution)/shard_map/ppermute | solution.py:18
  175.2 77.2 %all-to-all-start.2 = ((f32[32,16,1400]{2,1,0:T(8,128)}), f32[32,16,1400]{2,1,0:T(8,128)S(1)}, u32[]{:S(2)}, u32[]{:S(2)}) async-start(f32[32,16,1400]{2,1,0:T(8,128)} %bitcast.10), calls=%async_computation.2 | async-start | bytes 5767168 | tf_op jit(solution)/shard_map/all_to_all | solution.py:202
  182.9 1.4 copy-start.1
  184.4 1.3 copy-start.3
  (8 other events, 8.1 us)
Sparse Core Ops, SparseCore 0:
  16.9 48.5 all-gather.2

commit v6 on v5

v6 whole, which is shorter than its diff:
```python
import functools
import math

import jax
import jax.numpy as jnp
from jax import lax
from jax.experimental import pallas as pl
from jax.experimental.pallas import tpu as pltpu
from jax.sharding import Mesh, PartitionSpec as P

AXES = ("yl", "x", "z", "yh", "core")
TILE = 256
CUT = 3
GROUP = 16


def swap_core(value):
    return lax.ppermute(value, "core", [(0, 1), (1, 0)])


def shift_x(value, by):
    return lax.ppermute(value, "x", [(i, (i + by) % 4) for i in range(4)])


def swap_near(value):
    return lax.ppermute(value, "yl", [(0, 1), (1, 0)])


def swap_far(value):
    return lax.ppermute(value, ("yl", "yh"), [(2, 1), (1, 2), (3, 0), (0, 3)])


def halves(value):
    top = value.astype(jnp.bfloat16)
    rest = (value - top.astype(jnp.float32)).astype(jnp.bfloat16)
    return top, rest


def load_amplitudes(place_ref, first_refs, last_ref, top_ref, rest_ref):
    here_ref, ahead_ref, low_ref, high_ref, behind_ref = first_refs
    own, x = place_ref[0], place_ref[1]
    heights, _, rows, half = last_ref.shape
    part = half // 2

    @pl.loop(0, 4 * heights)
    def _(i):
        q, there = i // heights, lax.rem(i, heights)
        source = own ^ q
        take = pl.ds(pl.multiple_of((source & 1) * part, part), part)
        into = pl.ds(pl.multiple_of(q * part, part), part)
        below = there < heights // 2
        opposite = jnp.where(
            below,
            low_ref[jnp.minimum(there, heights // 2 - 1), :, take],
            high_ref[jnp.maximum(there - heights // 2, 0), :, take],
        )
        first = [here_ref[there, :, take], ahead_ref[there, :, take], opposite, behind_ref[there, :, take]]
        for d in range(4):
            value = jnp.where(source < 2, first[d], last_ref[there, d, :, take])
            row = lax.rem(x + d, 4) * (heights * rows) + there * rows
            into_rows = pl.ds(pl.multiple_of(row, rows), rows)
            top_ref[into_rows, into], rest_ref[into_rows, into] = halves(value)


def product_kernel(counts, lo, place_ref, *refs):
    pieces = refs[6 : 6 + sum(len(tiles) for tiles in counts)]
    out_ref, top_ref, rest_ref = refs[-3:]

    @pl.when(pl.program_id(0) == 0)
    def _():
        load_amplitudes(place_ref, refs[:5], refs[5], top_ref, rest_ref)

    dot = functools.partial(
        lax.dot_general,
        dimension_numbers=(((1,), (1,)), ((), ())),
        preferred_element_type=jnp.float32,
    )
    total, at = None, 0
    for q, tiles in enumerate(counts):
        value, start = pieces[at][...], tiles[0] - lo
        for i, count in enumerate(tiles[1:]):
            value = jnp.where(pl.program_id(0) < start, value, pieces[at + 1 + i][...])
            start += count
        at += len(tiles)
        top, rest = halves(value)
        depth = pl.ds(q * value.shape[1], value.shape[1])
        t_top, t_rest = top_ref[:, depth], rest_ref[:, depth]
        term = dot(t_top, rest) + dot(t_rest, top) + dot(t_top, top)
        total = term if total is None else total + term
    out_ref[...] = 0.5 * total


def product(place, amplitudes, quarters, tiles=None, columns=None, out=None):
    last = amplitudes[-1]
    rows, depth = math.prod(last.shape[:3]), 2 * last.shape[3]
    part = depth // 4
    whole_count = sum(piece.shape[0] for piece in quarters[0])
    lo, hi = tiles or (0, pl.cdiv(whole_count, TILE))
    count = min(hi * TILE, whole_count) - lo * TILE
    columns = out.shape[1] if out is not None else columns or count
    skip = (columns - count) // TILE if out is not None else 0
    specs, counts = [], []
    for quarter in quarters:
        start, sizes = -lo, []
        for piece in quarter:
            size = pl.cdiv(piece.shape[0], TILE)
            specs.append(
                pl.BlockSpec(
                    (TILE, part),
                    lambda n, place, start=start, size=size: (jnp.clip(n - start, 0, size - 1), 0),
                )
            )
            sizes.append(size)
            start += size
        counts.append(sizes)
    whole = [
        pl.BlockSpec(v.shape, lambda n, place, v=v: (0,) * v.ndim, pipeline_mode=pl.Buffered(1))
        for v in amplitudes
    ]
    return pl.pallas_call(
        functools.partial(product_kernel, counts, lo),
        grid_spec=pltpu.PrefetchScalarGridSpec(
            num_scalar_prefetch=1,
            grid=(hi - lo,),
            in_specs=whole + specs + ([] if out is None else [pl.BlockSpec(memory_space=pl.ANY)]),
            out_specs=pl.BlockSpec((rows, TILE), lambda n, place: (0, n + skip)),
            scratch_shapes=[pltpu.VMEM((rows, depth), jnp.bfloat16)] * 2,
        ),
        out_shape=jax.ShapeDtypeStruct((rows, columns), jnp.float32),
        input_output_aliases={} if out is None else {1 + len(whole) + len(specs): 0},
        compiler_params=pltpu.CompilerParams(vmem_limit_bytes=60 << 20),
        cost_estimate=pl.CostEstimate(
            flops=6 * rows * depth * count,
            bytes_accessed=4 * (rows * depth + depth * count + rows * count),
            transcendentals=0,
        ),
    )(place, *amplitudes, *[v for q in quarters for v in q], *([] if out is None else [out]))


def place_kernel(at_ref, first_ref, second_ref, out_ref):
    kept = out_ref.shape[1] // GROUP - first_ref.shape[2]
    other = pl.program_id(1) == 0

    @pl.when(other)
    def _():
        for s in range(GROUP):
            start = s * (kept + first_ref.shape[2])
            out_ref[:, start : start + kept] = second_ref[s, :, :kept]
            out_ref[:, start + kept : start + kept + first_ref.shape[2]] = first_ref[s]

    @pl.when(jnp.logical_not(other))
    def _():
        width = second_ref.shape[2] - kept
        for s in range(GROUP):
            out_ref[:, s * width : (s + 1) * width] = second_ref[s, :, kept:]


def place(at, first, second):
    sources, rows, _ = first.shape
    width = (first.shape[2] + second.shape[2]) // 2
    steps = sources // GROUP
    return pl.pallas_call(
        place_kernel,
        grid_spec=pltpu.PrefetchScalarGridSpec(
            num_scalar_prefetch=1,
            grid=(steps, 2),
            in_specs=[
                pl.BlockSpec((GROUP, rows, v.shape[2]), lambda g, i, at: (g, 0, 0))
                for v in (first, second)
            ],
            out_specs=pl.BlockSpec(
                (rows, GROUP * width), lambda g, i, at: (0, lax.rem(at[0] + 1 + i, 2) * steps + g)
            ),
        ),
        out_shape=jax.ShapeDtypeStruct((rows, 2 * sources * width), jnp.float32),
        compiler_params=pltpu.CompilerParams(vmem_limit_bytes=24 << 20),
        cost_estimate=pl.CostEstimate(
            flops=0, bytes_accessed=16 * sources * rows * width, transcendentals=0
        ),
    )(at, first, second)


def after(value, *others):
    return lax.optimization_barrier((value, *others))[0]


def on_device(amplitudes, integrals):
    x, yl, yh, core = (lax.axis_index(name) for name in ("x", "yl", "yh", "core"))
    rows, depth = amplitudes.shape
    columns = integrals.shape[1]
    half = depth // 2
    spot = jnp.stack([2 * yh + core, x])

    turns = [shift_x(amplitudes[:, half:], -d) for d in (1, 2, 3)]
    last = jnp.concatenate([amplitudes[:, half:]] + turns)
    here = jnp.broadcast_to(after(amplitudes[:, :half], last)[None], (8, rows, half))
    here = lax.all_to_all(here, "z", split_axis=0, concat_axis=0, tiled=True)
    last = lax.all_gather(last, "z", axis=0).reshape(8, 4, rows, half)
    ahead, behind = shift_x(here, -1), shift_x(here, 1)
    low, high = shift_x(ahead[:4], -1), shift_x(behind[4:], 1)
    t = (here, ahead, low, high, behind, last)

    own = integrals.T
    near, far = after((swap_near(own), swap_far(own)), low, high)
    across = [swap_far(near[: CUT * TILE]), swap_near(far[CUT * TILE :])]
    pieces = [[near], [swap_core(near)], [far], [swap_core(far)]]

    def exchange(v):
        return lax.all_to_all(
            v.reshape(-1, rows, v.shape[1]), ("x", "z"), split_axis=0, concat_axis=0, tiled=True
        )

    first = product(spot, t, pieces, tiles=(CUT, pl.cdiv(columns, TILE)))
    t = after(t, first)
    second = product(spot, t, pieces, tiles=(0, CUT), columns=CUT * TILE + columns)
    first = exchange(first)
    own2, across2 = swap_core(own), [swap_core(v) for v in across]
    second = product(spot, t, [[own], [own2], across, across2], out=second)
    first, second, at = lax.optimization_barrier((first, second, yl.reshape(1)))
    return place(at, first, exchange(second))


def solution(mesh):
    grid = Mesh(mesh.devices.reshape(2, 4, 8, 2, 2), AXES)
    return jax.shard_map(
        on_device,
        mesh=grid,
        in_specs=(P(AXES, None), P(("yh", "core"), ("yl", "x", "z"))),
        out_specs=P(AXES, None),
        check_vma=False,
    )
```

time: 262 us -> 268 us (1.023)
  blocking collectives: 0 us -> 113 us
  waiting for transfers between devices: 135 us -> 55.5 us
  starting transfers between devices: 51.4 us -> 32.5 us
  local copies, waits for them, and re-layouts: 14.9 us -> 6.57 us
    all_to_all x0 -> x1, blocking collectives: none -> 113 us  [exchange(): lax.all_to_all(v.reshape(-1, rows, v.shape[1]), ('x', 'z'), split_axis=0,...]
    all_to_all x3 -> x1, waiting for transfers between devices: 66.8 us -> 0.13 us  [exchange(): lax.all_to_all(v.reshape(-1, rows, v.shape[1]), ('x', 'z'), split_axis=0,...]
    ppermute x3 -> x2, waiting for transfers between devices: 34.4 us -> 5.57 us  [swap_far(): return lax.ppermute(value, ('yl', 'yh'), [(2, 1), (1, 2), (3, 0), (0, 3)])]
    all_to_all x3 -> x1, starting transfers between devices: 24.5 us -> 11.3 us  [exchange(): lax.all_to_all(v.reshape(-1, rows, v.shape[1]), ('x', 'z'), split_axis=0,...]
    ppermute x7, waiting for transfers between devices: 7.74 us -> 20.9 us  [shift_x(): return lax.ppermute(value, 'x', [(i, (i + by) % 4) for i in range(4)])]
    unnamed x28 -> x14, local copies, waits for them, and re-layouts: 9.26 us -> 1.08 us
    ppermute x3 -> x2, waiting for transfers between devices: 0.15 us -> 5.76 us  [swap_near(): return lax.ppermute(value, 'yl', [(0, 1), (1, 0)])]
    ppermute x7, starting transfers between devices: 12.2 us -> 8.57 us  [shift_x(): return lax.ppermute(value, 'x', [(i, (i + by) % 4) for i in range(4)])]
  transfers between devices with their start and end apart: 26 -> 19, of which waited for: 16 -> 13; matrix products, arithmetic and copies ran while one was open for 2% -> 3% of each run, Pallas kernels for 16% -> 15%
where the time goes in v6:
time: 268 us; the launch traced here: 267 us
  blocking collectives  113 us (42%)
  waiting for transfers between devices  55.5 us (21%)
  Pallas kernels  43.8 us (16%)
  starting transfers between devices  32.5 us (12%)
  between operations  13.5 us (5%)
  local copies, waits for them, and re-layouts  6.57 us (2%)
    all_to_all x1, blocking collectives, exchange(): lax.all_to_all(v.reshape(-1, rows, v.shape[1]), ('x', 'z'), split_axis=0,...  113 us
    pallas_call x3, Pallas kernels, product(): pl.pallas_call(functools.partial(product_kernel, counts, lo), grid_spec=p...  40.3 us
    ppermute x7, waiting for transfers between devices, shift_x(): return lax.ppermute(value, 'x', [(i, (i + by) % 4) for i in range(4)])  20.9 us
    all_to_all x1, waiting for transfers between devices, on_device(): here = lax.all_to_all(here, 'z', split_axis=0, concat_axis=0, tiled=True)  15.2 us
    all_to_all x1, starting transfers between devices, exchange(): lax.all_to_all(v.reshape(-1, rows, v.shape[1]), ('x', 'z'), split_axis=0,...  11.3 us
    ppermute x7, starting transfers between devices, shift_x(): return lax.ppermute(value, 'x', [(i, (i + by) % 4) for i in range(4)])  8.57 us
    all_to_all x1, starting transfers between devices, on_device(): here = lax.all_to_all(here, 'z', split_axis=0, concat_axis=0, tiled=True)  8.47 us
    ppermute x5, waiting for transfers between devices, swap_core(): return lax.ppermute(value, 'core', [(0, 1), (1, 0)])  7.22 us
  transfers between devices with their start and end apart: 19, of which 13 were waited for; matrix products, arithmetic and copies ran while one was open for 3% of the time, Pallas kernels for 15%

profile of v6, /device:TPU:24, one launch (start us, length us, event | category | flops | bytes accessed | tf_op | source)
XLA Modules:
  0.0 266.7 jit_solution(9748288560663596728)
XLA Ops:
  6.5 0.7 collective-permute-start.7
  7.3 1.2 collective-permute-start.8
  8.5 0.9 fusion
  9.4 2.7 %collective-permute-start = (f32[16,1024]{1,0:T(8,128)S(1)}, f32[16,1024]{1,0:T(8,128)S(1)}, u32[]{:S(2)}, u32[]{:S(2)}) collective-permute-start(f32[16,1024]{1,0:T(8,128)S(1)} %get-tuple-element.29), channel_id=1, source_target_pairs={{0,96},{32,0},{64,32},{96,64},{1,97},{33,1},{65,33},{97,65},{2,98}... | collective-permute-start | bytes 196616 | tf_op jit(solution)/shard_map/ppermute | solution.py:22
  12.1 0.8 collective-permute-start.1
  12.9 0.9 collective-permute-start.2
  14.1 3.7 %collective-permute-done.1 = f32[16,1024]{1,0:T(8,128)S(1)} collective-permute-done((f32[16,1024]{1,0:T(8,128)S(1)}, f32[16,1024]{1,0:T(8,128)S(1)}, u32[]{:S(2)}, u32[]{:S(2)}) %collective-permute-start.1) | collective-permute-done | bytes 65568 | tf_op jit(solution)/shard_map/ppermute | solution.py:22
  18.5 0.7 pad_maximum_fusion
  19.2 0.8 broadcast_in_dim.2
  20.1 8.5 %all-to-all-start = ((f32[8,16,1024]{2,1,0:T(8,128)}), f32[8,16,1024]{2,1,0:T(8,128)S(1)}, u32[]{:S(2)}, u32[]{:S(2)}) async-start(f32[8,16,1024]{2,1,0:T(8,128)} %broadcast_in_dim.2), calls=%async_computation | async-start | bytes 1048576 | tf_op jit(solution)/shard_map/all_to_all | solution.py:197
  29.3 15.2 %all-to-all-done.refs_0_ = f32[8,16,1024]{2,1,0:T(8,128)S(1)} async-done(((f32[8,16,1024]{2,1,0:T(8,128)}), f32[8,16,1024]{2,1,0:T(8,128)S(1)}, u32[]{:S(2)}, u32[]{:S(2)}) %all-to-all-start) | async-done | bytes 524320 | tf_op jit(solution)/shard_map/all_to_all | solution.py:197
  45.0 1.5 collective-permute-start.5
  46.5 9.9 %collective-permute-done.3.refs_1_ = f32[8,16,1024]{2,1,0:T(8,128)S(1)} collective-permute-done((f32[8,16,1024]{2,1,0:T(8,128)S(1)}, f32[8,16,1024]{2,1,0:T(8,128)S(1)}, u32[]{:S(2)}, u32[]{:S(2)}) %collective-permute-start.3) | collective-permute-done | bytes 524320 | tf_op jit(solution)/shard_map/ppermute | solution.py:22
  56.4 0.8 collective-permute-start.4
  57.2 1.4 collective-permute-start.6
  58.6 4.2 %collective-permute-done.4.refs_2_ = f32[4,16,1024]{2,1,0:T(8,128)S(1)} collective-permute-done((f32[4,16,1024]{2,1,0:T(8,128)S(1)}, f32[4,16,1024]{2,1,0:T(8,128)S(1)}, u32[]{:S(2)}, u32[]{:S(2)}) %collective-permute-start.4) | collective-permute-done | bytes 262176 | tf_op jit(solution)/shard_map/ppermute | solution.py:22
  62.8 2.0 collective-permute-done.6.refs_3_
  64.9 5.8 %collective-permute-done.7.refs_6_ = f32[1400,512]{1,0:T(8,128)S(1)} collective-permute-done((f32[1400,512]{1,0:T(8,128)}, f32[1400,512]{1,0:T(8,128)S(1)}, u32[]{:S(2)}, u32[]{:S(2)}) %collective-permute-start.7) | collective-permute-done | bytes 2867232 | tf_op jit(solution)/shard_map/ppermute | solution.py:26
  70.6 1.8 collective-permute-done.8.refs_8_
  73.0 1.3 slice.25
  74.3 1.1 collective-permute-start.12
  75.3 2.5 slice.26
  78.4 2.5 collective-permute-done.10.refs_9_
  81.0 4.7 %collective-permute-done.9.refs_7_ = f32[1400,512]{1,0:T(8,128)} collective-permute-done((f32[1400,512]{1,0:T(8,128)S(1)}, f32[1400,512]{1,0:T(8,128)}, u32[]{:S(2)}, u32[]{:S(2)}) %collective-permute-start.9) | collective-permute-done | bytes 2867232 | tf_op jit(solution)/shard_map/ppermute | solution.py:18
  85.6 11.4 %shard_map.28 = f32[512,632]{1,0:T(8,128)} custom-call(s32[2]{0:T(128)} %pad_add_fusion.place_ref, f32[8,16,1024]{2,1,0:T(8,128)} %copy-done.1, f32[8,16,1024]{2,1,0:T(8,128)} %copy-done.2, f32[4,16,1024]{2,1,0:T(8,128)} %copy-done.4, f32[4,16,1024]{2,1,0:T(8,128)} %copy-done.5, f32[8,16,1024]{2,1,0:T(8,128)} %copy-done.3, f32[8,4,16,1024]{3,2,1,0:T(8,128)} %bitcast.8, ...), custom_call_target="tpu_custom_call" | custom-call | flops 3976200192 | bytes 10665984 | tf_op jit(solution)/shard_map/pallas_call | solution.py:120
  97.0 11.3 %all-to-all-start.1 = ((f32[32,16,632]{2,1,0:T(8,128)}), f32[32,16,632]{2,1,0:T(8,128)S(1)}, u32[]{:S(2)}, u32[]{:S(2)}) async-start(f32[32,16,632]{2,1,0:T(8,128)} %bitcast.11), calls=%async_computation.1 | async-start | bytes 2621440 | tf_op jit(solution)/shard_map/all_to_all | solution.py:209
  108.3 3.8 %collective-permute-done.12.refs_8_ = f32[768,512]{1,0:T(8,128)} collective-permute-done((f32[768,512]{1,0:T(8,128)}, f32[768,512]{1,0:T(8,128)}, u32[]{:S(2)}, u32[]{:S(2)}) %collective-permute-start.12) | collective-permute-done | bytes 1572896 | tf_op jit(solution)/shard_map/ppermute | solution.py:30
  112.6 11.4 %shard_map.29.refs_12_ = f32[512,2168]{1,0:T(8,128)} custom-call(s32[2]{0:T(128)} %pad_add_fusion.place_ref, f32[8,16,1024]{2,1,0:T(8,128)} %copy-done.1, f32[8,16,1024]{2,1,0:T(8,128)} %copy-done.2, f32[4,16,1024]{2,1,0:T(8,128)} %copy-done.4, f32[4,16,1024]{2,1,0:T(8,128)} %copy-done.5, f32[8,16,1024]{2,1,0:T(8,128)} %copy-done.3, ...), custom_call_target="tpu_custom_call" | custom-call | flops 4831838208 | bytes 12058624 | tf_op jit(solution)/shard_map/pallas_call | solution.py:120
  124.0 1.1 copy-done.6
  125.1 17.6 %shard_map.30 = f32[512,2168]{1,0:T(8,128)} custom-call(s32[2]{0:T(128)} %pad_add_fusion.place_ref, f32[8,16,1024]{2,1,0:T(8,128)} %copy-done.1, f32[8,16,1024]{2,1,0:T(8,128)} %copy-done.2, f32[4,16,1024]{2,1,0:T(8,128)} %copy-done.4, f32[4,16,1024]{2,1,0:T(8,128)} %copy-done.5, f32[8,16,1024]{2,1,0:T(8,128)} %copy-done.3, ...), custom_call_target="tpu_custom_call", output_to_operand_aliasing={{}: (13, {})} | custom-call | flops 8808038400 | bytes 18530304 | tf_op jit(solution)/shard_map/pallas_call | solution.py:120
  142.8 113.5 %all_to_all.15.second_ref = f32[32,16,2168]{2,1,0:T(8,128)S(1)} all-to-all(f32[32,16,2168]{2,1,0:T(8,128)} %bitcast.7), channel_id=1, replica_groups=mesh['yl'=2,'x'=4,'z'=8,'yh'=2,'core'=2] {'x','z'}, dimensions={0} | all-to-all | bytes 8880128 | tf_op jit(solution)/shard_map/all_to_all | solution.py:209
  256.3 3.5 %shard_map.31 = f32[16,89600]{1,0:T(8,128)} custom-call(s32[1]{0:T(128)} %bitcast.5.at_ref, f32[32,16,632]{2,1,0:T(8,128)S(1)} %all-to-all-done.1.first_ref, f32[32,16,2168]{2,1,0:T(8,128)S(1)} %all_to_all.15.second_ref), custom_call_target="tpu_custom_call" | custom-call | bytes 11468800 | tf_op jit(solution)/shard_map/pallas_call | solution.py:162
  (34 shorter events, 4.3 us)
Async XLA Ops:
  6.5 64.1 %collective-permute-start.7 = (f32[1400,512]{1,0:T(8,128)}, f32[1400,512]{1,0:T(8,128)S(1)}, u32[]{:S(2)}, u32[]{:S(2)}) collective-permute-start(f32[1400,512]{1,0:T(8,128)} %bitcast.3.refs_6_), channel_id=1, source_target_pairs={{0,128},{128,0},{1,129},{129,1},{2,130},{130,2},{3,131},{131,3},{4... | collective-permute-start | bytes 8601608 | tf_op jit(solution)/shard_map/ppermute | solution.py:26
  7.3 65.1 %collective-permute-start.8 = (f32[1400,512]{1,0:T(8,128)}, f32[1400,512]{1,0:T(8,128)}, u32[]{:S(2)}, u32[]{:S(2)}) collective-permute-start(f32[1400,512]{1,0:T(8,128)} %bitcast.3.refs_6_), channel_id=1, source_target_pairs={{128,2},{2,128},{130,0},{0,130},{129,3},{3,129},{131,1},{1,131},{1... | collective-permute-start | bytes 8601608 | tf_op jit(solution)/shard_map/ppermute | solution.py:30
  9.4 4.8 %collective-permute-start = (f32[16,1024]{1,0:T(8,128)S(1)}, f32[16,1024]{1,0:T(8,128)S(1)}, u32[]{:S(2)}, u32[]{:S(2)}) collective-permute-start(f32[16,1024]{1,0:T(8,128)S(1)} %get-tuple-element.29), channel_id=1, source_target_pairs={{0,96},{32,0},{64,32},{96,64},{1,97},{33,1},{65,33},{97,65},{2,98}... | collective-permute-start | bytes 196616 | tf_op jit(solution)/shard_map/ppermute | solution.py:22
  12.1 5.8 %collective-permute-start.1 = (f32[16,1024]{1,0:T(8,128)S(1)}, f32[16,1024]{1,0:T(8,128)S(1)}, u32[]{:S(2)}, u32[]{:S(2)}) collective-permute-start(f32[16,1024]{1,0:T(8,128)S(1)} %get-tuple-element.29), channel_id=1, source_target_pairs={{0,64},{32,96},{64,0},{96,32},{1,65},{33,97},{65,1},{97,33},{2,66}... | collective-permute-start | bytes 196616 | tf_op jit(solution)/shard_map/ppermute | solution.py:22
  12.9 5.7 %collective-permute-start.2 = (f32[16,1024]{1,0:T(8,128)S(1)}, f32[16,1024]{1,0:T(8,128)S(1)}, u32[]{:S(2)}, u32[]{:S(2)}) collective-permute-start(f32[16,1024]{1,0:T(8,128)S(1)} %get-tuple-element.29), channel_id=1, source_target_pairs={{0,32},{32,64},{64,96},{96,0},{1,33},{33,65},{65,97},{97,1},{2,34}... | collective-permute-start | bytes 196616 | tf_op jit(solution)/shard_map/ppermute | solution.py:22
  20.1 24.4 %all-to-all-start = ((f32[8,16,1024]{2,1,0:T(8,128)}), f32[8,16,1024]{2,1,0:T(8,128)S(1)}, u32[]{:S(2)}, u32[]{:S(2)}) async-start(f32[8,16,1024]{2,1,0:T(8,128)} %broadcast_in_dim.2), calls=%async_computation | async-start | bytes 1048576 | tf_op jit(solution)/shard_map/all_to_all | solution.py:197
  28.6 49.9 %all-gather.3.cloned.1.call-start = ((), (), s32[]{:S(2)}) async-start(), calls=%async_computation.3 | async-start | bytes 2359296 | tf_op jit(solution)/shard_map/all_gather | solution.py:198
  44.5 33.3 %copy-start.1 = (f32[8,16,1024]{2,1,0:T(8,128)}, f32[8,16,1024]{2,1,0:T(8,128)S(1)}, u32[]{:S(2)}) copy-start(f32[8,16,1024]{2,1,0:T(8,128)S(1)} %all-to-all-done.refs_0_) | copy-start | bytes 1572868
  44.5 11.9 %collective-permute-start.3 = (f32[8,16,1024]{2,1,0:T(8,128)S(1)}, f32[8,16,1024]{2,1,0:T(8,128)S(1)}, u32[]{:S(2)}, u32[]{:S(2)}) collective-permute-start(f32[8,16,1024]{2,1,0:T(8,128)S(1)} %all-to-all-done.refs_0_), channel_id=1, source_target_pairs={{0,96},{32,0},{64,32},{96,64},{1,97},{33,1},{65,33},{97,65},{2,98}... | collective-permute-start | bytes 1572872 | tf_op jit(solution)/shard_map/ppermute | solution.py:22
  45.0 12.1 %collective-permute-start.5 = (f32[8,16,1024]{2,1,0:T(8,128)S(1)}, f32[8,16,1024]{2,1,0:T(8,128)S(1)}, u32[]{:S(2)}, u32[]{:S(2)}) collective-permute-start(f32[8,16,1024]{2,1,0:T(8,128)S(1)} %all-to-all-done.refs_0_), channel_id=1, source_target_pairs={{0,32},{32,64},{64,96},{96,0},{1,33},{33,65},{65,97},{97,1},{2,34}... | collective-permute-start | bytes 1572872 | tf_op jit(solution)/shard_map/ppermute | solution.py:22
  56.3 16.1 %copy-start.2 = (f32[8,16,1024]{2,1,0:T(8,128)}, f32[8,16,1024]{2,1,0:T(8,128)S(1)}, u32[]{:S(2)}) copy-start(f32[8,16,1024]{2,1,0:T(8,128)S(1)} %collective-permute-done.3.refs_1_) | copy-start | bytes 1572868
  56.4 6.4 %collective-permute-start.4 = (f32[4,16,1024]{2,1,0:T(8,128)S(1)}, f32[4,16,1024]{2,1,0:T(8,128)S(1)}, u32[]{:S(2)}, u32[]{:S(2)}) collective-permute-start(f32[4,16,1024]{2,1,0:T(8,128)S(1)} %slice.27), channel_id=1, source_target_pairs={{0,96},{32,0},{64,32},{96,64},{1,97},{33,1},{65,33},{97,65},{2,98}... | collective-permute-start | bytes 786440 | tf_op jit(solution)/shard_map/ppermute | solution.py:22
  57.2 15.2 %copy-start.3 = (f32[8,16,1024]{2,1,0:T(8,128)}, f32[8,16,1024]{2,1,0:T(8,128)S(1)}, u32[]{:S(2)}) copy-start(f32[8,16,1024]{2,1,0:T(8,128)S(1)} %collective-permute-done.5.refs_4_) | copy-start | bytes 1572868
  57.2 7.7 %collective-permute-start.6 = (f32[4,16,1024]{2,1,0:T(8,128)S(1)}, f32[4,16,1024]{2,1,0:T(8,128)S(1)}, u32[]{:S(2)}, u32[]{:S(2)}) collective-permute-start(f32[4,16,1024]{2,1,0:T(8,128)S(1)} %slice.28), channel_id=1, source_target_pairs={{0,32},{32,64},{64,96},{96,0},{1,33},{33,65},{65,97},{97,1},{2,34}... | collective-permute-start | bytes 786440 | tf_op jit(solution)/shard_map/ppermute | solution.py:22
  62.8 9.6 %copy-start.4 = (f32[4,16,1024]{2,1,0:T(8,128)}, f32[4,16,1024]{2,1,0:T(8,128)S(1)}, u32[]{:S(2)}) copy-start(f32[4,16,1024]{2,1,0:T(8,128)S(1)} %collective-permute-done.4.refs_2_) | copy-start | bytes 786436
  64.9 7.6 %copy-start.5 = (f32[4,16,1024]{2,1,0:T(8,128)}, f32[4,16,1024]{2,1,0:T(8,128)S(1)}, u32[]{:S(2)}) copy-start(f32[4,16,1024]{2,1,0:T(8,128)S(1)} %collective-permute-done.6.refs_3_) | copy-start | bytes 786436
  70.6 7.2 %copy-start = (f32[1400,512]{1,0:T(8,128)}, f32[1400,512]{1,0:T(8,128)S(1)}, u32[]{:S(2)}) copy-start(f32[1400,512]{1,0:T(8,128)S(1)} %collective-permute-done.7.refs_6_) | copy-start | bytes 8601604
  72.4 8.6 %collective-permute-start.10 = (f32[1400,512]{1,0:T(8,128)}, f32[1400,512]{1,0:T(8,128)}, u32[]{:S(2)}, u32[]{:S(2)}) collective-permute-start(f32[1400,512]{1,0:T(8,128)} %collective-permute-done.8.refs_8_), channel_id=1, source_target_pairs={{0,1},{1,0},{2,3},{3,2},{4,5},{5,4},{6,7},{7,6},{8,9},{9,8},{10,11... | collective-permute-start | bytes 8601608 | tf_op jit(solution)/shard_map/ppermute | solution.py:18
  72.4 13.2 %collective-permute-start.9 = (f32[1400,512]{1,0:T(8,128)S(1)}, f32[1400,512]{1,0:T(8,128)}, u32[]{:S(2)}, u32[]{:S(2)}) collective-permute-start(f32[1400,512]{1,0:T(8,128)S(1)} %collective-permute-done.7.refs_6_), channel_id=1, source_target_pairs={{0,1},{1,0},{2,3},{3,2},{4,5},{5,4},{6,7},{7,6},{8,9},{9,8},{10,11... | collective-permute-start | bytes 8601608 | tf_op jit(solution)/shard_map/ppermute | solution.py:18
  74.3 37.9 %collective-permute-start.12 = (f32[768,512]{1,0:T(8,128)}, f32[768,512]{1,0:T(8,128)}, u32[]{:S(2)}, u32[]{:S(2)}) collective-permute-start(f32[768,512]{1,0:T(8,128)} %slice.25), channel_id=1, source_target_pairs={{128,2},{2,128},{130,0},{0,130},{129,3},{3,129},{131,1},{1,131},{1... | collective-permute-start | bytes 4718600 | tf_op jit(solution)/shard_map/ppermute | solution.py:30
  75.3 48.7 %collective-permute-start.11 = (f32[1400,512]{1,0:T(8,128)}, f32[1400,512]{1,0:T(8,128)}, u32[]{:S(2)}, u32[]{:S(2)}) collective-permute-start(f32[1400,512]{1,0:T(8,128)} %bitcast.3.refs_6_), channel_id=1, source_target_pairs={{0,1},{1,0},{2,3},{3,2},{4,5},{5,4},{6,7},{7,6},{8,9},{9,8},{10,11... | collective-permute-start | bytes 8601608 | tf_op jit(solution)/shard_map/ppermute | solution.py:18
  77.8 34.3 %collective-permute-start.13 = (f32[632,512]{1,0:T(8,128)}, f32[632,512]{1,0:T(8,128)}, u32[]{:S(2)}, u32[]{:S(2)}) collective-permute-start(f32[632,512]{1,0:T(8,128)} %slice.26), channel_id=1, source_target_pairs={{0,128},{128,0},{1,129},{129,1},{2,130},{130,2},{3,131},{131,3},{4... | collective-permute-start | bytes 3883016 | tf_op jit(solution)/shard_map/ppermute | solution.py:26
  97.0 45.8 %all-to-all-start.1 = ((f32[32,16,632]{2,1,0:T(8,128)}), f32[32,16,632]{2,1,0:T(8,128)S(1)}, u32[]{:S(2)}, u32[]{:S(2)}) async-start(f32[32,16,632]{2,1,0:T(8,128)} %bitcast.11), calls=%async_computation.1 | async-start | bytes 2621440 | tf_op jit(solution)/shard_map/all_to_all | solution.py:209
  112.1 11.9 %collective-permute-start.14 = (f32[768,512]{1,0:T(8,128)}, f32[768,512]{1,0:T(8,128)}, u32[]{:S(2)}, u32[]{:S(2)}) collective-permute-start(f32[768,512]{1,0:T(8,128)} %collective-permute-done.12.refs_8_), channel_id=1, source_target_pairs={{0,1},{1,0},{2,3},{3,2},{4,5},{5,4},{6,7},{7,6},{8,9},{9,8},{10,11... | collective-permute-start | bytes 4718600 | tf_op jit(solution)/shard_map/ppermute | solution.py:18
  112.1 11.9 %collective-permute-start.15 = (f32[632,512]{1,0:T(8,128)}, f32[632,512]{1,0:T(8,128)S(1)}, u32[]{:S(2)}, u32[]{:S(2)}) collective-permute-start(f32[632,512]{1,0:T(8,128)} %collective-permute-done.13.refs_9_), channel_id=1, source_target_pairs={{0,1},{1,0},{2,3},{3,2},{4,5},{5,4},{6,7},{7,6},{8,9},{9,8},{10,11... | collective-permute-start | bytes 3883016 | tf_op jit(solution)/shard_map/ppermute | solution.py:18
  124.0 1.1 copy-start.6
Sparse Core Ops, SparseCore 0:
  31.2 40.8 all-gather.2

commit v7 on v6

--- a/solution.py
+++ b/solution.py
@@ -137,47 +137,40 @@
     )(place, *amplitudes, *[v for q in quarters for v in q], *([] if out is None else [out]))
 
 
-def place_kernel(at_ref, first_ref, second_ref, out_ref):
-    kept = out_ref.shape[1] // GROUP - first_ref.shape[2]
-    other = pl.program_id(1) == 0
-
-    @pl.when(other)
-    def _():
-        for s in range(GROUP):
-            start = s * (kept + first_ref.shape[2])
-            out_ref[:, start : start + kept] = second_ref[s, :, :kept]
-            out_ref[:, start + kept : start + kept + first_ref.shape[2]] = first_ref[s]
-
-    @pl.when(jnp.logical_not(other))
-    def _():
-        width = second_ref.shape[2] - kept
-        for s in range(GROUP):
-            out_ref[:, s * width : (s + 1) * width] = second_ref[s, :, kept:]
-
-
-def place(at, first, second):
-    sources, rows, _ = first.shape
-    width = (first.shape[2] + second.shape[2]) // 2
+def place_kernel(count, at_ref, *refs):
+    blocks, out_ref = refs[:count], refs[-1]
+    width = sum(ref.shape[2] for ref in blocks)
+    for s in range(GROUP):
+        start = s * width
+        for ref in blocks:
+            out_ref[:, start : start + ref.shape[2]] = ref[s]
+            start += ref.shape[2]
+
+
+def place(at, blocks, out=None):
+    sources, rows, _ = blocks[0].shape
+    width = sum(block.shape[2] for block in blocks)
     steps = sources // GROUP
+    count = len(blocks)
     return pl.pallas_call(
-        place_kernel,
+        functools.partial(place_kernel, count),
         grid_spec=pltpu.PrefetchScalarGridSpec(
             num_scalar_prefetch=1,
-            grid=(steps, 2),
+            grid=(steps,),
             in_specs=[
-                pl.BlockSpec((GROUP, rows, v.shape[2]), lambda g, i, at: (g, 0, 0))
-                for v in (first, second)
-            ],
-            out_specs=pl.BlockSpec(
-                (rows, GROUP * width), lambda g, i, at: (0, lax.rem(at[0] + 1 + i, 2) * steps + g)
-            ),
+                pl.BlockSpec((GROUP, rows, block.shape[2]), lambda g, at: (g, 0, 0))
+                for block in blocks
+            ]
+            + ([] if out is None else [pl.BlockSpec(memory_space=pl.ANY)]),
+            out_specs=pl.BlockSpec((rows, GROUP * width), lambda g, at: (0, at[0] * steps + g)),
         ),
         out_shape=jax.ShapeDtypeStruct((rows, 2 * sources * width), jnp.float32),
-        compiler_params=pltpu.CompilerParams(vmem_limit_bytes=24 << 20),
+        input_output_aliases={} if out is None else {1 + count: 0},
+        compiler_params=pltpu.CompilerParams(vmem_limit_bytes=16 << 20),
         cost_estimate=pl.CostEstimate(
-            flops=0, bytes_accessed=16 * sources * rows * width, transcendentals=0
-        ),
-    )(at, first, second)
+            flops=0, bytes_accessed=8 * sources * rows * width, transcendentals=0
+        ),
+    )(at, *blocks, *([] if out is None else [out]))
 
 
 def after(value, *others):
@@ -202,7 +195,6 @@
 
     own = integrals.T
     near, far = after((swap_near(own), swap_far(own)), low, high)
-    across = [swap_far(near[: CUT * TILE]), swap_near(far[CUT * TILE :])]
     pieces = [[near], [swap_core(near)], [far], [swap_core(far)]]
 
     def exchange(v):
@@ -211,13 +203,16 @@
         )
 
     first = product(spot, t, pieces, tiles=(CUT, pl.cdiv(columns, TILE)))
-    t = after(t, first)
-    second = product(spot, t, pieces, tiles=(0, CUT), columns=CUT * TILE + columns)
+    t, own, near, far = after((t, own, near, far), first)
+    across = [swap_far(near[: CUT * TILE]), swap_near(far[CUT * TILE :])]
+    second = product(spot, t, pieces, tiles=(0, CUT))
     first = exchange(first)
+    second = exchange(after(second, first))
     own2, across2 = swap_core(own), [swap_core(v) for v in across]
-    second = product(spot, t, [[own], [own2], across, across2], out=second)
-    first, second, at = lax.optimization_barrier((first, second, yl.reshape(1)))
-    return place(at, first, exchange(second))
+    own_block = product(spot, t, [[own], [own2], across, across2])
+    out = place((1 - yl).reshape(1), [second, first])
+    own_block, out, at = lax.optimization_barrier((own_block, out, yl.reshape(1)))
+    return place(at, [exchange(own_block)], out)
 
 
 def solution(mesh):

time: 268 us -> 269 us (level)
  blocking collectives: 113 us -> 73.2 us
  waiting for transfers between devices: 55.5 us -> 86 us
  starting transfers between devices: 32.5 us -> 41.3 us
    all_to_all x1, blocking collectives: 113 us -> 73.2 us  [exchange(): lax.all_to_all(v.reshape(-1, rows, v.shape[1]), ('x', 'z'), split_axis=0,...]
    all_to_all x1 -> x2, waiting for transfers between devices: 0.13 us -> 31.1 us  [exchange(): lax.all_to_all(v.reshape(-1, rows, v.shape[1]), ('x', 'z'), split_axis=0,...]
    ppermute x5, waiting for transfers between devices: 7.22 us -> 13.4 us  [swap_core(): return lax.ppermute(value, 'core', [(0, 1), (1, 0)])]
    ppermute x2, waiting for transfers between devices: 5.76 us -> 0.01 us  [swap_near(): return lax.ppermute(value, 'yl', [(0, 1), (1, 0)])]
    all_to_all x1 -> x2, starting transfers between devices: 11.3 us -> 16.7 us  [exchange(): lax.all_to_all(v.reshape(-1, rows, v.shape[1]), ('x', 'z'), split_axis=0,...]
    ppermute x7, waiting for transfers between devices: 20.9 us -> 16.4 us  [shift_x(): return lax.ppermute(value, 'x', [(i, (i + by) % 4) for i in range(4)])]
    ppermute x2, waiting for transfers between devices: 5.57 us -> 9.02 us  [swap_far(): return lax.ppermute(value, ('yl', 'yh'), [(2, 1), (1, 2), (3, 0), (0, 3)])]
    ppermute x7, starting transfers between devices: 8.57 us -> 11.6 us  [shift_x(): return lax.ppermute(value, 'x', [(i, (i + by) % 4) for i in range(4)])]
  transfers between devices with their start and end apart: 19 -> 20, of which waited for: 13 -> 13; matrix products, arithmetic and copies ran while one was open for 3% -> 3% of each run, Pallas kernels for 15% -> 11%
where the time goes in v7:
time: 269 us; the launch traced here: 268 us
  waiting for transfers between devices  86 us (32%)
  blocking collectives  73.2 us (27%)
  Pallas kernels  44.4 us (17%)
  starting transfers between devices  41.3 us (15%)
  between operations  13.5 us (5%)
  local copies, waits for them, and re-layouts  7.79 us (3%)
    all_to_all x1, blocking collectives, exchange(): lax.all_to_all(v.reshape(-1, rows, v.shape[1]), ('x', 'z'), split_axis=0,...  73.2 us
    pallas_call x3, Pallas kernels, product(): pl.pallas_call(functools.partial(product_kernel, counts, lo), grid_spec=p...  40.4 us
    all_to_all x2, waiting for transfers between devices, exchange(): lax.all_to_all(v.reshape(-1, rows, v.shape[1]), ('x', 'z'), split_axis=0,...  31.1 us
    all_to_all x2, starting transfers between devices, exchange(): lax.all_to_all(v.reshape(-1, rows, v.shape[1]), ('x', 'z'), split_axis=0,...  16.7 us
    ppermute x7, waiting for transfers between devices, shift_x(): return lax.ppermute(value, 'x', [(i, (i + by) % 4) for i in range(4)])  16.4 us
    all_to_all x1, waiting for transfers between devices, on_device(): here = lax.all_to_all(here, 'z', split_axis=0, concat_axis=0, tiled=True)  15.5 us
    ppermute x5, waiting for transfers between devices, swap_core(): return lax.ppermute(value, 'core', [(0, 1), (1, 0)])  13.4 us
    ppermute x7, starting transfers between devices, shift_x(): return lax.ppermute(value, 'x', [(i, (i + by) % 4) for i in range(4)])  11.6 us
  transfers between devices with their start and end apart: 20, of which 13 were waited for; matrix products, arithmetic and copies ran while one was open for 3% of the time, Pallas kernels for 11%

profile of v7, /device:TPU:24, one launch (start us, length us, event | category | flops | bytes accessed | tf_op | source)
XLA Modules:
  0.0 267.9 jit_solution(8929638504952755848)
XLA Ops:
  6.5 2.0 collective-permute-start.8
  8.5 0.9 fusion
  10.2 2.7 %collective-permute-start.1 = (f32[16,1024]{1,0:T(8,128)S(1)}, f32[16,1024]{1,0:T(8,128)S(1)}, u32[]{:S(2)}, u32[]{:S(2)}) collective-permute-start(f32[16,1024]{1,0:T(8,128)S(1)} %get-tuple-element.37), channel_id=1, source_target_pairs={{0,64},{32,96},{64,0},{96,32},{1,65},{33,97},{65,1},{97,33},{2,66}... | collective-permute-start | bytes 196616 | tf_op jit(solution)/shard_map/ppermute | solution.py:22
  12.9 1.4 collective-permute-start
  14.9 1.0 collective-permute-done.1
  16.0 1.2 collective-permute-done
  17.9 0.8 broadcast_in_dim.2
  18.7 8.5 %all-to-all-start = ((f32[8,16,1024]{2,1,0:T(8,128)}), f32[8,16,1024]{2,1,0:T(8,128)S(1)}, u32[]{:S(2)}, u32[]{:S(2)}) async-start(f32[8,16,1024]{2,1,0:T(8,128)} %broadcast_in_dim.2), calls=%async_computation | async-start | bytes 1048576 | tf_op jit(solution)/shard_map/all_to_all | solution.py:190
  27.9 15.5 %all-to-all-done.refs_0_ = f32[8,16,1024]{2,1,0:T(8,128)S(1)} async-done(((f32[8,16,1024]{2,1,0:T(8,128)}), f32[8,16,1024]{2,1,0:T(8,128)S(1)}, u32[]{:S(2)}, u32[]{:S(2)}) %all-to-all-start) | async-done | bytes 524320 | tf_op jit(solution)/shard_map/all_to_all | solution.py:190
  43.4 3.2 %collective-permute-start.3 = (f32[8,16,1024]{2,1,0:T(8,128)S(1)}, f32[8,16,1024]{2,1,0:T(8,128)S(1)}, u32[]{:S(2)}, u32[]{:S(2)}) collective-permute-start(f32[8,16,1024]{2,1,0:T(8,128)S(1)} %all-to-all-done.refs_0_), channel_id=1, source_target_pairs={{0,96},{32,0},{64,32},{96,64},{1,97},{33,1},{65,33},{97,65},{2,98}... | collective-permute-start | bytes 1572872 | tf_op jit(solution)/shard_map/ppermute | solution.py:22
  46.7 9.3 %collective-permute-done.5.refs_4_ = f32[8,16,1024]{2,1,0:T(8,128)S(1)} collective-permute-done((f32[8,16,1024]{2,1,0:T(8,128)S(1)}, f32[8,16,1024]{2,1,0:T(8,128)S(1)}, u32[]{:S(2)}, u32[]{:S(2)}) %collective-permute-start.5) | collective-permute-done | bytes 524320 | tf_op jit(solution)/shard_map/ppermute | solution.py:22
  56.1 3.3 %collective-permute-start.4 = (f32[4,16,1024]{2,1,0:T(8,128)S(1)}, f32[4,16,1024]{2,1,0:T(8,128)S(1)}, u32[]{:S(2)}, u32[]{:S(2)}) collective-permute-start(f32[4,16,1024]{2,1,0:T(8,128)S(1)} %slice.27), channel_id=1, source_target_pairs={{0,96},{32,0},{64,32},{96,64},{1,97},{33,1},{65,33},{97,65},{2,98}... | collective-permute-start | bytes 786440 | tf_op jit(solution)/shard_map/ppermute | solution.py:22
  59.4 4.2 %collective-permute-done.6.refs_3_ = f32[4,16,1024]{2,1,0:T(8,128)S(1)} collective-permute-done((f32[4,16,1024]{2,1,0:T(8,128)S(1)}, f32[4,16,1024]{2,1,0:T(8,128)S(1)}, u32[]{:S(2)}, u32[]{:S(2)}) %collective-permute-start.6) | collective-permute-done | bytes 262176 | tf_op jit(solution)/shard_map/ppermute | solution.py:22
  63.6 8.3 %collective-permute-done.8.refs_8_ = f32[1400,512]{1,0:T(8,128)} collective-permute-done((f32[1400,512]{1,0:T(8,128)}, f32[1400,512]{1,0:T(8,128)}, u32[]{:S(2)}, u32[]{:S(2)}) %collective-permute-start.8) | collective-permute-done | bytes 2867232 | tf_op jit(solution)/shard_map/ppermute | solution.py:30
  72.5 0.9 pad_add_fusion.place_ref
  73.5 6.9 %collective-permute-done.9.refs_7_ = f32[1400,512]{1,0:T(8,128)} collective-permute-done((f32[1400,512]{1,0:T(8,128)S(1)}, f32[1400,512]{1,0:T(8,128)}, u32[]{:S(2)}, u32[]{:S(2)}) %collective-permute-start.9) | collective-permute-done | bytes 2867232 | tf_op jit(solution)/shard_map/ppermute | solution.py:18
  80.4 1.3 collective-permute-done.10.refs_9_
  81.7 11.4 %shard_map.28 = f32[512,632]{1,0:T(8,128)} custom-call(s32[2]{0:T(128)} %pad_add_fusion.place_ref, f32[8,16,1024]{2,1,0:T(8,128)} %copy-done.2, f32[8,16,1024]{2,1,0:T(8,128)} %copy-done.4, f32[4,16,1024]{2,1,0:T(8,128)} %copy-done.6, f32[4,16,1024]{2,1,0:T(8,128)} %copy-done.5, f32[8,16,1024]{2,1,0:T(8,128)} %copy-done.3, f32[8,4,16,1024]{3,2,1,0:T(8,128)} %bitcast.11, ...), custom_call_target="tpu_custom_call" | custom-call | flops 3976200192 | bytes 10665984 | tf_op jit(solution)/shard_map/pallas_call | solution.py:120
  93.1 11.3 %all-to-all-start.1 = ((f32[32,16,632]{2,1,0:T(8,128)}), f32[32,16,632]{2,1,0:T(8,128)S(1)}, u32[]{:S(2)}, u32[]{:S(2)}) async-start(f32[32,16,632]{2,1,0:T(8,128)} %bitcast.9), calls=%async_computation.1 | async-start | bytes 2621440 | tf_op jit(solution)/shard_map/all_to_all | solution.py:201
  104.4 2.7 %slice.25 = f32[768,512]{1,0:T(8,128)} slice(f32[1400,512]{1,0:T(8,128)} %copy-done), slice={[0:768], [0:512]} | slice | bytes 3145728 | tf_op jit(solution)/shard_map/slice | solution.py:207
  107.1 1.5 collective-permute-start.12
  108.6 2.5 slice.26
  111.1 11.4 %shard_map.30 = f32[512,768]{1,0:T(8,128)} custom-call(s32[2]{0:T(128)} %pad_add_fusion.place_ref, f32[8,16,1024]{2,1,0:T(8,128)} %copy-done.2, f32[8,16,1024]{2,1,0:T(8,128)} %copy-done.4, f32[4,16,1024]{2,1,0:T(8,128)} %copy-done.6, f32[4,16,1024]{2,1,0:T(8,128)} %copy-done.5, f32[8,16,1024]{2,1,0:T(8,128)} %copy-done.3, f32[8,4,16,1024]{3,2,1,0:T(8,128)} %bitcast.12, ...), custom_call_target="tpu_custom_call" | custom-call | flops 4831838208 | bytes 12058624 | tf_op jit(solution)/shard_map/pallas_call | solution.py:120
  122.6 16.1 %all-to-all-done.1.refs_1_ = f32[32,16,632]{2,1,0:T(8,128)S(1)} async-done(((f32[32,16,632]{2,1,0:T(8,128)}), f32[32,16,632]{2,1,0:T(8,128)S(1)}, u32[]{:S(2)}, u32[]{:S(2)}) %all-to-all-start.1) | async-done | bytes 1294368 | tf_op jit(solution)/shard_map/all_to_all | solution.py:201
  138.7 5.4 %all-to-all-start.2 = ((f32[32,16,768]{2,1,0:T(8,128)}), f32[32,16,768]{2,1,0:T(8,128)S(1)}, u32[]{:S(2)}, u32[]{:S(2)}) async-start(f32[32,16,768]{2,1,0:T(8,128)} %bitcast.14), calls=%async_computation.2 | async-start | bytes 3145728 | tf_op jit(solution)/shard_map/all_to_all | solution.py:201
  145.3 5.1 %collective-permute-done.15.refs_11_ = f32[632,512]{1,0:T(8,128)} collective-permute-done((f32[632,512]{1,0:T(8,128)}, f32[632,512]{1,0:T(8,128)}, u32[]{:S(2)}, u32[]{:S(2)}) %collective-permute-start.15) | collective-permute-done | bytes 1294368 | tf_op jit(solution)/shard_map/ppermute | solution.py:18
  150.4 17.6 %shard_map.29 = f32[512,1400]{1,0:T(8,128)} custom-call(s32[2]{0:T(128)} %pad_add_fusion.place_ref, f32[8,16,1024]{2,1,0:T(8,128)} %copy-done.2, f32[8,16,1024]{2,1,0:T(8,128)} %copy-done.4, f32[4,16,1024]{2,1,0:T(8,128)} %copy-done.6, f32[4,16,1024]{2,1,0:T(8,128)} %copy-done.5, f32[8,16,1024]{2,1,0:T(8,128)} %copy-done.3, f32[8,4,16,1024]{3,2,1,0:T(8,128)} %bitcast.13, ...), custom_call_target="tpu_custom_call" | custom-call | flops 8808038400 | bytes 18530304 | tf_op jit(solution)/shard_map/pallas_call | solution.py:120
  168.0 14.9 %all-to-all-done.2.refs_0_ = f32[32,16,768]{2,1,0:T(8,128)S(1)} async-done(((f32[32,16,768]{2,1,0:T(8,128)}), f32[32,16,768]{2,1,0:T(8,128)S(1)}, u32[]{:S(2)}, u32[]{:S(2)}) %all-to-all-start.2) | async-done | bytes 1572896 | tf_op jit(solution)/shard_map/all_to_all | solution.py:201
  183.0 2.0 shard_map.31.refs_1_
  185.0 0.9 copy-done.1
  185.8 73.2 %all_to_all.20.refs_0_ = f32[32,16,1400]{2,1,0:T(8,128)S(1)} all-to-all(f32[32,16,1400]{2,1,0:T(8,128)S(1)} %bitcast.10), channel_id=1, replica_groups=mesh['yl'=2,'x'=4,'z'=8,'yh'=2,'core'=2] {'x','z'}, dimensions={0} | all-to-all | bytes 5734400 | tf_op jit(solution)/shard_map/all_to_all | solution.py:201
  259.0 2.0 shard_map.32
  (37 shorter events, 4.8 us)
Async XLA Ops:
  6.5 65.4 %collective-permute-start.8 = (f32[1400,512]{1,0:T(8,128)}, f32[1400,512]{1,0:T(8,128)}, u32[]{:S(2)}, u32[]{:S(2)}) collective-permute-start(f32[1400,512]{1,0:T(8,128)} %bitcast.3.refs_6_), channel_id=1, source_target_pairs={{128,2},{2,128},{130,0},{0,130},{129,3},{3,129},{131,1},{1,131},{1... | collective-permute-start | bytes 8601608 | tf_op jit(solution)/shard_map/ppermute | solution.py:30
  8.5 63.4 %collective-permute-start.7 = (f32[1400,512]{1,0:T(8,128)}, f32[1400,512]{1,0:T(8,128)S(1)}, u32[]{:S(2)}, u32[]{:S(2)}) collective-permute-start(f32[1400,512]{1,0:T(8,128)} %bitcast.3.refs_6_), channel_id=1, source_target_pairs={{0,128},{128,0},{1,129},{129,1},{2,130},{130,2},{3,131},{131,3},{4... | collective-permute-start | bytes 8601608 | tf_op jit(solution)/shard_map/ppermute | solution.py:26
  9.4 5.6 %collective-permute-start.2 = (f32[16,1024]{1,0:T(8,128)S(1)}, f32[16,1024]{1,0:T(8,128)S(1)}, u32[]{:S(2)}, u32[]{:S(2)}) collective-permute-start(f32[16,1024]{1,0:T(8,128)S(1)} %get-tuple-element.37), channel_id=1, source_target_pairs={{0,32},{32,64},{64,96},{96,0},{1,33},{33,65},{65,97},{97,1},{2,34}... | collective-permute-start | bytes 196616 | tf_op jit(solution)/shard_map/ppermute | solution.py:22
  10.2 5.8 %collective-permute-start.1 = (f32[16,1024]{1,0:T(8,128)S(1)}, f32[16,1024]{1,0:T(8,128)S(1)}, u32[]{:S(2)}, u32[]{:S(2)}) collective-permute-start(f32[16,1024]{1,0:T(8,128)S(1)} %get-tuple-element.37), channel_id=1, source_target_pairs={{0,64},{32,96},{64,0},{96,32},{1,65},{33,97},{65,1},{97,33},{2,66}... | collective-permute-start | bytes 196616 | tf_op jit(solution)/shard_map/ppermute | solution.py:22
  12.9 4.3 %collective-permute-start = (f32[16,1024]{1,0:T(8,128)S(1)}, f32[16,1024]{1,0:T(8,128)S(1)}, u32[]{:S(2)}, u32[]{:S(2)}) collective-permute-start(f32[16,1024]{1,0:T(8,128)S(1)} %get-tuple-element.37), channel_id=1, source_target_pairs={{0,96},{32,0},{64,32},{96,64},{1,97},{33,1},{65,33},{97,65},{2,98}... | collective-permute-start | bytes 196616 | tf_op jit(solution)/shard_map/ppermute | solution.py:22
  18.7 24.7 %all-to-all-start = ((f32[8,16,1024]{2,1,0:T(8,128)}), f32[8,16,1024]{2,1,0:T(8,128)S(1)}, u32[]{:S(2)}, u32[]{:S(2)}) async-start(f32[8,16,1024]{2,1,0:T(8,128)} %broadcast_in_dim.2), calls=%async_computation | async-start | bytes 1048576 | tf_op jit(solution)/shard_map/all_to_all | solution.py:190
  27.2 46.3 %all-gather.3.cloned.1.call-start = ((), (), s32[]{:S(2)}) async-start(), calls=%async_computation.4 | async-start | bytes 2359296 | tf_op jit(solution)/shard_map/all_gather | solution.py:191
  43.4 38.3 %copy-start.2 = (f32[8,16,1024]{2,1,0:T(8,128)}, f32[8,16,1024]{2,1,0:T(8,128)S(1)}, u32[]{:S(2)}) copy-start(f32[8,16,1024]{2,1,0:T(8,128)S(1)} %all-to-all-done.refs_0_) | copy-start | bytes 1572868
  43.4 12.5 %collective-permute-start.5 = (f32[8,16,1024]{2,1,0:T(8,128)S(1)}, f32[8,16,1024]{2,1,0:T(8,128)S(1)}, u32[]{:S(2)}, u32[]{:S(2)}) collective-permute-start(f32[8,16,1024]{2,1,0:T(8,128)S(1)} %all-to-all-done.refs_0_), channel_id=1, source_target_pairs={{0,32},{32,64},{64,96},{96,0},{1,33},{33,65},{65,97},{97,1},{2,34}... | collective-permute-start | bytes 1572872 | tf_op jit(solution)/shard_map/ppermute | solution.py:22
  43.4 12.6 %collective-permute-start.3 = (f32[8,16,1024]{2,1,0:T(8,128)S(1)}, f32[8,16,1024]{2,1,0:T(8,128)S(1)}, u32[]{:S(2)}, u32[]{:S(2)}) collective-permute-start(f32[8,16,1024]{2,1,0:T(8,128)S(1)} %all-to-all-done.refs_0_), channel_id=1, source_target_pairs={{0,96},{32,0},{64,32},{96,64},{1,97},{33,1},{65,33},{97,65},{2,98}... | collective-permute-start | bytes 1572872 | tf_op jit(solution)/shard_map/ppermute | solution.py:22
  55.9 16.0 %copy-start.3 = (f32[8,16,1024]{2,1,0:T(8,128)}, f32[8,16,1024]{2,1,0:T(8,128)S(1)}, u32[]{:S(2)}) copy-start(f32[8,16,1024]{2,1,0:T(8,128)S(1)} %collective-permute-done.5.refs_4_) | copy-start | bytes 1572868
  56.0 7.7 %collective-permute-start.6 = (f32[4,16,1024]{2,1,0:T(8,128)S(1)}, f32[4,16,1024]{2,1,0:T(8,128)S(1)}, u32[]{:S(2)}, u32[]{:S(2)}) collective-permute-start(f32[4,16,1024]{2,1,0:T(8,128)S(1)} %slice.28), channel_id=1, source_target_pairs={{0,32},{32,64},{64,96},{96,0},{1,33},{33,65},{65,97},{97,1},{2,34}... | collective-permute-start | bytes 786440 | tf_op jit(solution)/shard_map/ppermute | solution.py:22
  56.1 16.0 %copy-start.4 = (f32[8,16,1024]{2,1,0:T(8,128)}, f32[8,16,1024]{2,1,0:T(8,128)S(1)}, u32[]{:S(2)}) copy-start(f32[8,16,1024]{2,1,0:T(8,128)S(1)} %collective-permute-done.3.refs_1_) | copy-start | bytes 1572868
  56.1 7.5 %collective-permute-start.4 = (f32[4,16,1024]{2,1,0:T(8,128)S(1)}, f32[4,16,1024]{2,1,0:T(8,128)S(1)}, u32[]{:S(2)}, u32[]{:S(2)}) collective-permute-start(f32[4,16,1024]{2,1,0:T(8,128)S(1)} %slice.27), channel_id=1, source_target_pairs={{0,96},{32,0},{64,32},{96,64},{1,97},{33,1},{65,33},{97,65},{2,98}... | collective-permute-start | bytes 786440 | tf_op jit(solution)/shard_map/ppermute | solution.py:22
  63.6 8.9 %copy-start.5 = (f32[4,16,1024]{2,1,0:T(8,128)}, f32[4,16,1024]{2,1,0:T(8,128)S(1)}, u32[]{:S(2)}) copy-start(f32[4,16,1024]{2,1,0:T(8,128)S(1)} %collective-permute-done.6.refs_3_) | copy-start | bytes 786436
  63.6 8.9 %copy-start.6 = (f32[4,16,1024]{2,1,0:T(8,128)}, f32[4,16,1024]{2,1,0:T(8,128)S(1)}, u32[]{:S(2)}) copy-start(f32[4,16,1024]{2,1,0:T(8,128)S(1)} %collective-permute-done.4.refs_2_) | copy-start | bytes 786436
  71.9 9.8 %copy-start = (f32[1400,512]{1,0:T(8,128)}, f32[1400,512]{1,0:T(8,128)S(1)}, u32[]{:S(2)}) copy-start(f32[1400,512]{1,0:T(8,128)S(1)} %collective-permute-done.7.refs_6_) | copy-start | bytes 8601604
  71.9 8.5 %collective-permute-start.9 = (f32[1400,512]{1,0:T(8,128)S(1)}, f32[1400,512]{1,0:T(8,128)}, u32[]{:S(2)}, u32[]{:S(2)}) collective-permute-start(f32[1400,512]{1,0:T(8,128)S(1)} %collective-permute-done.7.refs_6_), channel_id=1, source_target_pairs={{0,1},{1,0},{2,3},{3,2},{4,5},{5,4},{6,7},{7,6},{8,9},{9,8},{10,11... | collective-permute-start | bytes 8601608 | tf_op jit(solution)/shard_map/ppermute | solution.py:18
  72.1 9.7 %collective-permute-start.10 = (f32[1400,512]{1,0:T(8,128)}, f32[1400,512]{1,0:T(8,128)}, u32[]{:S(2)}, u32[]{:S(2)}) collective-permute-start(f32[1400,512]{1,0:T(8,128)} %collective-permute-done.8.refs_8_), channel_id=1, source_target_pairs={{0,1},{1,0},{2,3},{3,2},{4,5},{5,4},{6,7},{7,6},{8,9},{9,8},{10,11... | collective-permute-start | bytes 8601608 | tf_op jit(solution)/shard_map/ppermute | solution.py:18
  93.1 45.6 %all-to-all-start.1 = ((f32[32,16,632]{2,1,0:T(8,128)}), f32[32,16,632]{2,1,0:T(8,128)S(1)}, u32[]{:S(2)}, u32[]{:S(2)}) async-start(f32[32,16,632]{2,1,0:T(8,128)} %bitcast.9), calls=%async_computation.1 | async-start | bytes 2621440 | tf_op jit(solution)/shard_map/all_to_all | solution.py:201
  107.1 37.7 %collective-permute-start.12 = (f32[768,512]{1,0:T(8,128)}, f32[768,512]{1,0:T(8,128)}, u32[]{:S(2)}, u32[]{:S(2)}) collective-permute-start(f32[768,512]{1,0:T(8,128)} %slice.25), channel_id=1, source_target_pairs={{128,2},{2,128},{130,0},{0,130},{129,3},{3,129},{131,1},{1,131},{1... | collective-permute-start | bytes 4718600 | tf_op jit(solution)/shard_map/ppermute | solution.py:30
  108.6 41.7 %collective-permute-start.11 = (f32[1400,512]{1,0:T(8,128)}, f32[1400,512]{1,0:T(8,128)}, u32[]{:S(2)}, u32[]{:S(2)}) collective-permute-start(f32[1400,512]{1,0:T(8,128)} %bitcast.3.refs_6_), channel_id=1, source_target_pairs={{0,1},{1,0},{2,3},{3,2},{4,5},{5,4},{6,7},{7,6},{8,9},{9,8},{10,11... | collective-permute-start | bytes 8601608 | tf_op jit(solution)/shard_map/ppermute | solution.py:18
  111.1 33.7 %collective-permute-start.13 = (f32[632,512]{1,0:T(8,128)}, f32[632,512]{1,0:T(8,128)}, u32[]{:S(2)}, u32[]{:S(2)}) collective-permute-start(f32[632,512]{1,0:T(8,128)} %slice.26), channel_id=1, source_target_pairs={{0,128},{128,0},{1,129},{129,1},{2,130},{130,2},{3,131},{131,3},{4... | collective-permute-start | bytes 3883016 | tf_op jit(solution)/shard_map/ppermute | solution.py:26
  138.7 44.3 %all-to-all-start.2 = ((f32[32,16,768]{2,1,0:T(8,128)}), f32[32,16,768]{2,1,0:T(8,128)S(1)}, u32[]{:S(2)}, u32[]{:S(2)}) async-start(f32[32,16,768]{2,1,0:T(8,128)} %bitcast.14), calls=%async_computation.2 | async-start | bytes 3145728 | tf_op jit(solution)/shard_map/all_to_all | solution.py:201
  144.8 5.6 %collective-permute-start.14 = (f32[768,512]{1,0:T(8,128)}, f32[768,512]{1,0:T(8,128)}, u32[]{:S(2)}, u32[]{:S(2)}) collective-permute-start(f32[768,512]{1,0:T(8,128)} %collective-permute-done.12.refs_8_), channel_id=1, source_target_pairs={{0,1},{1,0},{2,3},{3,2},{4,5},{5,4},{6,7},{7,6},{8,9},{9,8},{10,11... | collective-permute-start | bytes 4718600 | tf_op jit(solution)/shard_map/ppermute | solution.py:18
  144.8 5.6 %collective-permute-start.15 = (f32[632,512]{1,0:T(8,128)}, f32[632,512]{1,0:T(8,128)}, u32[]{:S(2)}, u32[]{:S(2)}) collective-permute-start(f32[632,512]{1,0:T(8,128)} %collective-permute-done.13.refs_9_), channel_id=1, source_target_pairs={{0,1},{1,0},{2,3},{3,2},{4,5},{5,4},{6,7},{7,6},{8,9},{9,8},{10,11... | collective-permute-start | bytes 3883016 | tf_op jit(solution)/shard_map/ppermute | solution.py:18
  183.0 2.9 %copy-start.1 = (f32[512,1400]{1,0:T(8,128)S(1)}, f32[512,1400]{1,0:T(8,128)}, u32[]{:S(2)}) copy-start(f32[512,1400]{1,0:T(8,128)} %shard_map.29) | copy-start | bytes 8601604
Sparse Core Ops, SparseCore 0:
  29.8 43.0 all-gather.2

commit v8 on v3

--- a/solution.py
+++ b/solution.py
@@ -11,7 +11,7 @@
 AXES = ("yl", "x", "z", "yh", "core")
 TILE = 256
 CUT = 768
-ORDER = (1, 7, 3, 5, 2, 6, 4)
+ORDER = (3, 5, 1, 7, 2, 6, 4)
 GROUP = 16
 
 
@@ -257,21 +257,20 @@
 
     turns = [shift_x(amplitudes[:, half:], -d) for d in (1, 2, 3)]
     last = jnp.concatenate([amplitudes[:, half:]] + turns)
-    here = jnp.broadcast_to(after(amplitudes[:, :half], turns[2])[None], (8, rows, half))
+    here = jnp.broadcast_to(after(amplitudes[:, :half], last)[None], (8, rows, half))
     here = lax.all_to_all(here, "z", split_axis=0, concat_axis=0, tiled=True)
-    here = after(here, last)
+    own2 = swap_core(integrals.T)
+    here = after(here, own2)
     last = lax.all_gather(last, "z", axis=0).reshape(8, 4, rows, half)
     ahead, behind = shift_x(here, -1), shift_x(here, 1)
     low, high = shift_x(ahead[:4], -1), shift_x(behind[4:], 1)
     t = (here, ahead, low, high, behind, last)
 
-    own = after(integrals.T, *turns)
-    near, far = swap_near(own), swap_far(own)
-    near, far = after((near, far), low, high)
+    own = integrals.T
+    near, far = after((swap_near(own), swap_far(own)), low, high)
     across = [swap_far(near[:CUT]), swap_near(far[CUT:])]
     results = product(spot, t, [[near], [swap_core(near)], [far], [swap_core(far)]], around=True)
     sent = {e: shift_z(results[e], e) for e in ORDER}
-    own2 = swap_core(after(own, here))
     across = after(across, sent[3], sent[5])
     across2 = [swap_core(v) for v in across]
     t = after(t, sent[3], sent[5])

time: 281 us -> 274 us (0.975)
  waiting for transfers between devices: 141 us -> 132 us
    ppermute x10, waiting for transfers between devices: 73.9 us -> 67.4 us  [shift_x(): return lax.ppermute(value, 'x', [(i, (i + by) % 4) for i in range(4)])]
  transfers between devices with their start and end apart: 29 -> 29, of which waited for: 17 -> 14; matrix products, arithmetic and copies ran while one was open for 2% -> 2% of each run, Pallas kernels for 15% -> 15%
where the time goes in v8:
time: 274 us; the launch traced here: 272 us
  waiting for transfers between devices  132 us (48%)
  starting transfers between devices  62.1 us (23%)
  Pallas kernels  43 us (16%)
  local copies, waits for them, and re-layouts  19.5 us (7%)
  between operations  13.6 us (5%)
    ppermute x10, waiting for transfers between devices, shift_x(): return lax.ppermute(value, 'x', [(i, (i + by) % 4) for i in range(4)])  67.4 us
    pallas_call x2, Pallas kernels, product(): pl.pallas_call(functools.partial(product_kernel, around, counts), grid_sp...  35.1 us
    ppermute x7, waiting for transfers between devices, shift_z(): return lax.ppermute(value, 'z', [(i, (i + by) % 8) for i in range(8)])  25.9 us
    ppermute x7, starting transfers between devices, shift_z(): return lax.ppermute(value, 'z', [(i, (i + by) % 8) for i in range(8)])  21.4 us
    ppermute x10, starting transfers between devices, shift_x(): return lax.ppermute(value, 'x', [(i, (i + by) % 4) for i in range(4)])  17.7 us
    all_to_all x1, waiting for transfers between devices, on_device(): here = lax.all_to_all(here, 'z', split_axis=0, concat_axis=0, tiled=True)  15.4 us
    unnamed x48, local copies, waits for them, and re-layouts  14.8 us
    ppermute x2, waiting for transfers between devices, swap_near(): return lax.ppermute(value, 'yl', [(0, 1), (1, 0)])  13.1 us
  transfers between devices with their start and end apart: 29, of which 14 were waited for; matrix products, arithmetic and copies ran while one was open for 2% of the time, Pallas kernels for 15%

profile of v8, /device:TPU:24, one launch (start us, length us, event | category | flops | bytes accessed | tf_op | source)
XLA Modules:
  0.0 271.8 jit_solution(8400019251217314556)
XLA Ops:
  10.8 2.7 %collective-permute-start.1 = (f32[16,1024]{1,0:T(8,128)S(1)}, f32[16,1024]{1,0:T(8,128)S(1)}, u32[]{:S(2)}, u32[]{:S(2)}) collective-permute-start(f32[16,1024]{1,0:T(8,128)S(1)} %get-tuple-element.55), channel_id=1, source_target_pairs={{0,64},{32,96},{64,0},{96,32},{1,65},{33,97},{65,1},{97,33},{2,66}... | collective-permute-start | bytes 196616 | tf_op jit(solution)/shard_map/ppermute | solution.py:23
  13.5 1.9 collective-permute-done.2
  16.8 2.9 %collective-permute-done = f32[16,1024]{1,0:T(8,128)S(1)} collective-permute-done((f32[16,1024]{1,0:T(8,128)S(1)}, f32[16,1024]{1,0:T(8,128)S(1)}, u32[]{:S(2)}, u32[]{:S(2)}) %collective-permute-start) | collective-permute-done | bytes 65568 | tf_op jit(solution)/shard_map/ppermute | solution.py:23
  21.3 7.8 %all-to-all-start = ((f32[8,16,1024]{2,1,0:T(8,128)}), f32[8,16,1024]{2,1,0:T(8,128)S(1)}, u32[]{:S(2)}, u32[]{:S(2)}) async-start(f32[8,16,1024]{2,1,0:T(8,128)} %broadcast_in_dim.2), calls=%async_computation | async-start | bytes 1048576 | tf_op jit(solution)/shard_map/all_to_all | solution.py:261
  29.8 15.4 %all-to-all-done.refs_0_ = f32[8,16,1024]{2,1,0:T(8,128)S(1)} async-done(((f32[8,16,1024]{2,1,0:T(8,128)}), f32[8,16,1024]{2,1,0:T(8,128)S(1)}, u32[]{:S(2)}, u32[]{:S(2)}) %all-to-all-start) | async-done | bytes 524320 | tf_op jit(solution)/shard_map/all_to_all | solution.py:261
  45.2 2.8 %collective-permute-start.4 = (f32[8,16,1024]{2,1,0:T(8,128)S(1)}, f32[8,16,1024]{2,1,0:T(8,128)S(1)}, u32[]{:S(2)}, u32[]{:S(2)}) collective-permute-start(f32[8,16,1024]{2,1,0:T(8,128)S(1)} %all-to-all-done.refs_0_), channel_id=1, source_target_pairs={{0,96},{32,0},{64,32},{96,64},{1,97},{33,1},{65,33},{97,65},{2,98}... | collective-permute-start | bytes 1572872 | tf_op jit(solution)/shard_map/ppermute | solution.py:23
  48.0 8.4 %collective-permute-done.4.refs_1_ = f32[8,16,1024]{2,1,0:T(8,128)S(1)} collective-permute-done((f32[8,16,1024]{2,1,0:T(8,128)S(1)}, f32[8,16,1024]{2,1,0:T(8,128)S(1)}, u32[]{:S(2)}, u32[]{:S(2)}) %collective-permute-start.4) | collective-permute-done | bytes 524320 | tf_op jit(solution)/shard_map/ppermute | solution.py:23
  56.4 3.5 %collective-permute-start.5 = (f32[4,16,1024]{2,1,0:T(8,128)S(1)}, f32[4,16,1024]{2,1,0:T(8,128)S(1)}, u32[]{:S(2)}, u32[]{:S(2)}) collective-permute-start(f32[4,16,1024]{2,1,0:T(8,128)S(1)} %slice.27), channel_id=1, source_target_pairs={{0,96},{32,0},{64,32},{96,64},{1,97},{33,1},{65,33},{97,65},{2,98}... | collective-permute-start | bytes 786440 | tf_op jit(solution)/shard_map/ppermute | solution.py:23
  60.1 11.3 %collective-permute-done.8.refs_6_ = f32[1400,512]{1,0:T(8,128)} collective-permute-done((f32[1400,512]{1,0:T(8,128)}, f32[1400,512]{1,0:T(8,128)}, u32[]{:S(2)}, u32[]{:S(2)}) %collective-permute-start.8) | collective-permute-done | bytes 2867232 | tf_op jit(solution)/shard_map/ppermute | solution.py:31
  71.4 1.7 collective-permute-done.9.refs_8_
  75.4 1.6 collective-permute-start.14
  79.2 3.7 %collective-permute-done.11.refs_9_ = f32[1400,512]{1,0:T(8,128)} collective-permute-done((f32[1400,512]{1,0:T(8,128)}, f32[1400,512]{1,0:T(8,128)}, u32[]{:S(2)}, u32[]{:S(2)}) %collective-permute-start.11) | collective-permute-done | bytes 2867232 | tf_op jit(solution)/shard_map/ppermute | solution.py:19
  82.9 17.5 %shard_map.28 = (f32[64,1400]{1,0:T(8,128)}, f32[64,1400]{1,0:T(8,128)}, f32[64,1400]{1,0:T(8,128)}, f32[64,1400]{1,0:T(8,128)}, f32[64,1400]{1,0:T(8,128)}, /*i...) custom-call(s32[3]{0:T(128)} %pad_add_fusion.place_ref, f32[8,16,1024]{2,1,0:T(8,128)} %copy-done.17, ...), custom_call_target="tpu_custom_call" | custom-call | flops 8808038400 | bytes 18530304 | tf_op jit(solution)/shard_map/pallas_call | solution.py:127
  100.3 4.9 %collective-permute-start.12 = (f32[64,1400]{1,0:T(8,128)}, f32[64,1400]{1,0:T(8,128)S(1)}, u32[]{:S(2)}, u32[]{:S(2)}) collective-permute-start(f32[64,1400]{1,0:T(8,128)} %get-tuple-element.34), channel_id=1, source_target_pairs={{0,12},{4,16},{8,20},{12,24},{16,28},{20,0},{24,4},{28,8},{1,13},{... | collective-permute-start | bytes 1075208 | tf_op jit(solution)/shard_map/ppermute | solution.py:27
  105.2 2.2 collective-permute-start.13
  107.4 1.7 collective-permute-done.15.refs_9_
  109.2 4.5 %collective-permute-done.14.refs_8_ = f32[768,512]{1,0:T(8,128)} collective-permute-done((f32[768,512]{1,0:T(8,128)S(1)}, f32[768,512]{1,0:T(8,128)}, u32[]{:S(2)}, u32[]{:S(2)}) %collective-permute-start.14) | collective-permute-done | bytes 1572896 | tf_op jit(solution)/shard_map/ppermute | solution.py:35
  113.6 15.7 %collective-permute-done.12 = f32[64,1400]{1,0:T(8,128)S(1)} collective-permute-done((f32[64,1400]{1,0:T(8,128)}, f32[64,1400]{1,0:T(8,128)S(1)}, u32[]{:S(2)}, u32[]{:S(2)}) %collective-permute-start.12) | collective-permute-done | bytes 358432 | tf_op jit(solution)/shard_map/ppermute | solution.py:27
  131.4 6.1 %collective-permute-start.18 = (f32[64,1400]{1,0:T(8,128)}, f32[64,1400]{1,0:T(8,128)S(1)}, u32[]{:S(2)}, u32[]{:S(2)}) collective-permute-start(f32[64,1400]{1,0:T(8,128)} %get-tuple-element.44), channel_id=1, source_target_pairs={{0,4},{4,8},{8,12},{12,16},{16,20},{20,24},{24,28},{28,0},{1,5},{5... | collective-permute-start | bytes 1075208 | tf_op jit(solution)/shard_map/ppermute | solution.py:27
  137.5 1.8 collective-permute-start.20
  139.3 3.7 %collective-permute-start.21 = (f32[64,1400]{1,0:T(8,128)}, f32[64,1400]{1,0:T(8,128)S(1)}, u32[]{:S(2)}, u32[]{:S(2)}) collective-permute-start(f32[64,1400]{1,0:T(8,128)} %get-tuple-element.47), channel_id=1, source_target_pairs={{0,24},{4,28},{8,0},{12,4},{16,8},{20,12},{24,16},{28,20},{1,25},{... | collective-permute-start | bytes 1075208 | tf_op jit(solution)/shard_map/ppermute | solution.py:27
  143.0 2.6 collective-permute-start.22
  145.7 17.6 %shard_map.29 = f32[512,1400]{1,0:T(8,128)} custom-call(s32[3]{0:T(128)} %pad_add_fusion.place_ref, f32[8,16,1024]{2,1,0:T(8,128)} %copy-done.17, f32[8,16,1024]{2,1,0:T(8,128)} %copy-done.18, f32[4,16,1024]{2,1,0:T(8,128)} %copy-done.22, f32[4,16,1024]{2,1,0:T(8,128)} %copy-done.23, f32[8,16,1024]{2,1,0:T(8,128)} %copy-done.19, ...), custom_call_target="tpu_custom_call" | custom-call | flops 8808038400 | bytes 18530304 | tf_op jit(solution)/shard_map/pallas_call | solution.py:127
  165.6 10.2 %collective-permute-done.21 = f32[64,1400]{1,0:T(8,128)S(1)} collective-permute-done((f32[64,1400]{1,0:T(8,128)}, f32[64,1400]{1,0:T(8,128)S(1)}, u32[]{:S(2)}, u32[]{:S(2)}) %collective-permute-start.21) | collective-permute-done | bytes 358432 | tf_op jit(solution)/shard_map/ppermute | solution.py:27
  177.2 10.9 %all-to-all-start.1 = ((f32[32,16,1400]{2,1,0:T(8,128)}), f32[32,16,1400]{2,1,0:T(8,128)S(1)}, u32[]{:S(2)}, u32[]{:S(2)}) async-start(f32[32,16,1400]{2,1,0:T(8,128)} %bitcast.24), calls=%async_computation.1 | async-start | bytes 5767168 | tf_op jit(solution)/shard_map/all_to_all | solution.py:279
  195.1 1.5 shard_map.30
  197.5 1.8 collective-permute-start.23
  199.3 2.7 collective-permute-start.24
  203.5 28.4 %collective-permute-done.23.refs_1_ = f32[8,16,1400]{2,1,0:T(8,128)} collective-permute-done((f32[8,16,1400]{2,1,0:T(8,128)}, f32[8,16,1400]{2,1,0:T(8,128)}, u32[]{:S(2)}, u32[]{:S(2)}) %collective-permute-start.23) | collective-permute-done | bytes 716832 | tf_op jit(solution)/shard_map/ppermute | solution.py:23
  231.9 25.6 %collective-permute-done.24.refs_2_ = f32[8,16,1400]{2,1,0:T(8,128)} collective-permute-done((f32[8,16,1400]{2,1,0:T(8,128)}, f32[8,16,1400]{2,1,0:T(8,128)}, u32[]{:S(2)}, u32[]{:S(2)}) %collective-permute-start.24) | collective-permute-done | bytes 716832 | tf_op jit(solution)/shard_map/ppermute | solution.py:23
  258.6 4.4 %shard_map.31._ = f32[16,89600]{1,0:T(8,128)} custom-call(s32[2]{0:T(128)S(1)} %pad_add_fusion.1.at_ref, f32[8,16,1400]{2,1,0:T(8,128)S(1)} %copy-done.1, f32[8,16,1400]{2,1,0:T(8,128)} %collective-permute-done.23.refs_1_, f32[8,16,1400]{2,1,0:T(8,128)} %collective-permute-done.24.refs_2_, f32[8,16,1400]{2,1,0:T(8,128)} %collective-permute-done.25.refs_3_), custom_call_target="tpu_custom_call" | custom-call | bytes 5734400 | tf_op jit(solution)/shard_map/pallas_call | solution.py:230
  263.0 2.0 shard_map.32
  (89 shorter events, 28.7 us)
Async XLA Ops:
  6.5 38.7 %collective-permute-start.3 = (f32[1400,512]{1,0:T(8,128)}, f32[1400,512]{1,0:T(8,128)}, u32[]{:S(2)}, u32[]{:S(2)}) collective-permute-start(f32[1400,512]{1,0:T(8,128)} %bitcast.25), channel_id=1, source_target_pairs={{0,1},{1,0},{2,3},{3,2},{4,5},{5,4},{6,7},{7,6},{8,9},{9,8},{10,11... | collective-permute-start | bytes 8601608 | tf_op jit(solution)/shard_map/ppermute | solution.py:19
  6.5 64.9 %collective-permute-start.8 = (f32[1400,512]{1,0:T(8,128)}, f32[1400,512]{1,0:T(8,128)}, u32[]{:S(2)}, u32[]{:S(2)}) collective-permute-start(f32[1400,512]{1,0:T(8,128)} %bitcast.26), channel_id=1, source_target_pairs={{0,128},{128,0},{1,129},{129,1},{2,130},{130,2},{3,131},{131,3},{4... | collective-permute-start | bytes 8601608 | tf_op jit(solution)/shard_map/ppermute | solution.py:31
  7.3 65.8 %collective-permute-start.9 = (f32[1400,512]{1,0:T(8,128)}, f32[1400,512]{1,0:T(8,128)}, u32[]{:S(2)}, u32[]{:S(2)}) collective-permute-start(f32[1400,512]{1,0:T(8,128)} %bitcast.27), channel_id=1, source_target_pairs={{128,2},{2,128},{130,0},{0,130},{129,3},{3,129},{131,1},{1,131},{1... | collective-permute-start | bytes 8601608 | tf_op jit(solution)/shard_map/ppermute | solution.py:35
  9.4 6.1 %collective-permute-start.2 = (f32[16,1024]{1,0:T(8,128)S(1)}, f32[16,1024]{1,0:T(8,128)S(1)}, u32[]{:S(2)}, u32[]{:S(2)}) collective-permute-start(f32[16,1024]{1,0:T(8,128)S(1)} %get-tuple-element.55), channel_id=1, source_target_pairs={{0,32},{32,64},{64,96},{96,0},{1,33},{33,65},{65,97},{97,1},{2,34}... | collective-permute-start | bytes 196616 | tf_op jit(solution)/shard_map/ppermute | solution.py:23
  10.8 6.1 %collective-permute-start.1 = (f32[16,1024]{1,0:T(8,128)S(1)}, f32[16,1024]{1,0:T(8,128)S(1)}, u32[]{:S(2)}, u32[]{:S(2)}) collective-permute-start(f32[16,1024]{1,0:T(8,128)S(1)} %get-tuple-element.55), channel_id=1, source_target_pairs={{0,64},{32,96},{64,0},{96,32},{1,65},{33,97},{65,1},{97,33},{2,66}... | collective-permute-start | bytes 196616 | tf_op jit(solution)/shard_map/ppermute | solution.py:23
  15.5 4.3 %collective-permute-start = (f32[16,1024]{1,0:T(8,128)S(1)}, f32[16,1024]{1,0:T(8,128)S(1)}, u32[]{:S(2)}, u32[]{:S(2)}) collective-permute-start(f32[16,1024]{1,0:T(8,128)S(1)} %get-tuple-element.55), channel_id=1, source_target_pairs={{0,96},{32,0},{64,32},{96,64},{1,97},{33,1},{65,33},{97,65},{2,98}... | collective-permute-start | bytes 196616 | tf_op jit(solution)/shard_map/ppermute | solution.py:23
  21.3 23.9 %all-to-all-start = ((f32[8,16,1024]{2,1,0:T(8,128)}), f32[8,16,1024]{2,1,0:T(8,128)S(1)}, u32[]{:S(2)}, u32[]{:S(2)}) async-start(f32[8,16,1024]{2,1,0:T(8,128)} %broadcast_in_dim.2), calls=%async_computation | async-start | bytes 1048576 | tf_op jit(solution)/shard_map/all_to_all | solution.py:261
  29.1 50.1 %all-gather.3.cloned.1.call-start = ((), (), s32[]{:S(2)}) async-start(), calls=%async_computation.2 | async-start | bytes 2359296 | tf_op jit(solution)/shard_map/all_gather | solution.py:264
  45.2 33.2 %copy-start.17 = (f32[8,16,1024]{2,1,0:T(8,128)}, f32[8,16,1024]{2,1,0:T(8,128)S(1)}, u32[]{:S(2)}) copy-start(f32[8,16,1024]{2,1,0:T(8,128)S(1)} %all-to-all-done.refs_0_) | copy-start | bytes 1572868
  45.2 11.2 %collective-permute-start.4 = (f32[8,16,1024]{2,1,0:T(8,128)S(1)}, f32[8,16,1024]{2,1,0:T(8,128)S(1)}, u32[]{:S(2)}, u32[]{:S(2)}) collective-permute-start(f32[8,16,1024]{2,1,0:T(8,128)S(1)} %all-to-all-done.refs_0_), channel_id=1, source_target_pairs={{0,96},{32,0},{64,32},{96,64},{1,97},{33,1},{65,33},{97,65},{2,98}... | collective-permute-start | bytes 1572872 | tf_op jit(solution)/shard_map/ppermute | solution.py:23
  47.9 12.0 %collective-permute-start.6 = (f32[8,16,1024]{2,1,0:T(8,128)S(1)}, f32[8,16,1024]{2,1,0:T(8,128)S(1)}, u32[]{:S(2)}, u32[]{:S(2)}) collective-permute-start(f32[8,16,1024]{2,1,0:T(8,128)S(1)} %all-to-all-done.refs_0_), channel_id=1, source_target_pairs={{0,32},{32,64},{64,96},{96,0},{1,33},{33,65},{65,97},{97,1},{2,34}... | collective-permute-start | bytes 1572872 | tf_op jit(solution)/shard_map/ppermute | solution.py:23
  56.4 16.7 %collective-permute-start.5 = (f32[4,16,1024]{2,1,0:T(8,128)S(1)}, f32[4,16,1024]{2,1,0:T(8,128)S(1)}, u32[]{:S(2)}, u32[]{:S(2)}) collective-permute-start(f32[4,16,1024]{2,1,0:T(8,128)S(1)} %slice.27), channel_id=1, source_target_pairs={{0,96},{32,0},{64,32},{96,64},{1,97},{33,1},{65,33},{97,65},{2,98}... | collective-permute-start | bytes 786440 | tf_op jit(solution)/shard_map/ppermute | solution.py:23
  59.9 13.3 %copy-start.19 = (f32[8,16,1024]{2,1,0:T(8,128)}, f32[8,16,1024]{2,1,0:T(8,128)S(1)}, u32[]{:S(2)}) copy-start(f32[8,16,1024]{2,1,0:T(8,128)S(1)} %collective-permute-done.6.refs_4_) | copy-start | bytes 1572868
  60.0 13.1 %collective-permute-start.7 = (f32[4,16,1024]{2,1,0:T(8,128)S(1)}, f32[4,16,1024]{2,1,0:T(8,128)S(1)}, u32[]{:S(2)}, u32[]{:S(2)}) collective-permute-start(f32[4,16,1024]{2,1,0:T(8,128)S(1)} %slice.28), channel_id=1, source_target_pairs={{0,32},{32,64},{64,96},{96,0},{1,33},{33,65},{65,97},{97,1},{2,34}... | collective-permute-start | bytes 786440 | tf_op jit(solution)/shard_map/ppermute | solution.py:23
  73.1 6.1 %collective-permute-start.10 = (f32[1400,512]{1,0:T(8,128)}, f32[1400,512]{1,0:T(8,128)}, u32[]{:S(2)}, u32[]{:S(2)}) collective-permute-start(f32[1400,512]{1,0:T(8,128)} %collective-permute-done.8.refs_6_), channel_id=1, source_target_pairs={{0,1},{1,0},{2,3},{3,2},{4,5},{5,4},{6,7},{7,6},{8,9},{9,8},{10,11... | collective-permute-start | bytes 8601608 | tf_op jit(solution)/shard_map/ppermute | solution.py:19
  73.9 9.0 %collective-permute-start.11 = (f32[1400,512]{1,0:T(8,128)}, f32[1400,512]{1,0:T(8,128)}, u32[]{:S(2)}, u32[]{:S(2)}) collective-permute-start(f32[1400,512]{1,0:T(8,128)} %collective-permute-done.9.refs_8_), channel_id=1, source_target_pairs={{0,1},{1,0},{2,3},{3,2},{4,5},{5,4},{6,7},{7,6},{8,9},{9,8},{10,11... | collective-permute-start | bytes 8601608 | tf_op jit(solution)/shard_map/ppermute | solution.py:19
  75.4 38.2 %collective-permute-start.14 = (f32[768,512]{1,0:T(8,128)S(1)}, f32[768,512]{1,0:T(8,128)}, u32[]{:S(2)}, u32[]{:S(2)}) collective-permute-start(f32[768,512]{1,0:T(8,128)S(1)} %slice.25), channel_id=1, source_target_pairs={{128,2},{2,128},{130,0},{0,130},{129,3},{3,129},{131,1},{1,131},{1... | collective-permute-start | bytes 4718600 | tf_op jit(solution)/shard_map/ppermute | solution.py:35
  78.4 30.8 %collective-permute-start.15 = (f32[632,512]{1,0:T(8,128)S(1)}, f32[632,512]{1,0:T(8,128)}, u32[]{:S(2)}, u32[]{:S(2)}) collective-permute-start(f32[632,512]{1,0:T(8,128)S(1)} %slice.26), channel_id=1, source_target_pairs={{0,128},{128,0},{1,129},{129,1},{2,130},{130,2},{3,131},{131,3},{4... | collective-permute-start | bytes 3883016 | tf_op jit(solution)/shard_map/ppermute | solution.py:31
  100.3 29.0 %collective-permute-start.12 = (f32[64,1400]{1,0:T(8,128)}, f32[64,1400]{1,0:T(8,128)S(1)}, u32[]{:S(2)}, u32[]{:S(2)}) collective-permute-start(f32[64,1400]{1,0:T(8,128)} %get-tuple-element.34), channel_id=1, source_target_pairs={{0,12},{4,16},{8,20},{12,24},{16,28},{20,0},{24,4},{28,8},{1,13},{... | collective-permute-start | bytes 1075208 | tf_op jit(solution)/shard_map/ppermute | solution.py:27
  105.2 24.9 %collective-permute-start.13 = (f32[64,1400]{1,0:T(8,128)}, f32[64,1400]{1,0:T(8,128)S(1)}, u32[]{:S(2)}, u32[]{:S(2)}) collective-permute-start(f32[64,1400]{1,0:T(8,128)} %get-tuple-element.35), channel_id=1, source_target_pairs={{0,20},{4,24},{8,28},{12,0},{16,4},{20,8},{24,12},{28,16},{1,21},{... | collective-permute-start | bytes 1075208 | tf_op jit(solution)/shard_map/ppermute | solution.py:27
  130.9 12.2 %collective-permute-start.16 = (f32[768,512]{1,0:T(8,128)}, f32[768,512]{1,0:T(8,128)S(1)}, u32[]{:S(2)}, u32[]{:S(2)}) collective-permute-start(f32[768,512]{1,0:T(8,128)} %collective-permute-done.14.refs_8_), channel_id=1, source_target_pairs={{0,1},{1,0},{2,3},{3,2},{4,5},{5,4},{6,7},{7,6},{8,9},{9,8},{10,11... | collective-permute-start | bytes 4718600 | tf_op jit(solution)/shard_map/ppermute | solution.py:19
  130.9 8.5 %collective-permute-start.17 = (f32[632,512]{1,0:T(8,128)}, f32[632,512]{1,0:T(8,128)S(1)}, u32[]{:S(2)}, u32[]{:S(2)}) collective-permute-start(f32[632,512]{1,0:T(8,128)} %collective-permute-done.15.refs_9_), channel_id=1, source_target_pairs={{0,1},{1,0},{2,3},{3,2},{4,5},{5,4},{6,7},{7,6},{8,9},{9,8},{10,11... | collective-permute-start | bytes 3883016 | tf_op jit(solution)/shard_map/ppermute | solution.py:19
  131.4 32.0 %collective-permute-start.18 = (f32[64,1400]{1,0:T(8,128)}, f32[64,1400]{1,0:T(8,128)S(1)}, u32[]{:S(2)}, u32[]{:S(2)}) collective-permute-start(f32[64,1400]{1,0:T(8,128)} %get-tuple-element.44), channel_id=1, source_target_pairs={{0,4},{4,8},{8,12},{12,16},{16,20},{20,24},{24,28},{28,0},{1,5},{5... | collective-permute-start | bytes 1075208 | tf_op jit(solution)/shard_map/ppermute | solution.py:27
  137.5 26.6 %collective-permute-start.19 = (f32[64,1400]{1,0:T(8,128)}, f32[64,1400]{1,0:T(8,128)S(1)}, u32[]{:S(2)}, u32[]{:S(2)}) collective-permute-start(f32[64,1400]{1,0:T(8,128)} %get-tuple-element.45), channel_id=1, source_target_pairs={{0,28},{4,0},{8,4},{12,8},{16,12},{20,16},{24,20},{28,24},{1,29},{... | collective-permute-start | bytes 1075208 | tf_op jit(solution)/shard_map/ppermute | solution.py:27
  137.5 27.3 %collective-permute-start.20 = (f32[64,1400]{1,0:T(8,128)}, f32[64,1400]{1,0:T(8,128)S(1)}, u32[]{:S(2)}, u32[]{:S(2)}) collective-permute-start(f32[64,1400]{1,0:T(8,128)} %get-tuple-element.46), channel_id=1, source_target_pairs={{0,8},{4,12},{8,16},{12,20},{16,24},{20,28},{24,0},{28,4},{1,9},{5... | collective-permute-start | bytes 1075208 | tf_op jit(solution)/shard_map/ppermute | solution.py:27
  139.3 36.4 %collective-permute-start.21 = (f32[64,1400]{1,0:T(8,128)}, f32[64,1400]{1,0:T(8,128)S(1)}, u32[]{:S(2)}, u32[]{:S(2)}) collective-permute-start(f32[64,1400]{1,0:T(8,128)} %get-tuple-element.47), channel_id=1, source_target_pairs={{0,24},{4,28},{8,0},{12,4},{16,8},{20,12},{24,16},{28,20},{1,25},{... | collective-permute-start | bytes 1075208 | tf_op jit(solution)/shard_map/ppermute | solution.py:27
  143.0 33.5 %collective-permute-start.22 = (f32[64,1400]{1,0:T(8,128)}, f32[64,1400]{1,0:T(8,128)S(1)}, u32[]{:S(2)}, u32[]{:S(2)}) collective-permute-start(f32[64,1400]{1,0:T(8,128)} %get-tuple-element.48), channel_id=1, source_target_pairs={{0,16},{4,20},{8,24},{12,28},{16,0},{20,4},{24,8},{28,12},{1,17},{... | collective-permute-start | bytes 1075208 | tf_op jit(solution)/shard_map/ppermute | solution.py:27
  177.2 10.9 %copy-start.2 = (f32[64,1400]{1,0:T(8,128)S(1)}, f32[64,1400]{1,0:T(8,128)}, u32[]{:S(2)}) copy-start(f32[64,1400]{1,0:T(8,128)} %get-tuple-element.50) | copy-start | bytes 1075204
  177.2 85.7 %all-to-all-start.1 = ((f32[32,16,1400]{2,1,0:T(8,128)}), f32[32,16,1400]{2,1,0:T(8,128)S(1)}, u32[]{:S(2)}, u32[]{:S(2)}) async-start(f32[32,16,1400]{2,1,0:T(8,128)} %bitcast.24), calls=%async_computation.1 | async-start | bytes 5767168 | tf_op jit(solution)/shard_map/all_to_all | solution.py:279
  197.5 34.4 %collective-permute-start.23 = (f32[8,16,1400]{2,1,0:T(8,128)}, f32[8,16,1400]{2,1,0:T(8,128)}, u32[]{:S(2)}, u32[]{:S(2)}) collective-permute-start(f32[8,16,1400]{2,1,0:T(8,128)} %get-tuple-element.52), channel_id=1, source_target_pairs={{0,32},{32,64},{64,96},{96,0},{1,33},{33,65},{65,97},{97,1},{2,34}... | collective-permute-start | bytes 2150408 | tf_op jit(solution)/shard_map/ppermute | solution.py:23
  199.3 58.2 %collective-permute-start.24 = (f32[8,16,1400]{2,1,0:T(8,128)}, f32[8,16,1400]{2,1,0:T(8,128)}, u32[]{:S(2)}, u32[]{:S(2)}) collective-permute-start(f32[8,16,1400]{2,1,0:T(8,128)} %get-tuple-element.53), channel_id=1, source_target_pairs={{0,64},{32,96},{64,0},{96,32},{1,65},{33,97},{65,1},{97,33},{2,66}... | collective-permute-start | bytes 2150408 | tf_op jit(solution)/shard_map/ppermute | solution.py:23
  202.0 55.5 %collective-permute-start.25 = (f32[8,16,1400]{2,1,0:T(8,128)}, f32[8,16,1400]{2,1,0:T(8,128)}, u32[]{:S(2)}, u32[]{:S(2)}) collective-permute-start(f32[8,16,1400]{2,1,0:T(8,128)} %get-tuple-element.54), channel_id=1, source_target_pairs={{0,96},{32,0},{64,32},{96,64},{1,97},{33,1},{65,33},{97,65},{2,98}... | collective-permute-start | bytes 2150408 | tf_op jit(solution)/shard_map/ppermute | solution.py:23
  (21 other events, 25.5 us)
Sparse Core Ops, SparseCore 0:
  31.7 42.6 all-gather.2

commit v9 on v5

--- a/solution.py
+++ b/solution.py
@@ -194,8 +194,9 @@
     low, high = shift_x(ahead[:4], -1), shift_x(behind[4:], 1)
     t = (here, ahead, low, high, behind, last)
 
-    first, second = after(integrals.T[:CUT], low, high), integrals.T[CUT:]
-    near, far = after((swap_near(first), swap_far(first)), ahead, behind)
+    first, second = integrals.T[:CUT], integrals.T[CUT:]
+    near = swap_near(after(first, ahead, behind))
+    far = swap_far(after(first, low, high))
     near_next, far_next = after((swap_near(second), swap_far(second)), ahead, behind)
 
     def exchange(v):

time: 262 us -> 261 us (level)
  waiting for transfers between devices: 135 us -> 142 us
  starting transfers between devices: 51.4 us -> 46 us
    ppermute x3, waiting for transfers between devices: 0.15 us -> 16.6 us  [swap_near(): return lax.ppermute(value, 'yl', [(0, 1), (1, 0)])]
    ppermute x3, waiting for transfers between devices: 34.4 us -> 23.9 us  [swap_far(): return lax.ppermute(value, ('yl', 'yh'), [(2, 1), (1, 2), (3, 0), (0, 3)])]
    all_to_all x3, starting transfers between devices: 24.5 us -> 21.3 us  [exchange(): lax.all_to_all(v.reshape(-1, rows, v.shape[1]), ('x', 'z'), split_axis=0,...]
    ppermute x7, waiting for transfers between devices: 7.74 us -> 10.5 us  [shift_x(): return lax.ppermute(value, 'x', [(i, (i + by) % 4) for i in range(4)])]
where the time goes in v9:
time: 261 us
  waiting for transfers between devices  142 us (54%)
  starting transfers between devices  46 us (18%)
  Pallas kernels  44.9 us (17%)
  between operations  13.5 us (5%)
  local copies, waits for them, and re-layouts  12.9 us (5%)
    all_to_all x3, waiting for transfers between devices, exchange(): lax.all_to_all(v.reshape(-1, rows, v.shape[1]), ('x', 'z'), split_axis=0,...  66.9 us
    pallas_call x3, Pallas kernels, product(): pl.pallas_call(functools.partial(product_kernel, around, counts), grid_sp...  40.9 us
    ppermute x3, waiting for transfers between devices, swap_far(): return lax.ppermute(value, ('yl', 'yh'), [(2, 1), (1, 2), (3, 0), (0, 3)])  23.9 us
    all_to_all x3, starting transfers between devices, exchange(): lax.all_to_all(v.reshape(-1, rows, v.shape[1]), ('x', 'z'), split_axis=0,...  21.3 us
    ppermute x3, waiting for transfers between devices, swap_near(): return lax.ppermute(value, 'yl', [(0, 1), (1, 0)])  16.6 us
    all_to_all x1, waiting for transfers between devices, on_device(): here = lax.all_to_all(here, 'z', split_axis=0, concat_axis=0, tiled=True)  15.9 us
    ppermute x7, starting transfers between devices, shift_x(): return lax.ppermute(value, 'x', [(i, (i + by) % 4) for i in range(4)])  10.8 us
    ppermute x7, waiting for transfers between devices, shift_x(): return lax.ppermute(value, 'x', [(i, (i + by) % 4) for i in range(4)])  10.5 us
  transfers between devices with their start and end apart: 26, of which 16 were waited for; matrix products, arithmetic and copies ran while one was open for 2% of the time, Pallas kernels for 16%

profile of v9, /device:TPU:24, one launch (start us, length us, event | category | flops | bytes accessed | tf_op | source)
XLA Modules:
  0.0 260.6 jit_solution(4885367424089823791)
XLA Ops:
  7.4 1.6 collective-permute-start.2
  9.0 2.7 %collective-permute-start.1 = (f32[16,1024]{1,0:T(8,128)S(1)}, f32[16,1024]{1,0:T(8,128)S(1)}, u32[]{:S(2)}, u32[]{:S(2)}) collective-permute-start(f32[16,1024]{1,0:T(8,128)S(1)} %get-tuple-element.17), channel_id=1, source_target_pairs={{0,64},{32,96},{64,0},{96,32},{1,65},{33,97},{65,1},{97,33},{2,66}... | collective-permute-start | bytes 196616 | tf_op jit(solution)/shard_map/ppermute | solution.py:22
  11.7 1.4 collective-permute-start
  13.6 1.4 collective-permute-done.1
  17.6 8.5 %all-to-all-start = ((f32[8,16,1024]{2,1,0:T(8,128)}), f32[8,16,1024]{2,1,0:T(8,128)S(1)}, u32[]{:S(2)}, u32[]{:S(2)}) async-start(f32[8,16,1024]{2,1,0:T(8,128)} %broadcast_in_dim.2), calls=%async_computation | async-start | bytes 1048576 | tf_op jit(solution)/shard_map/all_to_all | solution.py:191
  26.1 2.6 %slice.30.refs_7_ = f32[632,512]{1,0:T(8,128)} slice(f32[1400,512]{1,0:T(8,128)} %bitcast.11), slice={[768:1400], [0:512]} | slice | bytes 2588672 | tf_op jit(solution)/shard_map/slice | solution.py:197
  30.5 15.9 %all-to-all-done.refs_0_ = f32[8,16,1024]{2,1,0:T(8,128)S(1)} async-done(((f32[8,16,1024]{2,1,0:T(8,128)}), f32[8,16,1024]{2,1,0:T(8,128)S(1)}, u32[]{:S(2)}, u32[]{:S(2)}) %all-to-all-start) | async-done | bytes 524320 | tf_op jit(solution)/shard_map/all_to_all | solution.py:191
  46.4 2.6 collective-permute-start.3
  49.0 8.7 %collective-permute-done.11.refs_6_ = f32[632,512]{1,0:T(8,128)} collective-permute-done((f32[632,512]{1,0:T(8,128)}, f32[632,512]{1,0:T(8,128)}, u32[]{:S(2)}, u32[]{:S(2)}) %collective-permute-start.11) | collective-permute-done | bytes 1294368 | tf_op jit(solution)/shard_map/ppermute | solution.py:26
  57.7 1.7 collective-permute-done.12.refs_8_
  60.0 2.5 collective-permute-start.4
  62.6 1.3 slice.29.refs_6_
  64.2 4.3 %collective-permute-done.4.refs_2_ = f32[4,16,1024]{2,1,0:T(8,128)S(1)} collective-permute-done((f32[4,16,1024]{2,1,0:T(8,128)S(1)}, f32[4,16,1024]{2,1,0:T(8,128)S(1)}, u32[]{:S(2)}, u32[]{:S(2)}) %collective-permute-start.4) | collective-permute-done | bytes 262176 | tf_op jit(solution)/shard_map/ppermute | solution.py:22
  68.4 3.4 %collective-permute-done.6.refs_3_ = f32[4,16,1024]{2,1,0:T(8,128)S(1)} collective-permute-done((f32[4,16,1024]{2,1,0:T(8,128)S(1)}, f32[4,16,1024]{2,1,0:T(8,128)S(1)}, u32[]{:S(2)}, u32[]{:S(2)}) %collective-permute-start.6) | collective-permute-done | bytes 262176 | tf_op jit(solution)/shard_map/ppermute | solution.py:22
  73.5 11.4 %shard_map.29 = f32[512,632]{1,0:T(8,128)} custom-call(s32[3]{0:T(128)} %pad_add_fusion.place_ref, f32[8,16,1024]{2,1,0:T(8,128)} %copy-done.5, f32[8,16,1024]{2,1,0:T(8,128)} %copy-done.6, f32[4,16,1024]{2,1,0:T(8,128)} %copy-done.12, f32[4,16,1024]{2,1,0:T(8,128)} %copy-done.13, f32[8,16,1024]{2,1,0:T(8,128)} %copy-done.7, f32[8,4,16,1024]{3,2,1,0:T(8,128)} %bitcast.15, ...), custom_call_target="tpu_custom_call" | custom-call | flops 3976200192 | bytes 10665984 | tf_op jit(solution)/shard_map/pallas_call | solution.py:122
  84.8 7.6 %all-to-all-start.1 = ((f32[32,16,632]{2,1,0:T(8,128)}), f32[32,16,632]{2,1,0:T(8,128)S(1)}, u32[]{:S(2)}, u32[]{:S(2)}) async-start(f32[32,16,632]{2,1,0:T(8,128)} %bitcast.14), calls=%async_computation.1 | async-start | bytes 2621440 | tf_op jit(solution)/shard_map/all_to_all | solution.py:203
  92.5 7.9 %collective-permute-done.9.refs_6_ = f32[768,512]{1,0:T(8,128)} collective-permute-done((f32[768,512]{1,0:T(8,128)}, f32[768,512]{1,0:T(8,128)}, u32[]{:S(2)}, u32[]{:S(2)}) %collective-permute-start.9) | collective-permute-done | bytes 1572896 | tf_op jit(solution)/shard_map/ppermute | solution.py:26
  100.3 8.2 %collective-permute-done.19.refs_8_ = f32[768,512]{1,0:T(8,128)S(1)} collective-permute-done((f32[768,512]{1,0:T(8,128)}, f32[768,512]{1,0:T(8,128)S(1)}, u32[]{:S(2)}, u32[]{:S(2)}) %collective-permute-start.19) | collective-permute-done | bytes 1572896 | tf_op jit(solution)/shard_map/ppermute | solution.py:30
  109.6 2.5 collective-permute-done.20.refs_9_
  112.1 11.6 %shard_map.30 = f32[512,768]{1,0:T(8,128)} custom-call(s32[3]{0:T(128)} %pad_add_fusion.place_ref, f32[8,16,1024]{2,1,0:T(8,128)} %copy-done.5, f32[8,16,1024]{2,1,0:T(8,128)} %copy-done.6, f32[4,16,1024]{2,1,0:T(8,128)} %copy-done.12, f32[4,16,1024]{2,1,0:T(8,128)} %copy-done.13, f32[8,16,1024]{2,1,0:T(8,128)} %copy-done.7, f32[8,4,16,1024]{3,2,1,0:T(8,128)} %bitcast.16, ...), custom_call_target="tpu_custom_call" | custom-call | flops 4831838208 | bytes 12058624 | tf_op jit(solution)/shard_map/pallas_call | solution.py:122
  123.6 2.3 all-to-all-done.1.refs_1_
  125.9 1.1 copy-done.2
  127.0 5.7 %all-to-all-start.3 = ((f32[32,16,768]{2,1,0:T(8,128)}), f32[32,16,768]{2,1,0:T(8,128)S(1)}, u32[]{:S(2)}, u32[]{:S(2)}) async-start(f32[32,16,768]{2,1,0:T(8,128)} %bitcast.13), calls=%async_computation.3 | async-start | bytes 3145728 | tf_op jit(solution)/shard_map/all_to_all | solution.py:203
  132.8 14.0 %collective-permute-done.10.refs_10_ = f32[768,512]{1,0:T(8,128)} collective-permute-done((f32[768,512]{1,0:T(8,128)}, f32[768,512]{1,0:T(8,128)}, u32[]{:S(2)}, u32[]{:S(2)}) %collective-permute-start.10) | collective-permute-done | bytes 1572896 | tf_op jit(solution)/shard_map/ppermute | solution.py:30
  147.4 4.6 %collective-permute-done.8.refs_9_ = f32[632,512]{1,0:T(8,128)S(1)} collective-permute-done((f32[632,512]{1,0:T(8,128)}, f32[632,512]{1,0:T(8,128)S(1)}, u32[]{:S(2)}, u32[]{:S(2)}) %collective-permute-start.8) | collective-permute-done | bytes 1294368 | tf_op jit(solution)/shard_map/ppermute | solution.py:18
  155.3 18.0 %shard_map.28 = f32[512,1400]{1,0:T(8,128)} custom-call(s32[3]{0:T(128)} %pad_add_fusion.place_ref, f32[8,16,1024]{2,1,0:T(8,128)} %copy-done.5, f32[8,16,1024]{2,1,0:T(8,128)} %copy-done.6, f32[4,16,1024]{2,1,0:T(8,128)} %copy-done.12, f32[4,16,1024]{2,1,0:T(8,128)} %copy-done.13, f32[8,16,1024]{2,1,0:T(8,128)} %copy-done.7, f32[8,4,16,1024]{3,2,1,0:T(8,128)} %bitcast.17, ...), custom_call_target="tpu_custom_call" | custom-call | flops 8808038400 | bytes 18530304 | tf_op jit(solution)/shard_map/pallas_call | solution.py:122
  174.5 7.9 %all-to-all-start.2 = ((f32[32,16,1400]{2,1,0:T(8,128)}), f32[32,16,1400]{2,1,0:T(8,128)S(1)}, u32[]{:S(2)}, u32[]{:S(2)}) async-start(f32[32,16,1400]{2,1,0:T(8,128)} %bitcast.10), calls=%async_computation.2 | async-start | bytes 5767168 | tf_op jit(solution)/shard_map/all_to_all | solution.py:203
  182.4 1.4 copy-done.1
  183.8 1.3 copy-done.3
  185.1 2.0 shard_map.31.refs_1_
  187.1 64.7 %all-to-all-done.2.refs_0_ = f32[32,16,1400]{2,1,0:T(8,128)S(1)} async-done(((f32[32,16,1400]{2,1,0:T(8,128)}), f32[32,16,1400]{2,1,0:T(8,128)S(1)}, u32[]{:S(2)}, u32[]{:S(2)}) %all-to-all-start.2) | async-done | bytes 2867232 | tf_op jit(solution)/shard_map/all_to_all | solution.py:203
  251.8 2.0 shard_map.32
  (62 shorter events, 14.5 us)
Async XLA Ops:
  6.5 66.9 %all-gather.3.cloned.1.call-start = ((), (), s32[]{:S(2)}) async-start(), calls=%async_computation.4 | async-start | bytes 2359296 | tf_op jit(solution)/shard_map/all_gather | solution.py:192
  7.4 6.1 %collective-permute-start.2 = (f32[16,1024]{1,0:T(8,128)S(1)}, f32[16,1024]{1,0:T(8,128)S(1)}, u32[]{:S(2)}, u32[]{:S(2)}) collective-permute-start(f32[16,1024]{1,0:T(8,128)S(1)} %get-tuple-element.17), channel_id=1, source_target_pairs={{0,32},{32,64},{64,96},{96,0},{1,33},{33,65},{65,97},{97,1},{2,34}... | collective-permute-start | bytes 196616 | tf_op jit(solution)/shard_map/ppermute | solution.py:22
  9.0 5.9 %collective-permute-start.1 = (f32[16,1024]{1,0:T(8,128)S(1)}, f32[16,1024]{1,0:T(8,128)S(1)}, u32[]{:S(2)}, u32[]{:S(2)}) collective-permute-start(f32[16,1024]{1,0:T(8,128)S(1)} %get-tuple-element.17), channel_id=1, source_target_pairs={{0,64},{32,96},{64,0},{96,32},{1,65},{33,97},{65,1},{97,33},{2,66}... | collective-permute-start | bytes 196616 | tf_op jit(solution)/shard_map/ppermute | solution.py:22
  11.7 4.3 %collective-permute-start = (f32[16,1024]{1,0:T(8,128)S(1)}, f32[16,1024]{1,0:T(8,128)S(1)}, u32[]{:S(2)}, u32[]{:S(2)}) collective-permute-start(f32[16,1024]{1,0:T(8,128)S(1)} %get-tuple-element.17), channel_id=1, source_target_pairs={{0,96},{32,0},{64,32},{96,64},{1,97},{33,1},{65,33},{97,65},{2,98}... | collective-permute-start | bytes 196616 | tf_op jit(solution)/shard_map/ppermute | solution.py:22
  17.6 28.8 %all-to-all-start = ((f32[8,16,1024]{2,1,0:T(8,128)}), f32[8,16,1024]{2,1,0:T(8,128)S(1)}, u32[]{:S(2)}, u32[]{:S(2)}) async-start(f32[8,16,1024]{2,1,0:T(8,128)} %broadcast_in_dim.2), calls=%async_computation | async-start | bytes 1048576 | tf_op jit(solution)/shard_map/all_to_all | solution.py:191
  26.1 36.6 %copy-start.4 = (f32[512,1400]{0,1:T(8,128)S(1)}, f32[512,1400]{0,1:T(8,128)}, u32[]{:S(2)}) copy-start(f32[512,1400]{0,1:T(8,128)} %param.3) | copy-start | bytes 8601604
  28.7 29.0 %collective-permute-start.11 = (f32[632,512]{1,0:T(8,128)}, f32[632,512]{1,0:T(8,128)}, u32[]{:S(2)}, u32[]{:S(2)}) collective-permute-start(f32[632,512]{1,0:T(8,128)} %slice.30.refs_7_), channel_id=1, source_target_pairs={{0,128},{128,0},{1,129},{129,1},{2,130},{130,2},{3,131},{131,3},{4... | collective-permute-start | bytes 3883016 | tf_op jit(solution)/shard_map/ppermute | solution.py:26
  29.4 30.0 %collective-permute-start.12 = (f32[632,512]{1,0:T(8,128)}, f32[632,512]{1,0:T(8,128)}, u32[]{:S(2)}, u32[]{:S(2)}) collective-permute-start(f32[632,512]{1,0:T(8,128)} %slice.30.refs_7_), channel_id=1, source_target_pairs={{128,2},{2,128},{130,0},{0,130},{129,3},{3,129},{131,1},{1,131},{1... | collective-permute-start | bytes 3883016 | tf_op jit(solution)/shard_map/ppermute | solution.py:30
  46.4 17.5 %copy-start.5 = (f32[8,16,1024]{2,1,0:T(8,128)}, f32[8,16,1024]{2,1,0:T(8,128)S(1)}, u32[]{:S(2)}) copy-start(f32[8,16,1024]{2,1,0:T(8,128)S(1)} %all-to-all-done.refs_0_) | copy-start | bytes 1572868
  46.4 13.0 %collective-permute-start.3 = (f32[8,16,1024]{2,1,0:T(8,128)S(1)}, f32[8,16,1024]{2,1,0:T(8,128)S(1)}, u32[]{:S(2)}, u32[]{:S(2)}) collective-permute-start(f32[8,16,1024]{2,1,0:T(8,128)S(1)} %all-to-all-done.refs_0_), channel_id=1, source_target_pairs={{0,96},{32,0},{64,32},{96,64},{1,97},{33,1},{65,33},{97,65},{2,98}... | collective-permute-start | bytes 1572872 | tf_op jit(solution)/shard_map/ppermute | solution.py:22
  49.0 10.4 %collective-permute-start.5 = (f32[8,16,1024]{2,1,0:T(8,128)S(1)}, f32[8,16,1024]{2,1,0:T(8,128)S(1)}, u32[]{:S(2)}, u32[]{:S(2)}) collective-permute-start(f32[8,16,1024]{2,1,0:T(8,128)S(1)} %all-to-all-done.refs_0_), channel_id=1, source_target_pairs={{0,32},{32,64},{64,96},{96,0},{1,33},{33,65},{65,97},{97,1},{2,34}... | collective-permute-start | bytes 1572872 | tf_op jit(solution)/shard_map/ppermute | solution.py:22
  59.4 3.1 %copy-start.6 = (f32[8,16,1024]{2,1,0:T(8,128)}, f32[8,16,1024]{2,1,0:T(8,128)S(1)}, u32[]{:S(2)}) copy-start(f32[8,16,1024]{2,1,0:T(8,128)S(1)} %collective-permute-done.3.refs_1_) | copy-start | bytes 1572868
  59.4 3.1 %copy-start.7 = (f32[8,16,1024]{2,1,0:T(8,128)}, f32[8,16,1024]{2,1,0:T(8,128)S(1)}, u32[]{:S(2)}) copy-start(f32[8,16,1024]{2,1,0:T(8,128)S(1)} %collective-permute-done.5.refs_4_) | copy-start | bytes 1572868
  59.4 14.1 %collective-permute-start.16 = (f32[632,512]{1,0:T(8,128)}, f32[632,512]{1,0:T(8,128)}, u32[]{:S(2)}, u32[]{:S(2)}) collective-permute-start(f32[632,512]{1,0:T(8,128)} %collective-permute-done.11.refs_6_), channel_id=1, source_target_pairs={{0,1},{1,0},{2,3},{3,2},{4,5},{5,4},{6,7},{7,6},{8,9},{9,8},{10,11... | collective-permute-start | bytes 3883016 | tf_op jit(solution)/shard_map/ppermute | solution.py:18
  59.5 14.0 %collective-permute-start.17 = (f32[632,512]{1,0:T(8,128)}, f32[632,512]{1,0:T(8,128)}, u32[]{:S(2)}, u32[]{:S(2)}) collective-permute-start(f32[632,512]{1,0:T(8,128)} %collective-permute-done.12.refs_8_), channel_id=1, source_target_pairs={{0,1},{1,0},{2,3},{3,2},{4,5},{5,4},{6,7},{7,6},{8,9},{9,8},{10,11... | collective-permute-start | bytes 3883016 | tf_op jit(solution)/shard_map/ppermute | solution.py:18
  60.0 8.4 %collective-permute-start.4 = (f32[4,16,1024]{2,1,0:T(8,128)S(1)}, f32[4,16,1024]{2,1,0:T(8,128)S(1)}, u32[]{:S(2)}, u32[]{:S(2)}) collective-permute-start(f32[4,16,1024]{2,1,0:T(8,128)S(1)} %slice.27), channel_id=1, source_target_pairs={{0,96},{32,0},{64,32},{96,64},{1,97},{33,1},{65,33},{97,65},{2,98}... | collective-permute-start | bytes 786440 | tf_op jit(solution)/shard_map/ppermute | solution.py:22
  62.5 9.3 %collective-permute-start.6 = (f32[4,16,1024]{2,1,0:T(8,128)S(1)}, f32[4,16,1024]{2,1,0:T(8,128)S(1)}, u32[]{:S(2)}, u32[]{:S(2)}) collective-permute-start(f32[4,16,1024]{2,1,0:T(8,128)S(1)} %slice.28), channel_id=1, source_target_pairs={{0,32},{32,64},{64,96},{96,0},{1,33},{33,65},{65,97},{97,1},{2,34}... | collective-permute-start | bytes 786440 | tf_op jit(solution)/shard_map/ppermute | solution.py:22
  63.9 36.4 %collective-permute-start.9 = (f32[768,512]{1,0:T(8,128)}, f32[768,512]{1,0:T(8,128)}, u32[]{:S(2)}, u32[]{:S(2)}) collective-permute-start(f32[768,512]{1,0:T(8,128)} %slice.29.refs_6_), channel_id=1, source_target_pairs={{0,128},{128,0},{1,129},{129,1},{2,130},{130,2},{3,131},{131,3},{4... | collective-permute-start | bytes 4718600 | tf_op jit(solution)/shard_map/ppermute | solution.py:26
  68.4 3.4 %copy-start.12 = (f32[4,16,1024]{2,1,0:T(8,128)}, f32[4,16,1024]{2,1,0:T(8,128)S(1)}, u32[]{:S(2)}) copy-start(f32[4,16,1024]{2,1,0:T(8,128)S(1)} %collective-permute-done.4.refs_2_) | copy-start | bytes 786436
  71.8 36.7 %collective-permute-start.19 = (f32[768,512]{1,0:T(8,128)}, f32[768,512]{1,0:T(8,128)S(1)}, u32[]{:S(2)}, u32[]{:S(2)}) collective-permute-start(f32[768,512]{1,0:T(8,128)} %slice.29.refs_6_), channel_id=1, source_target_pairs={{128,2},{2,128},{130,0},{0,130},{129,3},{3,129},{131,1},{1,131},{1... | collective-permute-start | bytes 4718600 | tf_op jit(solution)/shard_map/ppermute | solution.py:30
  84.8 41.0 %all-to-all-start.1 = ((f32[32,16,632]{2,1,0:T(8,128)}), f32[32,16,632]{2,1,0:T(8,128)S(1)}, u32[]{:S(2)}, u32[]{:S(2)}) async-start(f32[32,16,632]{2,1,0:T(8,128)} %bitcast.14), calls=%async_computation.1 | async-start | bytes 2621440 | tf_op jit(solution)/shard_map/all_to_all | solution.py:203
  100.3 9.3 %collective-permute-start.18 = (f32[768,512]{1,0:T(8,128)}, f32[768,512]{1,0:T(8,128)}, u32[]{:S(2)}, u32[]{:S(2)}) collective-permute-start(f32[768,512]{1,0:T(8,128)} %collective-permute-done.9.refs_6_), channel_id=1, source_target_pairs={{0,1},{1,0},{2,3},{3,2},{4,5},{5,4},{6,7},{7,6},{8,9},{9,8},{10,11... | collective-permute-start | bytes 4718600 | tf_op jit(solution)/shard_map/ppermute | solution.py:18
  108.5 3.5 %copy-start.8 = (f32[768,512]{1,0:T(8,128)}, f32[768,512]{1,0:T(8,128)S(1)}, u32[]{:S(2)}) copy-start(f32[768,512]{1,0:T(8,128)S(1)} %collective-permute-done.19.refs_8_) | copy-start | bytes 4718596
  108.5 3.5 %collective-permute-start.20 = (f32[768,512]{1,0:T(8,128)S(1)}, f32[768,512]{1,0:T(8,128)}, u32[]{:S(2)}, u32[]{:S(2)}) collective-permute-start(f32[768,512]{1,0:T(8,128)S(1)} %collective-permute-done.19.refs_8_), channel_id=1, source_target_pairs={{0,1},{1,0},{2,3},{3,2},{4,5},{5,4},{6,7},{7,6},{8,9},{9,8},{10,11... | collective-permute-start | bytes 4718600 | tf_op jit(solution)/shard_map/ppermute | solution.py:18
  108.5 38.3 %collective-permute-start.10 = (f32[768,512]{1,0:T(8,128)}, f32[768,512]{1,0:T(8,128)}, u32[]{:S(2)}, u32[]{:S(2)}) collective-permute-start(f32[768,512]{1,0:T(8,128)} %collective-permute-done.9.refs_6_), channel_id=1, source_target_pairs={{128,2},{2,128},{130,0},{0,130},{129,3},{3,129},{131,1},{1,131},{1... | collective-permute-start | bytes 4718600 | tf_op jit(solution)/shard_map/ppermute | solution.py:30
  109.6 37.8 %collective-permute-start.13 = (f32[632,512]{1,0:T(8,128)}, f32[632,512]{1,0:T(8,128)}, u32[]{:S(2)}, u32[]{:S(2)}) collective-permute-start(f32[632,512]{1,0:T(8,128)} %collective-permute-done.12.refs_8_), channel_id=1, source_target_pairs={{0,128},{128,0},{1,129},{129,1},{2,130},{130,2},{3,131},{131,3},{4... | collective-permute-start | bytes 3883016 | tf_op jit(solution)/shard_map/ppermute | solution.py:26
  127.0 46.3 %all-to-all-start.3 = ((f32[32,16,768]{2,1,0:T(8,128)}), f32[32,16,768]{2,1,0:T(8,128)S(1)}, u32[]{:S(2)}, u32[]{:S(2)}) async-start(f32[32,16,768]{2,1,0:T(8,128)} %bitcast.13), calls=%async_computation.3 | async-start | bytes 3145728 | tf_op jit(solution)/shard_map/all_to_all | solution.py:203
  132.7 19.2 %collective-permute-start.7 = (f32[768,512]{1,0:T(8,128)}, f32[768,512]{1,0:T(8,128)S(1)}, u32[]{:S(2)}, u32[]{:S(2)}) collective-permute-start(f32[768,512]{1,0:T(8,128)} %slice.29.refs_6_), channel_id=1, source_target_pairs={{0,1},{1,0},{2,3},{3,2},{4,5},{5,4},{6,7},{7,6},{8,9},{9,8},{10,11... | collective-permute-start | bytes 4718600 | tf_op jit(solution)/shard_map/ppermute | solution.py:18
  146.8 8.4 %collective-permute-start.14 = (f32[768,512]{1,0:T(8,128)}, f32[768,512]{1,0:T(8,128)}, u32[]{:S(2)}, u32[]{:S(2)}) collective-permute-start(f32[768,512]{1,0:T(8,128)} %collective-permute-done.10.refs_10_), channel_id=1, source_target_pairs={{0,1},{1,0},{2,3},{3,2},{4,5},{5,4},{6,7},{7,6},{8,9},{9,8},{10,11... | collective-permute-start | bytes 4718600 | tf_op jit(solution)/shard_map/ppermute | solution.py:18
  146.8 5.1 %collective-permute-start.8 = (f32[632,512]{1,0:T(8,128)}, f32[632,512]{1,0:T(8,128)S(1)}, u32[]{:S(2)}, u32[]{:S(2)}) collective-permute-start(f32[632,512]{1,0:T(8,128)} %slice.30.refs_7_), channel_id=1, source_target_pairs={{0,1},{1,0},{2,3},{3,2},{4,5},{5,4},{6,7},{7,6},{8,9},{9,8},{10,11... | collective-permute-start | bytes 3883016 | tf_op jit(solution)/shard_map/ppermute | solution.py:18
  147.4 6.8 %collective-permute-start.15 = (f32[632,512]{1,0:T(8,128)}, f32[632,512]{1,0:T(8,128)S(1)}, u32[]{:S(2)}, u32[]{:S(2)}) collective-permute-start(f32[632,512]{1,0:T(8,128)} %collective-permute-done.13.refs_11_), channel_id=1, source_target_pairs={{0,1},{1,0},{2,3},{3,2},{4,5},{5,4},{6,7},{7,6},{8,9},{9,8},{10,11... | collective-permute-start | bytes 3883016 | tf_op jit(solution)/shard_map/ppermute | solution.py:18
  174.5 77.3 %all-to-all-start.2 = ((f32[32,16,1400]{2,1,0:T(8,128)}), f32[32,16,1400]{2,1,0:T(8,128)S(1)}, u32[]{:S(2)}, u32[]{:S(2)}) async-start(f32[32,16,1400]{2,1,0:T(8,128)} %bitcast.10), calls=%async_computation.2 | async-start | bytes 5767168 | tf_op jit(solution)/shard_map/all_to_all | solution.py:203
  (8 other events, 10.5 us)
Sparse Core Ops, SparseCore 0:
  16.9 48.5 all-gather.2

commit v10 on v2

--- a/solution.py
+++ b/solution.py
@@ -174,9 +174,11 @@
     here = jnp.broadcast_to(amplitudes[None, :, : 3 * part], (8, rows, 3 * part))
     here = lax.all_to_all(here, "z", split_axis=0, concat_axis=0, tiled=True).reshape(-1, 3 * part)
     ahead, behind = shift_x(here, -1), shift_x(here, 1)
-    half = here.shape[0] // 2
-    low, high = shift_x(ahead[:half], -1), shift_x(behind[half:], 1)
-    return [here, ahead, behind, low, high, last]
+    return [here, ahead, behind, last]
+
+
+def after(value, *others):
+    return lax.optimization_barrier((value, *others))[0]
 
 
 def on_device(amplitudes, integrals):
@@ -184,20 +186,25 @@
     rows = amplitudes.shape[0]
     columns = integrals.shape[1]
     spot = jnp.stack([2 * yh + core, x])
-    t = gather_amplitudes(amplitudes)
+    here, ahead, behind, last = gather_amplitudes(amplitudes)
 
     own = [integrals.T[:CUT], integrals.T[CUT:]]
     near, far = [swap_near(v) for v in own], [swap_far(v) for v in own]
     across = [swap_far(near[0]), swap_near(far[1])]
+    swapped = swap_core(near[1]), swap_core(far[1])
+    half = here.shape[0] // 2
+    low, high = shift_x(after(ahead[:half], *swapped), -1), shift_x(after(behind[half:], *swapped), 1)
+    t = [here, ahead, behind, low, high, last]
 
     def exchange(v):
         return lax.all_to_all(
             v.reshape(-1, rows, v.shape[1]), ("x", "z"), split_axis=0, concat_axis=0, tiled=True
         )
 
+    near2, far2 = (swap_core(near[0]), swapped[0]), (swap_core(far[0]), swapped[1])
     other_block = [
-        exchange(product(spot, t, [[n], [swap_core(n)], [f], [swap_core(f)]]))
-        for n, f in zip(near, far)
+        exchange(product(spot, t, [[n], [n2], [f], [f2]]))
+        for n, n2, f, f2 in zip(near, near2, far, far2)
     ]
     own2, across2 = [swap_core(v) for v in own], [swap_core(v) for v in across]
     own_block = exchange(product(spot, t, [own, own2, across, across2]))

time: 258 us -> 257 us (level)
  starting transfers between devices: 40.6 us -> 47.6 us
  waiting for transfers between devices: 141 us -> 136 us
  local copies, waits for them, and re-layouts: 17.7 us -> 13.9 us
    all_to_all x1, waiting for transfers between devices: 9.16 us -> 1.07 us  [gather_amplitudes(): lax.all_to_all(here, 'z', split_axis=0, concat_axis=0, tiled=True)]
    ppermute x3, waiting for transfers between devices: 6.91 us -> 14 us  [swap_far(): return lax.ppermute(value, ('yl', 'yh'), [(2, 1), (1, 2), (3, 0), (0, 3)])]
    ppermute x3, waiting for transfers between devices: 9.2 us -> 2.16 us  [swap_near(): return lax.ppermute(value, 'yl', [(0, 1), (1, 0)])]
    all_to_all x3, starting transfers between devices: 14.6 us -> 18.6 us  [exchange(): lax.all_to_all(v.reshape(-1, rows, v.shape[1]), ('x', 'z'), split_axis=0,...]
    ppermute x3, starting transfers between devices: 3.17 us -> 6.61 us  [swap_far(): return lax.ppermute(value, ('yl', 'yh'), [(2, 1), (1, 2), (3, 0), (0, 3)])]
    all_to_all x3, waiting for transfers between devices: 82.1 us -> 85.5 us  [exchange(): lax.all_to_all(v.reshape(-1, rows, v.shape[1]), ('x', 'z'), split_axis=0,...]
  transfers between devices with their start and end apart: 26 -> 26, of which waited for: 18 -> 16; matrix products, arithmetic and copies ran while one was open for 2% -> 1% of each run, Pallas kernels for 16% -> 16%
where the time goes in v10:
time: 257 us; the launch traced here: 255 us
  waiting for transfers between devices  136 us (53%)
  starting transfers between devices  47.6 us (19%)
  Pallas kernels  42.8 us (17%)
  local copies, waits for them, and re-layouts  13.9 us (5%)
  between operations  13.6 us (5%)
    all_to_all x3, waiting for transfers between devices, exchange(): lax.all_to_all(v.reshape(-1, rows, v.shape[1]), ('x', 'z'), split_axis=0,...  85.5 us
    pallas_call x3, Pallas kernels, product(): pl.pallas_call(functools.partial(product_kernel, counts), grid_spec=pltpu...  38.9 us
    ppermute x7, waiting for transfers between devices, shift_x(): return lax.ppermute(value, 'x', [(i, (i + by) % 4) for i in range(4)])  24.8 us
    all_to_all x3, starting transfers between devices, exchange(): lax.all_to_all(v.reshape(-1, rows, v.shape[1]), ('x', 'z'), split_axis=0,...  18.6 us
    ppermute x3, waiting for transfers between devices, swap_far(): return lax.ppermute(value, ('yl', 'yh'), [(2, 1), (1, 2), (3, 0), (0, 3)])  14 us
    ppermute x7, starting transfers between devices, shift_x(): return lax.ppermute(value, 'x', [(i, (i + by) % 4) for i in range(4)])  11.1 us
    unnamed x28, local copies, waits for them, and re-layouts  9.1 us
    all_to_all x1, starting transfers between devices, gather_amplitudes(): lax.all_to_all(here, 'z', split_axis=0, concat_axis=0, tiled=True)  7.7 us
  transfers between devices with their start and end apart: 26, of which 16 were waited for; matrix products, arithmetic and copies ran while one was open for 1% of the time, Pallas kernels for 16%

profile of v10, /device:TPU:24, one launch (start us, length us, event | category | flops | bytes accessed | tf_op | source)
XLA Modules:
  0.0 254.7 jit_solution(1768816150990621091)
XLA Ops:
  6.5 2.5 slice.25.refs_7_
  9.1 2.0 collective-permute-start.4
  12.0 7.7 %all-to-all-start = ((f32[8,16,1536]{2,1,0:T(8,128)}), f32[8,16,1536]{2,1,0:T(8,128)}, u32[]{:S(2)}, u32[]{:S(2)}) async-start(f32[8,16,1536]{2,1,0:T(8,128)} %broadcast_in_dim.2), calls=%async_computation | async-start | bytes 1572864 | tf_op jit(solution)/shard_map/all_to_all | solution.py:175
  19.7 1.6 collective-permute-start.10
  21.3 2.7 %collective-permute-start.9 = (f32[16,512]{1,0:T(8,128)S(1)}, f32[16,512]{1,0:T(8,128)S(1)}, u32[]{:S(2)}, u32[]{:S(2)}) collective-permute-start(f32[16,512]{1,0:T(8,128)S(1)} %slice.22), channel_id=1, source_target_pairs={{0,64},{32,96},{64,0},{96,32},{1,65},{33,97},{65,1},{97,33},{2,66}... | collective-permute-start | bytes 98312 | tf_op jit(solution)/shard_map/ppermute | solution.py:22
  24.0 1.4 collective-permute-start.8
  28.6 12.1 %collective-permute-done.4.refs_8_ = f32[632,512]{1,0:T(8,128)} collective-permute-done((f32[632,512]{1,0:T(8,128)}, f32[632,512]{1,0:T(8,128)}, u32[]{:S(2)}, u32[]{:S(2)}) %collective-permute-start.4) | collective-permute-done | bytes 1294368 | tf_op jit(solution)/shard_map/ppermute | solution.py:30
  42.3 1.5 collective-permute-start.1
  43.8 1.7 collective-permute-start
  46.8 2.3 collective-permute-start.19
  49.2 14.1 %collective-permute-done.1.refs_2_ = f32[128,1536]{1,0:T(8,128)S(1)} collective-permute-done((f32[128,1536]{1,0:T(8,128)}, f32[128,1536]{1,0:T(8,128)S(1)}, u32[]{:S(2)}, u32[]{:S(2)}) %collective-permute-start.1) | collective-permute-done | bytes 786464 | tf_op jit(solution)/shard_map/ppermute | solution.py:22
  64.4 1.9 collective-permute-start.6
  67.2 1.7 all-gather.3.cloned.1.call-done
  68.9 5.5 %collective-permute-done.6.refs_3_ = f32[64,1536]{1,0:T(8,128)S(1)} collective-permute-done((f32[64,1536]{1,0:T(8,128)S(1)}, f32[64,1536]{1,0:T(8,128)S(1)}, u32[]{:S(2)}, u32[]{:S(2)}) %collective-permute-start.6) | collective-permute-done | bytes 393248 | tf_op jit(solution)/shard_map/ppermute | solution.py:22
  74.4 2.8 %collective-permute-done.7.refs_4_ = f32[64,1536]{1,0:T(8,128)S(1)} collective-permute-done((f32[64,1536]{1,0:T(8,128)S(1)}, f32[64,1536]{1,0:T(8,128)S(1)}, u32[]{:S(2)}, u32[]{:S(2)}) %collective-permute-start.7) | collective-permute-done | bytes 393248 | tf_op jit(solution)/shard_map/ppermute | solution.py:22
  78.0 10.7 %shard_map.30 = f32[512,632]{1,0:T(8,128)} custom-call(s32[2]{0:T(128)} %pad_add_fusion.place_ref, f32[128,1536]{1,0:T(8,128)} %bitcast.3.refs_0_, f32[128,1536]{1,0:T(8,128)} %copy-done.7, f32[128,1536]{1,0:T(8,128)} %copy-done.6, f32[64,1536]{1,0:T(8,128)} %copy-done.12, f32[64,1536]{1,0:T(8,128)} %copy-done.13, f32[8,4,16,512]{3,2,1,0:T(8,128)} %bitcast.15, ...), custom_call_target="tpu_custom_call" | custom-call | flops 3976200192 | bytes 10665984 | tf_op jit(solution)/shard_map/pallas_call | solution.py:113
  88.6 7.9 %all-to-all-start.3 = ((f32[32,16,632]{2,1,0:T(8,128)}), f32[32,16,632]{2,1,0:T(8,128)S(1)}, u32[]{:S(2)}, u32[]{:S(2)}) async-start(f32[32,16,632]{2,1,0:T(8,128)} %bitcast.14), calls=%async_computation.3 | async-start | bytes 2621440 | tf_op jit(solution)/shard_map/all_to_all | solution.py:200
  96.9 2.2 collective-permute-done.13.refs_6_
  99.0 2.3 collective-permute-start.14
  102.6 10.8 %shard_map.29 = f32[512,768]{1,0:T(8,128)} custom-call(s32[2]{0:T(128)} %pad_add_fusion.place_ref, f32[128,1536]{1,0:T(8,128)} %bitcast.3.refs_0_, f32[128,1536]{1,0:T(8,128)} %copy-done.7, f32[128,1536]{1,0:T(8,128)} %copy-done.6, f32[64,1536]{1,0:T(8,128)} %copy-done.12, f32[64,1536]{1,0:T(8,128)} %copy-done.13, f32[8,4,16,512]{3,2,1,0:T(8,128)} %bitcast.16, ...), custom_call_target="tpu_custom_call" | custom-call | flops 4831838208 | bytes 12058624 | tf_op jit(solution)/shard_map/pallas_call | solution.py:113
  113.5 15.1 %all-to-all-done.3.refs_1_ = f32[32,16,632]{2,1,0:T(8,128)S(1)} async-done(((f32[32,16,632]{2,1,0:T(8,128)}), f32[32,16,632]{2,1,0:T(8,128)S(1)}, u32[]{:S(2)}, u32[]{:S(2)}) %all-to-all-start.3) | async-done | bytes 1294368 | tf_op jit(solution)/shard_map/all_to_all | solution.py:200
  129.6 5.5 %all-to-all-start.2 = ((f32[32,16,768]{2,1,0:T(8,128)}), f32[32,16,768]{2,1,0:T(8,128)S(1)}, u32[]{:S(2)}, u32[]{:S(2)}) async-start(f32[32,16,768]{2,1,0:T(8,128)} %bitcast.13), calls=%async_computation.2 | async-start | bytes 3145728 | tf_op jit(solution)/shard_map/all_to_all | solution.py:200
  135.3 1.9 collective-permute-done.14.refs_10_
  137.7 5.3 %collective-permute-done.12.refs_9_ = f32[632,512]{1,0:T(8,128)S(1)} collective-permute-done((f32[632,512]{1,0:T(8,128)}, f32[632,512]{1,0:T(8,128)S(1)}, u32[]{:S(2)}, u32[]{:S(2)}) %collective-permute-start.12) | collective-permute-done | bytes 1294368 | tf_op jit(solution)/shard_map/ppermute | solution.py:18
  147.2 17.4 %shard_map.28 = f32[512,1400]{1,0:T(8,128)} custom-call(s32[2]{0:T(128)} %pad_add_fusion.place_ref, f32[128,1536]{1,0:T(8,128)} %bitcast.3.refs_0_, f32[128,1536]{1,0:T(8,128)} %copy-done.7, f32[128,1536]{1,0:T(8,128)} %copy-done.6, f32[64,1536]{1,0:T(8,128)} %copy-done.12, f32[64,1536]{1,0:T(8,128)} %copy-done.13, f32[8,4,16,512]{3,2,1,0:T(8,128)} %bitcast.17, ...), custom_call_target="tpu_custom_call" | custom-call | flops 8808038400 | bytes 18530304 | tf_op jit(solution)/shard_map/pallas_call | solution.py:113
  164.6 8.2 %all-to-all-done.2.refs_0_ = f32[32,16,768]{2,1,0:T(8,128)S(1)} async-done(((f32[32,16,768]{2,1,0:T(8,128)}), f32[32,16,768]{2,1,0:T(8,128)S(1)}, u32[]{:S(2)}, u32[]{:S(2)}) %all-to-all-start.2) | async-done | bytes 1572896 | tf_op jit(solution)/shard_map/all_to_all | solution.py:200
  173.9 5.1 %all-to-all-start.1 = ((f32[32,16,1400]{2,1,0:T(8,128)}), f32[32,16,1400]{2,1,0:T(8,128)S(1)}, u32[]{:S(2)}, u32[]{:S(2)}) async-start(f32[32,16,1400]{2,1,0:T(8,128)} %bitcast.10), calls=%async_computation.1 | async-start | bytes 5767168 | tf_op jit(solution)/shard_map/all_to_all | solution.py:200
  179.0 1.4 copy-done.1
  180.4 1.3 copy-done.3
  181.8 2.0 shard_map.31.refs_1_
  183.7 62.2 %all-to-all-done.1.refs_0_ = f32[32,16,1400]{2,1,0:T(8,128)S(1)} async-done(((f32[32,16,1400]{2,1,0:T(8,128)}), f32[32,16,1400]{2,1,0:T(8,128)S(1)}, u32[]{:S(2)}, u32[]{:S(2)}) %all-to-all-start.1) | async-done | bytes 2867232 | tf_op jit(solution)/shard_map/all_to_all | solution.py:200
  245.9 2.0 shard_map.32
  (64 shorter events, 18.4 us)
Async XLA Ops:
  6.5 4.5 %slice-start = ((f32[16,2048]{1,0:T(8,128)}), f32[16,1536]{1,0:T(8,128)S(1)}, s32[]{:S(2)}) async-start(f32[16,2048]{1,0:T(8,128)} %param.2), calls=%async_computation.5 | async-start | bytes 196608 | tf_op jit(solution)/shard_map/slice | solution.py:174
  6.5 13.2 %copy-start.5 = (f32[16,2048]{1,0:T(8,128)S(1)}, f32[16,2048]{1,0:T(8,128)}, u32[]{:S(2)}) copy-start(f32[16,2048]{1,0:T(8,128)} %param.2) | copy-start | bytes 393220
  9.1 36.5 %copy-start.4 = (f32[512,1400]{0,1:T(8,128)S(1)}, f32[512,1400]{0,1:T(8,128)}, u32[]{:S(2)}) copy-start(f32[512,1400]{0,1:T(8,128)} %param.3) | copy-start | bytes 8601604
  9.1 31.7 %collective-permute-start.4 = (f32[632,512]{1,0:T(8,128)}, f32[632,512]{1,0:T(8,128)}, u32[]{:S(2)}, u32[]{:S(2)}) collective-permute-start(f32[632,512]{1,0:T(8,128)} %slice.25.refs_7_), channel_id=1, source_target_pairs={{128,2},{2,128},{130,0},{0,130},{129,3},{3,129},{131,1},{1,131},{1... | collective-permute-start | bytes 3883016 | tf_op jit(solution)/shard_map/ppermute | solution.py:30
  11.0 29.7 %collective-permute-start.2 = (f32[632,512]{1,0:T(8,128)}, f32[632,512]{1,0:T(8,128)}, u32[]{:S(2)}, u32[]{:S(2)}) collective-permute-start(f32[632,512]{1,0:T(8,128)} %slice.25.refs_7_), channel_id=1, source_target_pairs={{0,128},{128,0},{1,129},{129,1},{2,130},{130,2},{3,131},{131,3},{4... | collective-permute-start | bytes 3883016 | tf_op jit(solution)/shard_map/ppermute | solution.py:26
  12.0 30.4 %all-to-all-start = ((f32[8,16,1536]{2,1,0:T(8,128)}), f32[8,16,1536]{2,1,0:T(8,128)}, u32[]{:S(2)}, u32[]{:S(2)}) async-start(f32[8,16,1536]{2,1,0:T(8,128)} %broadcast_in_dim.2), calls=%async_computation | async-start | bytes 1572864 | tf_op jit(solution)/shard_map/all_to_all | solution.py:175
  19.7 49.2 %all-gather.3.cloned.1.call-start = ((), (), s32[]{:S(2)}) async-start(), calls=%async_computation.4 | async-start | bytes 1179648 | tf_op jit(solution)/shard_map/all_gather | solution.py:173
  19.7 5.7 %collective-permute-start.10 = (f32[16,512]{1,0:T(8,128)S(1)}, f32[16,512]{1,0:T(8,128)S(1)}, u32[]{:S(2)}, u32[]{:S(2)}) collective-permute-start(f32[16,512]{1,0:T(8,128)S(1)} %slice.22), channel_id=1, source_target_pairs={{0,32},{32,64},{64,96},{96,0},{1,33},{33,65},{65,97},{97,1},{2,34}... | collective-permute-start | bytes 98312 | tf_op jit(solution)/shard_map/ppermute | solution.py:22
  21.3 5.4 %collective-permute-start.9 = (f32[16,512]{1,0:T(8,128)S(1)}, f32[16,512]{1,0:T(8,128)S(1)}, u32[]{:S(2)}, u32[]{:S(2)}) collective-permute-start(f32[16,512]{1,0:T(8,128)S(1)} %slice.22), channel_id=1, source_target_pairs={{0,64},{32,96},{64,0},{96,32},{1,65},{33,97},{65,1},{97,33},{2,66}... | collective-permute-start | bytes 98312 | tf_op jit(solution)/shard_map/ppermute | solution.py:22
  24.0 3.9 %collective-permute-start.8 = (f32[16,512]{1,0:T(8,128)S(1)}, f32[16,512]{1,0:T(8,128)S(1)}, u32[]{:S(2)}, u32[]{:S(2)}) collective-permute-start(f32[16,512]{1,0:T(8,128)S(1)} %slice.22), channel_id=1, source_target_pairs={{0,96},{32,0},{64,32},{96,64},{1,97},{33,1},{65,33},{97,65},{2,98}... | collective-permute-start | bytes 98312 | tf_op jit(solution)/shard_map/ppermute | solution.py:22
  40.8 23.7 %collective-permute-start.5 = (f32[632,512]{1,0:T(8,128)}, f32[632,512]{1,0:T(8,128)}, u32[]{:S(2)}, u32[]{:S(2)}) collective-permute-start(f32[632,512]{1,0:T(8,128)} %collective-permute-done.4.refs_8_), channel_id=1, source_target_pairs={{0,1},{1,0},{2,3},{3,2},{4,5},{5,4},{6,7},{7,6},{8,9},{9,8},{10,11... | collective-permute-start | bytes 3883016 | tf_op jit(solution)/shard_map/ppermute | solution.py:18
  40.8 23.7 %collective-permute-start.3 = (f32[632,512]{1,0:T(8,128)}, f32[632,512]{1,0:T(8,128)}, u32[]{:S(2)}, u32[]{:S(2)}) collective-permute-start(f32[632,512]{1,0:T(8,128)} %collective-permute-done.2.refs_6_), channel_id=1, source_target_pairs={{0,1},{1,0},{2,3},{3,2},{4,5},{5,4},{6,7},{7,6},{8,9},{9,8},{10,11... | collective-permute-start | bytes 3883016 | tf_op jit(solution)/shard_map/ppermute | solution.py:18
  42.3 20.9 %collective-permute-start.1 = (f32[128,1536]{1,0:T(8,128)}, f32[128,1536]{1,0:T(8,128)S(1)}, u32[]{:S(2)}, u32[]{:S(2)}) collective-permute-start(f32[128,1536]{1,0:T(8,128)} %bitcast.3.refs_0_), channel_id=1, source_target_pairs={{0,32},{32,64},{64,96},{96,0},{1,33},{33,65},{65,97},{97,1},{2,34}... | collective-permute-start | bytes 2359304 | tf_op jit(solution)/shard_map/ppermute | solution.py:22
  43.8 20.5 %collective-permute-start = (f32[128,1536]{1,0:T(8,128)}, f32[128,1536]{1,0:T(8,128)S(1)}, u32[]{:S(2)}, u32[]{:S(2)}) collective-permute-start(f32[128,1536]{1,0:T(8,128)} %bitcast.3.refs_0_), channel_id=1, source_target_pairs={{0,96},{32,0},{64,32},{96,64},{1,97},{33,1},{65,33},{97,65},{2,98}... | collective-permute-start | bytes 2359304 | tf_op jit(solution)/shard_map/ppermute | solution.py:22
  46.8 49.7 %collective-permute-start.19 = (f32[768,512]{1,0:T(8,128)}, f32[768,512]{1,0:T(8,128)}, u32[]{:S(2)}, u32[]{:S(2)}) collective-permute-start(f32[768,512]{1,0:T(8,128)} %slice.27.refs_6_), channel_id=1, source_target_pairs={{128,2},{2,128},{130,0},{0,130},{129,3},{3,129},{131,1},{1,131},{1... | collective-permute-start | bytes 4718600 | tf_op jit(solution)/shard_map/ppermute | solution.py:30
  63.2 3.3 %copy-start.6 = (f32[128,1536]{1,0:T(8,128)}, f32[128,1536]{1,0:T(8,128)S(1)}, u32[]{:S(2)}) copy-start(f32[128,1536]{1,0:T(8,128)S(1)} %collective-permute-done.1.refs_2_) | copy-start | bytes 2359300
  63.2 35.8 %collective-permute-start.13 = (f32[768,512]{1,0:T(8,128)}, f32[768,512]{1,0:T(8,128)S(1)}, u32[]{:S(2)}, u32[]{:S(2)}) collective-permute-start(f32[768,512]{1,0:T(8,128)} %slice.27.refs_6_), channel_id=1, source_target_pairs={{0,128},{128,0},{1,129},{129,1},{2,130},{130,2},{3,131},{131,3},{4... | collective-permute-start | bytes 4718600 | tf_op jit(solution)/shard_map/ppermute | solution.py:26
  64.4 10.0 %collective-permute-start.6 = (f32[64,1536]{1,0:T(8,128)S(1)}, f32[64,1536]{1,0:T(8,128)S(1)}, u32[]{:S(2)}, u32[]{:S(2)}) collective-permute-start(f32[64,1536]{1,0:T(8,128)S(1)} %slice.24), channel_id=1, source_target_pairs={{0,96},{32,0},{64,32},{96,64},{1,97},{33,1},{65,33},{97,65},{2,98}... | collective-permute-start | bytes 1179656 | tf_op jit(solution)/shard_map/ppermute | solution.py:22
  66.3 10.9 %collective-permute-start.7 = (f32[64,1536]{1,0:T(8,128)S(1)}, f32[64,1536]{1,0:T(8,128)S(1)}, u32[]{:S(2)}, u32[]{:S(2)}) collective-permute-start(f32[64,1536]{1,0:T(8,128)S(1)} %slice.26), channel_id=1, source_target_pairs={{0,32},{32,64},{64,96},{96,0},{1,33},{33,65},{65,97},{97,1},{2,34}... | collective-permute-start | bytes 1179656 | tf_op jit(solution)/shard_map/ppermute | solution.py:22
  74.4 2.8 %copy-start.12 = (f32[64,1536]{1,0:T(8,128)}, f32[64,1536]{1,0:T(8,128)S(1)}, u32[]{:S(2)}) copy-start(f32[64,1536]{1,0:T(8,128)S(1)} %collective-permute-done.6.refs_3_) | copy-start | bytes 1179652
  88.6 40.0 %all-to-all-start.3 = ((f32[32,16,632]{2,1,0:T(8,128)}), f32[32,16,632]{2,1,0:T(8,128)S(1)}, u32[]{:S(2)}, u32[]{:S(2)}) async-start(f32[32,16,632]{2,1,0:T(8,128)} %bitcast.14), calls=%async_computation.3 | async-start | bytes 2621440 | tf_op jit(solution)/shard_map/all_to_all | solution.py:200
  96.6 5.9 %collective-permute-start.20 = (f32[768,512]{1,0:T(8,128)}, f32[768,512]{1,0:T(8,128)}, u32[]{:S(2)}, u32[]{:S(2)}) collective-permute-start(f32[768,512]{1,0:T(8,128)} %collective-permute-done.19.refs_8_), channel_id=1, source_target_pairs={{0,1},{1,0},{2,3},{3,2},{4,5},{5,4},{6,7},{7,6},{8,9},{9,8},{10,11... | collective-permute-start | bytes 4718600 | tf_op jit(solution)/shard_map/ppermute | solution.py:18
  99.0 3.6 %copy-start.8 = (f32[768,512]{1,0:T(8,128)}, f32[768,512]{1,0:T(8,128)S(1)}, u32[]{:S(2)}) copy-start(f32[768,512]{1,0:T(8,128)S(1)} %collective-permute-done.13.refs_6_) | copy-start | bytes 4718596
  99.0 3.6 %collective-permute-start.18 = (f32[768,512]{1,0:T(8,128)S(1)}, f32[768,512]{1,0:T(8,128)}, u32[]{:S(2)}, u32[]{:S(2)}) collective-permute-start(f32[768,512]{1,0:T(8,128)S(1)} %collective-permute-done.13.refs_6_), channel_id=1, source_target_pairs={{0,1},{1,0},{2,3},{3,2},{4,5},{5,4},{6,7},{7,6},{8,9},{9,8},{10,11... | collective-permute-start | bytes 4718600 | tf_op jit(solution)/shard_map/ppermute | solution.py:18
  99.0 38.1 %collective-permute-start.14 = (f32[768,512]{1,0:T(8,128)S(1)}, f32[768,512]{1,0:T(8,128)}, u32[]{:S(2)}, u32[]{:S(2)}) collective-permute-start(f32[768,512]{1,0:T(8,128)S(1)} %collective-permute-done.13.refs_6_), channel_id=1, source_target_pairs={{128,2},{2,128},{130,0},{0,130},{129,3},{3,129},{131,1},{1,131},{1... | collective-permute-start | bytes 4718600 | tf_op jit(solution)/shard_map/ppermute | solution.py:30
  101.3 36.3 %collective-permute-start.15 = (f32[632,512]{1,0:T(8,128)}, f32[632,512]{1,0:T(8,128)}, u32[]{:S(2)}, u32[]{:S(2)}) collective-permute-start(f32[632,512]{1,0:T(8,128)} %collective-permute-done.4.refs_8_), channel_id=1, source_target_pairs={{0,128},{128,0},{1,129},{129,1},{2,130},{130,2},{3,131},{131,3},{4... | collective-permute-start | bytes 3883016 | tf_op jit(solution)/shard_map/ppermute | solution.py:26
  129.6 43.1 %all-to-all-start.2 = ((f32[32,16,768]{2,1,0:T(8,128)}), f32[32,16,768]{2,1,0:T(8,128)S(1)}, u32[]{:S(2)}, u32[]{:S(2)}) async-start(f32[32,16,768]{2,1,0:T(8,128)} %bitcast.13), calls=%async_computation.2 | async-start | bytes 3145728 | tf_op jit(solution)/shard_map/all_to_all | solution.py:200
  135.2 7.8 %collective-permute-start.11 = (f32[768,512]{1,0:T(8,128)}, f32[768,512]{1,0:T(8,128)}, u32[]{:S(2)}, u32[]{:S(2)}) collective-permute-start(f32[768,512]{1,0:T(8,128)} %slice.27.refs_6_), channel_id=1, source_target_pairs={{0,1},{1,0},{2,3},{3,2},{4,5},{5,4},{6,7},{7,6},{8,9},{9,8},{10,11... | collective-permute-start | bytes 4718600 | tf_op jit(solution)/shard_map/ppermute | solution.py:18
  137.1 8.8 %collective-permute-start.16 = (f32[768,512]{1,0:T(8,128)}, f32[768,512]{1,0:T(8,128)S(1)}, u32[]{:S(2)}, u32[]{:S(2)}) collective-permute-start(f32[768,512]{1,0:T(8,128)} %collective-permute-done.14.refs_10_), channel_id=1, source_target_pairs={{0,1},{1,0},{2,3},{3,2},{4,5},{5,4},{6,7},{7,6},{8,9},{9,8},{10,11... | collective-permute-start | bytes 4718600 | tf_op jit(solution)/shard_map/ppermute | solution.py:18
  137.1 5.9 %collective-permute-start.12 = (f32[632,512]{1,0:T(8,128)}, f32[632,512]{1,0:T(8,128)S(1)}, u32[]{:S(2)}, u32[]{:S(2)}) collective-permute-start(f32[632,512]{1,0:T(8,128)} %slice.25.refs_7_), channel_id=1, source_target_pairs={{0,1},{1,0},{2,3},{3,2},{4,5},{5,4},{6,7},{7,6},{8,9},{9,8},{10,11... | collective-permute-start | bytes 3883016 | tf_op jit(solution)/shard_map/ppermute | solution.py:18
  137.7 7.2 %collective-permute-start.17 = (f32[632,512]{1,0:T(8,128)}, f32[632,512]{1,0:T(8,128)S(1)}, u32[]{:S(2)}, u32[]{:S(2)}) collective-permute-start(f32[632,512]{1,0:T(8,128)} %collective-permute-done.15.refs_11_), channel_id=1, source_target_pairs={{0,1},{1,0},{2,3},{3,2},{4,5},{5,4},{6,7},{7,6},{8,9},{9,8},{10,11... | collective-permute-start | bytes 3883016 | tf_op jit(solution)/shard_map/ppermute | solution.py:18
  173.9 72.0 %all-to-all-start.1 = ((f32[32,16,1400]{2,1,0:T(8,128)}), f32[32,16,1400]{2,1,0:T(8,128)S(1)}, u32[]{:S(2)}, u32[]{:S(2)}) async-start(f32[32,16,1400]{2,1,0:T(8,128)} %bitcast.10), calls=%async_computation.1 | async-start | bytes 5767168 | tf_op jit(solution)/shard_map/all_to_all | solution.py:200
  (9 other events, 11.3 us)
Sparse Core Ops, SparseCore 0:
  28.8 40.1 all-gather.2

commit v11 on v5

--- a/solution.py
+++ b/solution.py
@@ -191,12 +191,13 @@
     here = lax.all_to_all(here, "z", split_axis=0, concat_axis=0, tiled=True)
     last = lax.all_gather(last, "z", axis=0).reshape(8, 4, rows, half)
     ahead, behind = shift_x(here, -1), shift_x(here, 1)
-    low, high = shift_x(ahead[:4], -1), shift_x(behind[4:], 1)
+
+    first, second = integrals.T[:CUT], integrals.T[CUT:]
+    near, far = swap_near(first), swap_far(first)
+    near_next, far_next = swap_near(second), swap_far(second)
+    swapped = swap_core(near_next), swap_core(far_next)
+    low, high = shift_x(after(ahead[:4], *swapped), -1), shift_x(after(behind[4:], *swapped), 1)
     t = (here, ahead, low, high, behind, last)
-
-    first, second = after(integrals.T[:CUT], low, high), integrals.T[CUT:]
-    near, far = after((swap_near(first), swap_far(first)), ahead, behind)
-    near_next, far_next = after((swap_near(second), swap_far(second)), ahead, behind)
 
     def exchange(v):
         return lax.all_to_all(
@@ -205,7 +206,7 @@
 
     (result,) = product(spot, t, [[near], [swap_core(near)], [far], [swap_core(far)]])
     (result_next,) = product(
-        spot, t, [[near_next], [swap_core(near_next)], [far_next], [swap_core(far_next)]]
+        spot, t, [[near_next], [swapped[0]], [far_next], [swapped[1]]]
     )
     other_block = [exchange(result), exchange(result_next)]
     across = [swap_far(near), swap_near(far_next)]

time: 262 us -> 258 us (0.985)
  starting transfers between devices: 51.4 us -> 47.6 us
  local copies, waits for them, and re-layouts: 14.9 us -> 11.3 us
    all_to_all x3, waiting for transfers between devices: 66.8 us -> 85.7 us  [exchange(): lax.all_to_all(v.reshape(-1, rows, v.shape[1]), ('x', 'z'), split_axis=0,...]
    all_to_all x1, waiting for transfers between devices: 16.5 us -> 1.01 us  [on_device(): here = lax.all_to_all(here, 'z', split_axis=0, concat_axis=0, tiled=True)]
    ppermute x3, waiting for transfers between devices: 34.4 us -> 22.2 us  [swap_far(): return lax.ppermute(value, ('yl', 'yh'), [(2, 1), (1, 2), (3, 0), (0, 3)])]
    ppermute x7, waiting for transfers between devices: 7.74 us -> 16.3 us  [shift_x(): return lax.ppermute(value, 'x', [(i, (i + by) % 4) for i in range(4)])]
    all_to_all x3, starting transfers between devices: 24.5 us -> 20 us  [exchange(): lax.all_to_all(v.reshape(-1, rows, v.shape[1]), ('x', 'z'), split_axis=0,...]
    unnamed x28 -> x22, local copies, waits for them, and re-layouts: 9.26 us -> 5.69 us
  transfers between devices with their start and end apart: 26 -> 26, of which waited for: 16 -> 16; matrix products, arithmetic and copies ran while one was open for 2% -> 2% of each run, Pallas kernels for 16% -> 17%
where the time goes in v11:
time: 258 us; the launch traced here: 256 us
  waiting for transfers between devices  137 us (53%)
  starting transfers between devices  47.6 us (18%)
  Pallas kernels  44.9 us (17%)
  between operations  13.6 us (5%)
  local copies, waits for them, and re-layouts  11.3 us (4%)
    all_to_all x3, waiting for transfers between devices, exchange(): lax.all_to_all(v.reshape(-1, rows, v.shape[1]), ('x', 'z'), split_axis=0,...  85.7 us
    pallas_call x3, Pallas kernels, product(): pl.pallas_call(functools.partial(product_kernel, around, counts), grid_sp...  40.9 us
    ppermute x3, waiting for transfers between devices, swap_far(): return lax.ppermute(value, ('yl', 'yh'), [(2, 1), (1, 2), (3, 0), (0, 3)])  22.2 us
    all_to_all x3, starting transfers between devices, exchange(): lax.all_to_all(v.reshape(-1, rows, v.shape[1]), ('x', 'z'), split_axis=0,...  20 us
    ppermute x7, waiting for transfers between devices, shift_x(): return lax.ppermute(value, 'x', [(i, (i + by) % 4) for i in range(4)])  16.3 us
    ppermute x7, starting transfers between devices, shift_x(): return lax.ppermute(value, 'x', [(i, (i + by) % 4) for i in range(4)])  11.9 us
    ppermute x8, waiting for transfers between devices, swap_core(): return lax.ppermute(value, 'core', [(0, 1), (1, 0)])  9.07 us
    all_to_all x1, starting transfers between devices, on_device(): here = lax.all_to_all(here, 'z', split_axis=0, concat_axis=0, tiled=True)  8.47 us
  transfers between devices with their start and end apart: 26, of which 16 were waited for; matrix products, arithmetic and copies ran while one was open for 2% of the time, Pallas kernels for 17%

profile of v11, /device:TPU:24, one launch (start us, length us, event | category | flops | bytes accessed | tf_op | source)
XLA Modules:
  0.0 255.6 jit_solution(11751386122399764655)
XLA Ops:
  7.4 1.6 collective-permute-start.2
  9.0 2.7 %collective-permute-start.1 = (f32[16,1024]{1,0:T(8,128)S(1)}, f32[16,1024]{1,0:T(8,128)S(1)}, u32[]{:S(2)}, u32[]{:S(2)}) collective-permute-start(f32[16,1024]{1,0:T(8,128)S(1)} %get-tuple-element.13), channel_id=1, source_target_pairs={{0,64},{32,96},{64,0},{96,32},{1,65},{33,97},{65,1},{97,33},{2,66}... | collective-permute-start | bytes 196616 | tf_op jit(solution)/shard_map/ppermute | solution.py:22
  11.7 1.4 collective-permute-start
  13.6 1.4 collective-permute-done.1
  16.7 2.6 %slice.28.refs_7_ = f32[632,512]{1,0:T(8,128)} slice(f32[1400,512]{1,0:T(8,128)} %bitcast.11), slice={[768:1400], [0:512]} | slice | bytes 2588672 | tf_op jit(solution)/shard_map/slice | solution.py:195
  21.4 8.5 %all-to-all-start = ((f32[8,16,1024]{2,1,0:T(8,128)}), f32[8,16,1024]{2,1,0:T(8,128)S(1)}, u32[]{:S(2)}, u32[]{:S(2)}) async-start(f32[8,16,1024]{2,1,0:T(8,128)} %broadcast_in_dim.2), calls=%async_computation | async-start | bytes 1048576 | tf_op jit(solution)/shard_map/all_to_all | solution.py:191
  29.8 20.0 %collective-permute-done.6.refs_8_ = f32[632,512]{1,0:T(8,128)} collective-permute-done((f32[632,512]{1,0:T(8,128)}, f32[632,512]{1,0:T(8,128)}, u32[]{:S(2)}, u32[]{:S(2)}) %collective-permute-start.6) | collective-permute-done | bytes 1294368 | tf_op jit(solution)/shard_map/ppermute | solution.py:30
  51.4 3.2 %collective-permute-start.3 = (f32[8,16,1024]{2,1,0:T(8,128)S(1)}, f32[8,16,1024]{2,1,0:T(8,128)S(1)}, u32[]{:S(2)}, u32[]{:S(2)}) collective-permute-start(f32[8,16,1024]{2,1,0:T(8,128)S(1)} %all-to-all-done.refs_0_), channel_id=1, source_target_pairs={{0,96},{32,0},{64,32},{96,64},{1,97},{33,1},{65,33},{97,65},{2,98}... | collective-permute-start | bytes 1572872 | tf_op jit(solution)/shard_map/ppermute | solution.py:22
  54.6 1.3 slice.30.refs_6_
  55.9 3.1 %collective-permute-start.19 = (f32[768,512]{1,0:T(8,128)}, f32[768,512]{1,0:T(8,128)}, u32[]{:S(2)}, u32[]{:S(2)}) collective-permute-start(f32[768,512]{1,0:T(8,128)} %slice.30.refs_6_), channel_id=1, source_target_pairs={{128,2},{2,128},{130,0},{0,130},{129,3},{3,129},{131,1},{1,131},{1... | collective-permute-start | bytes 4718600 | tf_op jit(solution)/shard_map/ppermute | solution.py:30
  59.0 6.5 %collective-permute-done.9.refs_4_ = f32[8,16,1024]{2,1,0:T(8,128)S(1)} collective-permute-done((f32[8,16,1024]{2,1,0:T(8,128)S(1)}, f32[8,16,1024]{2,1,0:T(8,128)S(1)}, u32[]{:S(2)}, u32[]{:S(2)}) %collective-permute-start.9) | collective-permute-done | bytes 524320 | tf_op jit(solution)/shard_map/ppermute | solution.py:22
  65.6 3.0 %collective-permute-start.8 = (f32[4,16,1024]{2,1,0:T(8,128)S(1)}, f32[4,16,1024]{2,1,0:T(8,128)S(1)}, u32[]{:S(2)}, u32[]{:S(2)}) collective-permute-start(f32[4,16,1024]{2,1,0:T(8,128)S(1)} %slice.27), channel_id=1, source_target_pairs={{0,96},{32,0},{64,32},{96,64},{1,97},{33,1},{65,33},{97,65},{2,98}... | collective-permute-start | bytes 786440 | tf_op jit(solution)/shard_map/ppermute | solution.py:22
  69.2 3.3 %collective-permute-done.8.refs_2_ = f32[4,16,1024]{2,1,0:T(8,128)S(1)} collective-permute-done((f32[4,16,1024]{2,1,0:T(8,128)S(1)}, f32[4,16,1024]{2,1,0:T(8,128)S(1)}, u32[]{:S(2)}, u32[]{:S(2)}) %collective-permute-start.8) | collective-permute-done | bytes 262176 | tf_op jit(solution)/shard_map/ppermute | solution.py:22
  72.5 3.7 %collective-permute-done.10.refs_3_ = f32[4,16,1024]{2,1,0:T(8,128)S(1)} collective-permute-done((f32[4,16,1024]{2,1,0:T(8,128)S(1)}, f32[4,16,1024]{2,1,0:T(8,128)S(1)}, u32[]{:S(2)}, u32[]{:S(2)}) %collective-permute-start.10) | collective-permute-done | bytes 262176 | tf_op jit(solution)/shard_map/ppermute | solution.py:22
  76.9 11.3 %shard_map.29 = f32[512,632]{1,0:T(8,128)} custom-call(s32[3]{0:T(128)} %pad_add_fusion.place_ref, f32[8,16,1024]{2,1,0:T(8,128)} %copy-done.5, f32[8,16,1024]{2,1,0:T(8,128)} %copy-done.7, f32[4,16,1024]{2,1,0:T(8,128)} %copy-done.9, f32[4,16,1024]{2,1,0:T(8,128)} %copy-done.10, f32[8,16,1024]{2,1,0:T(8,128)} %copy-done.6, f32[8,4,16,1024]{3,2,1,0:T(8,128)} %bitcast.15, ...), custom_call_target="tpu_custom_call" | custom-call | flops 3976200192 | bytes 10665984 | tf_op jit(solution)/shard_map/pallas_call | solution.py:122
  88.2 9.5 %all-to-all-start.1 = ((f32[32,16,632]{2,1,0:T(8,128)}), f32[32,16,632]{2,1,0:T(8,128)S(1)}, u32[]{:S(2)}, u32[]{:S(2)}) async-start(f32[32,16,632]{2,1,0:T(8,128)} %bitcast.14), calls=%async_computation.1 | async-start | bytes 2621440 | tf_op jit(solution)/shard_map/all_to_all | solution.py:203
  97.8 2.6 %collective-permute-done.13.refs_6_ = f32[768,512]{1,0:T(8,128)} collective-permute-done((f32[768,512]{1,0:T(8,128)}, f32[768,512]{1,0:T(8,128)}, u32[]{:S(2)}, u32[]{:S(2)}) %collective-permute-start.13) | collective-permute-done | bytes 1572896 | tf_op jit(solution)/shard_map/ppermute | solution.py:26
  102.0 2.1 collective-permute-done.18.refs_7_
  104.1 11.6 %shard_map.30 = f32[512,768]{1,0:T(8,128)} custom-call(s32[3]{0:T(128)} %pad_add_fusion.place_ref, f32[8,16,1024]{2,1,0:T(8,128)} %copy-done.5, f32[8,16,1024]{2,1,0:T(8,128)} %copy-done.7, f32[4,16,1024]{2,1,0:T(8,128)} %copy-done.9, f32[4,16,1024]{2,1,0:T(8,128)} %copy-done.10, f32[8,16,1024]{2,1,0:T(8,128)} %copy-done.6, f32[8,4,16,1024]{3,2,1,0:T(8,128)} %bitcast.16, ...), custom_call_target="tpu_custom_call" | custom-call | flops 4831838208 | bytes 12058624 | tf_op jit(solution)/shard_map/pallas_call | solution.py:122
  115.7 13.9 %all-to-all-done.1.refs_1_ = f32[32,16,632]{2,1,0:T(8,128)S(1)} async-done(((f32[32,16,632]{2,1,0:T(8,128)}), f32[32,16,632]{2,1,0:T(8,128)S(1)}, u32[]{:S(2)}, u32[]{:S(2)}) %all-to-all-start.1) | async-done | bytes 1294368 | tf_op jit(solution)/shard_map/all_to_all | solution.py:203
  130.8 5.5 %all-to-all-start.3 = ((f32[32,16,768]{2,1,0:T(8,128)}), f32[32,16,768]{2,1,0:T(8,128)S(1)}, u32[]{:S(2)}, u32[]{:S(2)}) async-start(f32[32,16,768]{2,1,0:T(8,128)} %bitcast.13), calls=%async_computation.3 | async-start | bytes 3145728 | tf_op jit(solution)/shard_map/all_to_all | solution.py:203
  136.4 2.2 collective-permute-done.14.refs_10_
  139.1 4.7 %collective-permute-done.12.refs_9_ = f32[632,512]{1,0:T(8,128)} collective-permute-done((f32[632,512]{1,0:T(8,128)}, f32[632,512]{1,0:T(8,128)}, u32[]{:S(2)}, u32[]{:S(2)}) %collective-permute-start.12) | collective-permute-done | bytes 1294368 | tf_op jit(solution)/shard_map/ppermute | solution.py:18
  143.9 2.2 collective-permute-done.17.refs_13_
  146.1 18.0 %shard_map.28 = f32[512,1400]{1,0:T(8,128)} custom-call(s32[3]{0:T(128)} %pad_add_fusion.place_ref, f32[8,16,1024]{2,1,0:T(8,128)} %copy-done.5, f32[8,16,1024]{2,1,0:T(8,128)} %copy-done.7, f32[4,16,1024]{2,1,0:T(8,128)} %copy-done.9, f32[4,16,1024]{2,1,0:T(8,128)} %copy-done.10, f32[8,16,1024]{2,1,0:T(8,128)} %copy-done.6, f32[8,4,16,1024]{3,2,1,0:T(8,128)} %bitcast.17, ...), custom_call_target="tpu_custom_call" | custom-call | flops 8808038400 | bytes 18530304 | tf_op jit(solution)/shard_map/pallas_call | solution.py:122
  164.1 9.8 %all-to-all-done.3.refs_0_ = f32[32,16,768]{2,1,0:T(8,128)S(1)} async-done(((f32[32,16,768]{2,1,0:T(8,128)}), f32[32,16,768]{2,1,0:T(8,128)S(1)}, u32[]{:S(2)}, u32[]{:S(2)}) %all-to-all-start.3) | async-done | bytes 1572896 | tf_op jit(solution)/shard_map/all_to_all | solution.py:203
  175.0 5.1 %all-to-all-start.2 = ((f32[32,16,1400]{2,1,0:T(8,128)}), f32[32,16,1400]{2,1,0:T(8,128)S(1)}, u32[]{:S(2)}, u32[]{:S(2)}) async-start(f32[32,16,1400]{2,1,0:T(8,128)} %bitcast.10), calls=%async_computation.2 | async-start | bytes 5767168 | tf_op jit(solution)/shard_map/all_to_all | solution.py:203
  180.1 1.4 copy-done.1
  181.5 1.3 copy-done.3
  182.8 2.0 shard_map.31.refs_1_
  184.8 62.0 %all-to-all-done.2.refs_0_ = f32[32,16,1400]{2,1,0:T(8,128)S(1)} async-done(((f32[32,16,1400]{2,1,0:T(8,128)}), f32[32,16,1400]{2,1,0:T(8,128)S(1)}, u32[]{:S(2)}, u32[]{:S(2)}) %all-to-all-start.2) | async-done | bytes 2867232 | tf_op jit(solution)/shard_map/all_to_all | solution.py:203
  246.8 2.0 shard_map.32
  (56 shorter events, 12.6 us)
Async XLA Ops:
  6.5 69.6 %all-gather.3.cloned.1.call-start = ((), (), s32[]{:S(2)}) async-start(), calls=%async_computation.4 | async-start | bytes 2359296 | tf_op jit(solution)/shard_map/all_gather | solution.py:192
  7.4 6.1 %collective-permute-start.2 = (f32[16,1024]{1,0:T(8,128)S(1)}, f32[16,1024]{1,0:T(8,128)S(1)}, u32[]{:S(2)}, u32[]{:S(2)}) collective-permute-start(f32[16,1024]{1,0:T(8,128)S(1)} %get-tuple-element.13), channel_id=1, source_target_pairs={{0,32},{32,64},{64,96},{96,0},{1,33},{33,65},{65,97},{97,1},{2,34}... | collective-permute-start | bytes 196616 | tf_op jit(solution)/shard_map/ppermute | solution.py:22
  9.0 5.9 %collective-permute-start.1 = (f32[16,1024]{1,0:T(8,128)S(1)}, f32[16,1024]{1,0:T(8,128)S(1)}, u32[]{:S(2)}, u32[]{:S(2)}) collective-permute-start(f32[16,1024]{1,0:T(8,128)S(1)} %get-tuple-element.13), channel_id=1, source_target_pairs={{0,64},{32,96},{64,0},{96,32},{1,65},{33,97},{65,1},{97,33},{2,66}... | collective-permute-start | bytes 196616 | tf_op jit(solution)/shard_map/ppermute | solution.py:22
  11.7 4.3 %collective-permute-start = (f32[16,1024]{1,0:T(8,128)S(1)}, f32[16,1024]{1,0:T(8,128)S(1)}, u32[]{:S(2)}, u32[]{:S(2)}) collective-permute-start(f32[16,1024]{1,0:T(8,128)S(1)} %get-tuple-element.13), channel_id=1, source_target_pairs={{0,96},{32,0},{64,32},{96,64},{1,97},{33,1},{65,33},{97,65},{2,98}... | collective-permute-start | bytes 196616 | tf_op jit(solution)/shard_map/ppermute | solution.py:22
  16.7 37.9 %copy-start.4 = (f32[512,1400]{0,1:T(8,128)S(1)}, f32[512,1400]{0,1:T(8,128)}, u32[]{:S(2)}) copy-start(f32[512,1400]{0,1:T(8,128)} %param.3) | copy-start | bytes 8601604
  19.3 30.5 %collective-permute-start.6 = (f32[632,512]{1,0:T(8,128)}, f32[632,512]{1,0:T(8,128)}, u32[]{:S(2)}, u32[]{:S(2)}) collective-permute-start(f32[632,512]{1,0:T(8,128)} %slice.28.refs_7_), channel_id=1, source_target_pairs={{128,2},{2,128},{130,0},{0,130},{129,3},{3,129},{131,1},{1,131},{1... | collective-permute-start | bytes 3883016 | tf_op jit(solution)/shard_map/ppermute | solution.py:30
  19.8 30.0 %collective-permute-start.4 = (f32[632,512]{1,0:T(8,128)}, f32[632,512]{1,0:T(8,128)}, u32[]{:S(2)}, u32[]{:S(2)}) collective-permute-start(f32[632,512]{1,0:T(8,128)} %slice.28.refs_7_), channel_id=1, source_target_pairs={{0,128},{128,0},{1,129},{129,1},{2,130},{130,2},{3,131},{131,3},{4... | collective-permute-start | bytes 3883016 | tf_op jit(solution)/shard_map/ppermute | solution.py:26
  21.4 30.0 %all-to-all-start = ((f32[8,16,1024]{2,1,0:T(8,128)}), f32[8,16,1024]{2,1,0:T(8,128)S(1)}, u32[]{:S(2)}, u32[]{:S(2)}) async-start(f32[8,16,1024]{2,1,0:T(8,128)} %broadcast_in_dim.2), calls=%async_computation | async-start | bytes 1048576 | tf_op jit(solution)/shard_map/all_to_all | solution.py:191
  49.9 15.7 %collective-permute-start.7 = (f32[632,512]{1,0:T(8,128)}, f32[632,512]{1,0:T(8,128)}, u32[]{:S(2)}, u32[]{:S(2)}) collective-permute-start(f32[632,512]{1,0:T(8,128)} %collective-permute-done.6.refs_8_), channel_id=1, source_target_pairs={{0,1},{1,0},{2,3},{3,2},{4,5},{5,4},{6,7},{7,6},{8,9},{9,8},{10,11... | collective-permute-start | bytes 3883016 | tf_op jit(solution)/shard_map/ppermute | solution.py:18
  49.9 15.7 %collective-permute-start.5 = (f32[632,512]{1,0:T(8,128)}, f32[632,512]{1,0:T(8,128)}, u32[]{:S(2)}, u32[]{:S(2)}) collective-permute-start(f32[632,512]{1,0:T(8,128)} %collective-permute-done.4.refs_6_), channel_id=1, source_target_pairs={{0,1},{1,0},{2,3},{3,2},{4,5},{5,4},{6,7},{7,6},{8,9},{9,8},{10,11... | collective-permute-start | bytes 3883016 | tf_op jit(solution)/shard_map/ppermute | solution.py:18
  51.4 14.2 %copy-start.5 = (f32[8,16,1024]{2,1,0:T(8,128)}, f32[8,16,1024]{2,1,0:T(8,128)S(1)}, u32[]{:S(2)}) copy-start(f32[8,16,1024]{2,1,0:T(8,128)S(1)} %all-to-all-done.refs_0_) | copy-start | bytes 1572868
  51.4 14.1 %collective-permute-start.9 = (f32[8,16,1024]{2,1,0:T(8,128)S(1)}, f32[8,16,1024]{2,1,0:T(8,128)S(1)}, u32[]{:S(2)}, u32[]{:S(2)}) collective-permute-start(f32[8,16,1024]{2,1,0:T(8,128)S(1)} %all-to-all-done.refs_0_), channel_id=1, source_target_pairs={{0,32},{32,64},{64,96},{96,0},{1,33},{33,65},{65,97},{97,1},{2,34}... | collective-permute-start | bytes 1572872 | tf_op jit(solution)/shard_map/ppermute | solution.py:22
  51.4 14.2 %collective-permute-start.3 = (f32[8,16,1024]{2,1,0:T(8,128)S(1)}, f32[8,16,1024]{2,1,0:T(8,128)S(1)}, u32[]{:S(2)}, u32[]{:S(2)}) collective-permute-start(f32[8,16,1024]{2,1,0:T(8,128)S(1)} %all-to-all-done.refs_0_), channel_id=1, source_target_pairs={{0,96},{32,0},{64,32},{96,64},{1,97},{33,1},{65,33},{97,65},{2,98}... | collective-permute-start | bytes 1572872 | tf_op jit(solution)/shard_map/ppermute | solution.py:22
  55.9 41.8 %collective-permute-start.19 = (f32[768,512]{1,0:T(8,128)}, f32[768,512]{1,0:T(8,128)}, u32[]{:S(2)}, u32[]{:S(2)}) collective-permute-start(f32[768,512]{1,0:T(8,128)} %slice.30.refs_6_), channel_id=1, source_target_pairs={{128,2},{2,128},{130,0},{0,130},{129,3},{3,129},{131,1},{1,131},{1... | collective-permute-start | bytes 4718600 | tf_op jit(solution)/shard_map/ppermute | solution.py:30
  65.5 3.1 %copy-start.6 = (f32[8,16,1024]{2,1,0:T(8,128)}, f32[8,16,1024]{2,1,0:T(8,128)S(1)}, u32[]{:S(2)}) copy-start(f32[8,16,1024]{2,1,0:T(8,128)S(1)} %collective-permute-done.9.refs_4_) | copy-start | bytes 1572868
  65.5 34.9 %collective-permute-start.13 = (f32[768,512]{1,0:T(8,128)}, f32[768,512]{1,0:T(8,128)}, u32[]{:S(2)}, u32[]{:S(2)}) collective-permute-start(f32[768,512]{1,0:T(8,128)} %slice.30.refs_6_), channel_id=1, source_target_pairs={{0,128},{128,0},{1,129},{129,1},{2,130},{130,2},{3,131},{131,3},{4... | collective-permute-start | bytes 4718600 | tf_op jit(solution)/shard_map/ppermute | solution.py:26
  65.6 3.0 %copy-start.7 = (f32[8,16,1024]{2,1,0:T(8,128)}, f32[8,16,1024]{2,1,0:T(8,128)S(1)}, u32[]{:S(2)}) copy-start(f32[8,16,1024]{2,1,0:T(8,128)S(1)} %collective-permute-done.3.refs_1_) | copy-start | bytes 1572868
  65.6 6.9 %collective-permute-start.8 = (f32[4,16,1024]{2,1,0:T(8,128)S(1)}, f32[4,16,1024]{2,1,0:T(8,128)S(1)}, u32[]{:S(2)}, u32[]{:S(2)}) collective-permute-start(f32[4,16,1024]{2,1,0:T(8,128)S(1)} %slice.27), channel_id=1, source_target_pairs={{0,96},{32,0},{64,32},{96,64},{1,97},{33,1},{65,33},{97,65},{2,98}... | collective-permute-start | bytes 786440 | tf_op jit(solution)/shard_map/ppermute | solution.py:22
  68.6 7.6 %collective-permute-start.10 = (f32[4,16,1024]{2,1,0:T(8,128)S(1)}, f32[4,16,1024]{2,1,0:T(8,128)S(1)}, u32[]{:S(2)}, u32[]{:S(2)}) collective-permute-start(f32[4,16,1024]{2,1,0:T(8,128)S(1)} %slice.29), channel_id=1, source_target_pairs={{0,32},{32,64},{64,96},{96,0},{1,33},{33,65},{65,97},{97,1},{2,34}... | collective-permute-start | bytes 786440 | tf_op jit(solution)/shard_map/ppermute | solution.py:22
  72.5 3.7 %copy-start.9 = (f32[4,16,1024]{2,1,0:T(8,128)}, f32[4,16,1024]{2,1,0:T(8,128)S(1)}, u32[]{:S(2)}) copy-start(f32[4,16,1024]{2,1,0:T(8,128)S(1)} %collective-permute-done.8.refs_2_) | copy-start | bytes 786436
  88.2 41.5 %all-to-all-start.1 = ((f32[32,16,632]{2,1,0:T(8,128)}), f32[32,16,632]{2,1,0:T(8,128)S(1)}, u32[]{:S(2)}, u32[]{:S(2)}) async-start(f32[32,16,632]{2,1,0:T(8,128)} %bitcast.14), calls=%async_computation.1 | async-start | bytes 2621440 | tf_op jit(solution)/shard_map/all_to_all | solution.py:203
  97.7 4.4 %collective-permute-start.20 = (f32[768,512]{1,0:T(8,128)}, f32[768,512]{1,0:T(8,128)}, u32[]{:S(2)}, u32[]{:S(2)}) collective-permute-start(f32[768,512]{1,0:T(8,128)} %collective-permute-done.19.refs_8_), channel_id=1, source_target_pairs={{0,1},{1,0},{2,3},{3,2},{4,5},{5,4},{6,7},{7,6},{8,9},{9,8},{10,11... | collective-permute-start | bytes 4718600 | tf_op jit(solution)/shard_map/ppermute | solution.py:18
  100.4 3.8 %collective-permute-start.18 = (f32[768,512]{1,0:T(8,128)}, f32[768,512]{1,0:T(8,128)}, u32[]{:S(2)}, u32[]{:S(2)}) collective-permute-start(f32[768,512]{1,0:T(8,128)} %collective-permute-done.13.refs_6_), channel_id=1, source_target_pairs={{0,1},{1,0},{2,3},{3,2},{4,5},{5,4},{6,7},{7,6},{8,9},{9,8},{10,11... | collective-permute-start | bytes 4718600 | tf_op jit(solution)/shard_map/ppermute | solution.py:18
  100.4 38.2 %collective-permute-start.14 = (f32[768,512]{1,0:T(8,128)}, f32[768,512]{1,0:T(8,128)S(1)}, u32[]{:S(2)}, u32[]{:S(2)}) collective-permute-start(f32[768,512]{1,0:T(8,128)} %collective-permute-done.13.refs_6_), channel_id=1, source_target_pairs={{128,2},{2,128},{130,0},{0,130},{129,3},{3,129},{131,1},{1,131},{1... | collective-permute-start | bytes 4718600 | tf_op jit(solution)/shard_map/ppermute | solution.py:30
  100.9 38.2 %collective-permute-start.15 = (f32[632,512]{1,0:T(8,128)}, f32[632,512]{1,0:T(8,128)}, u32[]{:S(2)}, u32[]{:S(2)}) collective-permute-start(f32[632,512]{1,0:T(8,128)} %collective-permute-done.6.refs_8_), channel_id=1, source_target_pairs={{0,128},{128,0},{1,129},{129,1},{2,130},{130,2},{3,131},{131,3},{4... | collective-permute-start | bytes 3883016 | tf_op jit(solution)/shard_map/ppermute | solution.py:26
  130.8 43.1 %all-to-all-start.3 = ((f32[32,16,768]{2,1,0:T(8,128)}), f32[32,16,768]{2,1,0:T(8,128)S(1)}, u32[]{:S(2)}, u32[]{:S(2)}) async-start(f32[32,16,768]{2,1,0:T(8,128)} %bitcast.13), calls=%async_computation.3 | async-start | bytes 3145728 | tf_op jit(solution)/shard_map/all_to_all | solution.py:203
  136.3 7.6 %collective-permute-start.11 = (f32[768,512]{1,0:T(8,128)}, f32[768,512]{1,0:T(8,128)}, u32[]{:S(2)}, u32[]{:S(2)}) collective-permute-start(f32[768,512]{1,0:T(8,128)} %slice.30.refs_6_), channel_id=1, source_target_pairs={{0,1},{1,0},{2,3},{3,2},{4,5},{5,4},{6,7},{7,6},{8,9},{9,8},{10,11... | collective-permute-start | bytes 4718600 | tf_op jit(solution)/shard_map/ppermute | solution.py:18
  138.6 7.5 %copy-start.8 = (f32[768,512]{1,0:T(8,128)}, f32[768,512]{1,0:T(8,128)S(1)}, u32[]{:S(2)}) copy-start(f32[768,512]{1,0:T(8,128)S(1)} %collective-permute-done.14.refs_10_) | copy-start | bytes 4718596
  138.6 7.5 %collective-permute-start.16 = (f32[768,512]{1,0:T(8,128)S(1)}, f32[768,512]{1,0:T(8,128)}, u32[]{:S(2)}, u32[]{:S(2)}) collective-permute-start(f32[768,512]{1,0:T(8,128)S(1)} %collective-permute-done.14.refs_10_), channel_id=1, source_target_pairs={{0,1},{1,0},{2,3},{3,2},{4,5},{5,4},{6,7},{7,6},{8,9},{9,8},{10,11... | collective-permute-start | bytes 4718600 | tf_op jit(solution)/shard_map/ppermute | solution.py:18
  138.6 5.2 %collective-permute-start.12 = (f32[632,512]{1,0:T(8,128)}, f32[632,512]{1,0:T(8,128)}, u32[]{:S(2)}, u32[]{:S(2)}) collective-permute-start(f32[632,512]{1,0:T(8,128)} %slice.28.refs_7_), channel_id=1, source_target_pairs={{0,1},{1,0},{2,3},{3,2},{4,5},{5,4},{6,7},{7,6},{8,9},{9,8},{10,11... | collective-permute-start | bytes 3883016 | tf_op jit(solution)/shard_map/ppermute | solution.py:18
  139.1 7.0 %collective-permute-start.17 = (f32[632,512]{1,0:T(8,128)}, f32[632,512]{1,0:T(8,128)}, u32[]{:S(2)}, u32[]{:S(2)}) collective-permute-start(f32[632,512]{1,0:T(8,128)} %collective-permute-done.15.refs_11_), channel_id=1, source_target_pairs={{0,1},{1,0},{2,3},{3,2},{4,5},{5,4},{6,7},{7,6},{8,9},{9,8},{10,11... | collective-permute-start | bytes 3883016 | tf_op jit(solution)/shard_map/ppermute | solution.py:18
  175.0 71.8 %all-to-all-start.2 = ((f32[32,16,1400]{2,1,0:T(8,128)}), f32[32,16,1400]{2,1,0:T(8,128)S(1)}, u32[]{:S(2)}, u32[]{:S(2)}) async-start(f32[32,16,1400]{2,1,0:T(8,128)} %bitcast.10), calls=%async_computation.2 | async-start | bytes 5767168 | tf_op jit(solution)/shard_map/all_to_all | solution.py:203
  (5 other events, 5.7 us)
Sparse Core Ops, SparseCore 0:
  16.8 50.7 all-gather.2
